TPU v7x, 512 devices: a whole 4x8x8 slice. The times are simulated.
512 devices in a mesh: outer: 4 (over x), inner: 128 (over z, y, core).
Axes of the slice: x: 4, y: 8, z: 8, core: 2. Of those that a mesh axis runs over, the one named last changes fastest.
Arguments:
- acts: bfloat16 [512, 2, 512, 512], P(('outer', 'inner')), may hold values from -6 to 6
- cotangent: bfloat16 [512, 2, 512, 512], P(('outer', 'inner')), may hold values from -6 to 6
- residual: float32 [512, 2048, 128], P(('outer', 'inner')), may hold values from -0.6 to 0.6
- owner_residual: float32 [512, 16, 128], P(('outer', 'inner')), may hold values from -3 to 3
- in_count: int32 [512, 2, 128], P(('outer', 'inner')), may hold values from 1 to 8, as said below
- in_rank: int32 [512, 2, 2048], P(('outer', 'inner')), may hold values from 0 to 15, as said below
- out_count: int32 [512, 2], P(('outer', 'inner')), may hold values from 1 to 8
- out_rank: int32 [512, 2, 16], P(('outer', 'inner')), may hold values from 0 to 15, as said below
Outputs:
- applied: bfloat16 [512, 512], replicated
- new_residual: float32 [512, 2048, 128], P(('outer', 'inner'))
- new_owner_residual: float32 [512, 16, 128], P(('outer', 'inner'))
Inputs may be any that keep to these rules, and one draw needn't show every extreme that they name: `in_count`: each step has one owner that receives 8 blocks from every replica. `in_rank`: for each replica, step and owner, the ranks of that owner's 16 blocks are a permutation of 0 to 15. `out_rank`: for each replica and step a permutation of 0 to 15.
All inputs are finite; a program needn't handle non-finite values.
Results may differ from a plain program's by a relative error of at most 0.0065.
Values may be sent and summed in bfloat16 or wider, within the bound.
No kernel may reach another device: no remote copies, remote signals or barrier semaphores. Data moves between devices by JAX's collectives and lax.ppermute only.
A program may use at most 64 MiB of HBM per device.

v0:
```python
import math

import jax
import jax.numpy as jnp
from jax import lax
from jax.sharding import Mesh
from jax.sharding import PartitionSpec as P

INNER = ("inner_0", "inner_1", "inner_2")
OUTER_INNER = ("outer", "inner_0", "inner_1", "inner_2")


step_size = 0.0625


def sent_to_all(value, axis):
    copies = jnp.broadcast_to(value, (lax.axis_size(axis), *value.shape))
    return lax.all_to_all(copies, axis, split_axis=0, concat_axis=0, tiled=True)


def of_everyone(value, axis):
    everything = sent_to_all(value, axis)
    return jnp.sum(everything, axis=0)


def joined_along(pieces, dim):
    lengths = list(pieces.shape[1:])
    lengths[dim] *= pieces.shape[0]
    return jnp.moveaxis(pieces, 0, dim).reshape(lengths)


def gather_axes(value, axes, dim):
    far, near = axes
    pieces = sent_to_all(sent_to_all(value, far), near)
    return joined_along(pieces.swapaxes(0, 1).reshape(-1, *value.shape), dim)


def select_blocks(resid, grad, ranks_flat, counts, owners, region, width):
    blocks = resid.shape[0]
    accum = (resid + grad.reshape(blocks, width)).reshape(owners, region, width)
    ranks = ranks_flat.reshape(owners, region)
    chosen = (ranks < counts[:, None])[..., None]
    new_resid = jnp.where(chosen, jnp.float32(0.0), accum).reshape(blocks, width)
    return (accum, ranks, chosen, new_resid)


def pack_slots(accum, ranks, counts, slots, region):
    order = lax.iota(jnp.int32, slots)
    picks = (ranks[:, None, :] == order[None, :, None]) & (
        order[None, :, None] < counts[:, None, None]
    )
    picks_f = picks.astype(jnp.float32)
    places = lax.iota(jnp.int32, region).astype(jnp.float32)
    packed = jnp.einsum("nkr,nrd->nkd", picks_f, accum, precision=lax.Precision.HIGHEST)
    where_at = jnp.einsum("nkr,r->nk", picks_f, places, precision=lax.Precision.HIGHEST)
    return (packed, where_at)


def unpack_slots(arrived, spots, region, width):
    places = lax.iota(jnp.int32, region).astype(jnp.float32)
    placed = (spots.reshape(-1)[:, None] == places[None, :]).astype(jnp.float32)
    return jnp.einsum(
        "mr,md->rd", placed, arrived.reshape(-1, width), precision=lax.Precision.HIGHEST
    )


def owner_section(pod_sum, oresid, ranks_out, count_out):
    owner_acc = pod_sum + oresid
    passed = (ranks_out < count_out)[:, None]
    outgoing = jnp.where(passed, owner_acc, jnp.float32(0.0))
    kept = jnp.where(passed, jnp.float32(0.0), owner_acc)
    return (outgoing, kept)


def per_device(acts, cotangent, residual, owner_residual, in_count, in_rank, out_count, out_rank):
    owners = lax.axis_size(INNER)
    steps = acts.shape[1]
    tokens = acts.shape[2]
    rows = acts.shape[3]
    cols = cotangent.shape[3]
    blocks = residual.shape[1]
    width = residual.shape[2]
    region = blocks // owners
    slots = max(1, region // 2)
    scale = 1.0 / math.sqrt(tokens * owners)
    resid = residual[0]
    oresid = owner_residual[0]
    crosses = []
    packs = []
    spots_all = []
    for step in range(steps):
        grad = (
            jnp.einsum(
                "tr,tc->rc", acts[0, step], cotangent[0, step], preferred_element_type=jnp.float32
            )
            * scale
        )
        counts = in_count[0, step]
        accum, ranks, chosen, resid = select_blocks(
            resid, grad, in_rank[0, step], counts, owners, region, width
        )
        packed, where_at = pack_slots(accum, ranks, counts, slots, region)
        packs.append(packed)
        spots_all.append(where_at)
    arrived, spots = (
        lax.all_to_all(
            jnp.concatenate(packs, axis=1), INNER, split_axis=0, concat_axis=0, tiled=True
        ),
        lax.all_to_all(
            jnp.concatenate(spots_all, axis=1), INNER, split_axis=0, concat_axis=0, tiled=True
        ),
    )
    outgoings = []
    for step in range(steps):
        pod_sum = unpack_slots(
            arrived[:, step * slots : (step + 1) * slots],
            spots[:, step * slots : (step + 1) * slots],
            region,
            width,
        )
        outgoing, oresid = owner_section(pod_sum, oresid, out_rank[0, step], out_count[0, step])
        outgoings.append(outgoing)
    summed = of_everyone(jnp.stack(outgoings), "outer")
    for step in range(steps):
        crosses.append(summed[step])
    deltas = []
    for cross in crosses:
        delta = cross.astype(jnp.bfloat16)
        deltas.append(delta)
    total = deltas[0].astype(jnp.float32)
    for later in deltas[1:]:
        total = total + later.astype(jnp.float32)
    applied = (-step_size * total).astype(jnp.bfloat16)
    applied = gather_axes(applied, (("inner_0", "inner_1"), "inner_2"), 0)
    return (applied.reshape(rows, cols), resid[None], oresid[None])


def solution(mesh):
    finer = Mesh(
        mesh.devices.reshape(mesh.shape["outer"], 8, 8, 2),
        ("outer", "inner_0", "inner_1", "inner_2"),
    )
    in_specs = (
        P(OUTER_INNER, None, None, None),
        P(OUTER_INNER, None, None, None),
        P(OUTER_INNER, None, None),
        P(OUTER_INNER, None, None),
        P(OUTER_INNER, None, None),
        P(OUTER_INNER, None, None),
        P(OUTER_INNER, None),
        P(OUTER_INNER, None, None),
    )
    out_specs = (P(), P(OUTER_INNER, None, None), P(OUTER_INNER, None, None))
    return jax.shard_map(
        per_device, mesh=finer, in_specs=in_specs, out_specs=out_specs, check_vma=False
    )
```

profile of v0, /device:TPU:1, one launch (start us, length us, event | category | flops | bytes accessed | tf_op | source)
XLA Modules:
  0.0 115.3 jit_solution(6637989230640421976)
XLA Ops:
  0.6 0.0 copy-start.6
  0.7 0.7 copy-done.6
  1.3 0.8 slice_reduce_fusion
  2.2 0.1 eq.64
  2.2 0.1 eq.60
  2.3 0.1 iota_compare_fusion.2
  2.4 0.9 select_reduce_fusion.1
  3.3 0.1 copy.25
  3.4 0.8 copy.14
  4.2 18.4 %all-to-all-start = ((f32[128,1,16]{2,1,0:T(1,128)}), f32[128,1,16]{2,1,0:T(1,128)S(1)}, u32[]{:S(2)}, u32[]{:S(2)}) async-start(f32[128,1,16]{2,1,0:T(1,128)} %bitcast.6), calls=%async_computation | async-start | bytes 131072 | tf_op jit(solution)/shard_map/all_to_all | solution.py:109
  22.6 0.1 broadcast_compare_fusion
  22.7 0.0 copy-start.7
  22.7 0.0 copy-start.8
  22.7 2.8 %convolution_multiply_fusion = f32[512,512]{1,0:T(8,128)} fusion(bf16[1,2,512,512]{3,2,1,0:T(8,128)(2,1)} %param.9, bf16[1,2,512,512]{3,2,1,0:T(8,128)(2,1)} %param.8), kind=kOutput, calls=%fused_computation | convolution fusion | flops 268697600 | bytes 2097152 | tf_op jit(solution)/shard_map/tr,tc->rc/dot_general | solution.py:93
  25.5 0.0 copy-done.7
  25.5 0.0 copy-done.8
  25.5 0.5 convolution_multiply_fusion.1
  26.0 0.0 copy-start.1
  26.0 1.0 copy-done.1
  27.0 0.1 reshape.170
  27.0 0.0 copy-start
  27.1 1.4 %reshape.171 = f32[128,16,128]{2,1,0:T(8,128)S(1)} reshape(f32[512,512]{1,0:T(8,128)} %convolution_multiply_fusion) | data formatting | bytes 2097152 | tf_op jit(solution)/shard_map/reshape | solution.py:40
  28.4 0.1 copy-done
  28.6 0.8 fusion.13
  29.4 1.5 %fusion = f32[128,8,128]{2,1,0:T(8,128)S(1)} fusion(f32[128,16,128]{2,1,0:T(8,128)S(1)} %reshape.171, pred[128,16]{1,0:T(8,128)(4,1)S(1)} %broadcast_compare_fusion, f32[128,16,128]{2,1,0:T(8,128)S(1)} %bitcast.57, f32[128,16,128]{2,1,0:T(8,128)S(1)} %reshape.170, s32[128,16]{1,0:T(8,128)S(1)} %eq.64, pred[128,8]{1,0:T(8,128)(4,1)S(1)} %get-tuple-element.19), kind=kOutput, calls=%fused_computation.6 | convolution fusion | flops 25985024 | bytes 3681280 | tf_op jit(solution)/shard_map/nkr,nrd->nkd/dot_general | solution.py:54
  30.9 1.1 pad_maximum_fusion
  32.0 0.0 copy-start.4
  32.0 2.0 %all-to-all-done = f32[128,1,16]{2,1,0:T(1,128)S(1)} async-done(((f32[128,1,16]{2,1,0:T(1,128)}), f32[128,1,16]{2,1,0:T(1,128)S(1)}, u32[]{:S(2)}, u32[]{:S(2)}) %all-to-all-start) | async-done | bytes 8224 | tf_op jit(solution)/shard_map/all_to_all | solution.py:109
  34.0 0.0 copy-start.5
  34.0 0.0 copy-start.3
  34.0 11.9 %all-to-all-start.1 = ((f32[128,16,128]{2,1,0:T(8,128)}), f32[128,16,128]{2,1,0:T(8,128)S(1)}, u32[]{:S(2)}, u32[]{:S(2)}) async-start(f32[128,16,128]{2,1,0:T(8,128)} %pad_maximum_fusion), calls=%async_computation.1 | async-start | bytes 2097152 | tf_op jit(solution)/shard_map/all_to_all | solution.py:106
  45.9 0.0 copy-done.4
  45.9 0.0 copy-start.2
  45.9 0.6 fusion.35
  46.5 0.0 copy-done.5
  46.5 1.3 %compare_bitcast_fusion = (pred[16]{0:T(512)(128)(4,1)S(1)}, pred[16]{0:T(512)(128)(4,1)S(1)}) fusion(s32[1,2,16]{2,1,0:T(2,128)S(1)} %copy-done.5, s32[]{:T(128)} %bitcast.16, s32[]{:T(128)} %bitcast.2), kind=kLoop, calls=%fused_computation.52 | loop fusion | flops 32 | bytes 168 | tf_op jit(solution)/shard_map/lt | solution.py:69
  47.8 0.1 fusion.34
  47.8 0.1 eq.68
  47.9 0.1 eq.72
  48.0 28.7 %all-to-all-done.1 = f32[128,16,128]{2,1,0:T(8,128)S(1)} async-done(((f32[128,16,128]{2,1,0:T(8,128)}), f32[128,16,128]{2,1,0:T(8,128)S(1)}, u32[]{:S(2)}, u32[]{:S(2)}) %all-to-all-start.1) | async-done | bytes 1048608 | tf_op jit(solution)/shard_map/all_to_all | solution.py:106
  76.8 0.0 copy-done.3
  76.8 0.7 convolution_add_fusion.1
  77.5 0.1 select_bitcast_fusion.2
  77.6 1.3 %select_bitcast_fusion = (f32[1,16,128]{2,1,0:T(8,128)}, f32[1,16,128]{2,1,0:T(8,128)S(1)}) fusion(pred[16]{0:T(512)(128)(4,1)S(1)} %get-tuple-element.13, f32[16,128]{1,0:T(8,128)S(1)} %convolution_add_fusion.1, pred[16]{0:T(512)(128)(4,1)S(1)} %get-tuple-element.14, f32[128,16,128]{2,1,0:T(8,128)S(1)} %all-to-all-done.1, f32[16]{0:T(128)S(1)} %iota_convert_fusion, ...), kind=kOutput, calls=%fused_computation.47 | convolution fusion | flops 25190400 | bytes 554496 | tf_op jit(solution)/shard_map/mr,md->rd/dot_general | solution.py:62
  78.9 0.6 broadcast_in_dim.79
  79.5 4.0 %all-to-all-start.2 = ((f32[4,2,16,128]{3,2,1,0:T(8,128)}), f32[4,2,16,128]{3,2,1,0:T(8,128)S(1)}, u32[]{:S(2)}, u32[]{:S(2)}) async-start(f32[4,2,16,128]{3,2,1,0:T(8,128)} %broadcast_in_dim.79), calls=%async_computation.2 | async-start | bytes 131072 | tf_op jit(solution)/shard_map/all_to_all | solution.py:18
  83.6 0.0 copy-done.2
  83.6 0.1 reshape.174
  83.6 1.3 %reshape.175 = f32[1,2048,128]{2,1,0:T(8,128)S(1)} reshape(f32[512,512]{1,0:T(8,128)} %convolution_multiply_fusion) | data formatting | bytes 2097152 | tf_op jit(solution)/shard_map/reshape | solution.py:40
  84.9 0.1 lt.113
  85.0 0.1 lt.114
  85.1 0.1 lt.108
  85.2 0.1 lt.116
  85.3 2.7 %all-to-all-done.2 = f32[4,2,16,128]{3,2,1,0:T(8,128)S(1)} async-done(((f32[4,2,16,128]{3,2,1,0:T(8,128)}), f32[4,2,16,128]{3,2,1,0:T(8,128)S(1)}, u32[]{:S(2)}, u32[]{:S(2)}) %all-to-all-start.2) | async-done | bytes 65568 | tf_op jit(solution)/shard_map/all_to_all | solution.py:18
  88.1 0.7 broadcast_in_dim.80
  88.8 5.4 %all-to-all-start.3 = ((bf16[64,16,128]{2,1,0:T(8,128)(2,1)}), bf16[64,16,128]{2,1,0:T(8,128)(2,1)S(1)}, u32[]{:S(2)}, u32[]{:S(2)}) async-start(bf16[64,16,128]{2,1,0:T(8,128)(2,1)} %broadcast_in_dim.80), calls=%async_computation.3 | async-start | bytes 524288 | tf_op jit(solution)/shard_map/all_to_all | solution.py:18
  94.2 2.4 %add_select_fusion = f32[1,2048,128]{2,1,0:T(8,128)} fusion(f32[1,2048,128]{2,1,0:T(8,128)S(1)} %reshape.175, f32[1,2048,128]{2,1,0:T(8,128)S(1)} %copy-done, f32[1,2048,128]{2,1,0:T(8,128)S(1)} %reshape.174, pred[2048]{0:T(1024)(128)(4,1)S(1)} %lt.117, pred[2048]{0:T(1024)(128)(4,1)S(1)} %lt.115), kind=kLoop, calls=%fused_computation.5 | loop fusion | flops 1048576 | bytes 4198400 | tf_op jit(solution)/shard_map/jit(_where)/select_n | solution.py:43
  96.6 10.1 %all-to-all-done.3 = bf16[64,16,128]{2,1,0:T(8,128)(2,1)S(1)} async-done(((bf16[64,16,128]{2,1,0:T(8,128)(2,1)}), bf16[64,16,128]{2,1,0:T(8,128)(2,1)S(1)}, u32[]{:S(2)}, u32[]{:S(2)}) %all-to-all-start.3) | async-done | bytes 262176 | tf_op jit(solution)/shard_map/all_to_all | solution.py:18
  106.7 0.1 broadcast_in_dim.81
  106.7 7.4 %all_to_all.32 = bf16[2,64,16,128]{3,2,1,0:T(8,128)(2,1)S(1)} all-to-all(bf16[2,64,16,128]{3,2,1,0:T(8,128)(2,1)S(1)} %broadcast_in_dim.81), channel_id=1, replica_groups=mesh['outer'=4,'inner_0'=8,'inner_1'=8,'inner_2'=2] {'inner_2'}, dimensions={0} | all-to-all | bytes 1048576 | tf_op jit(solution)/shard_map/all_to_all | solution.py:18
  114.1 1.1 reshape_reshape_reshape.3
  (10 shorter events, 0.1 us)
Async XLA Ops:
  0.6 0.7 copy-start.6
  4.2 29.8 %all-to-all-start = ((f32[128,1,16]{2,1,0:T(1,128)}), f32[128,1,16]{2,1,0:T(1,128)S(1)}, u32[]{:S(2)}, u32[]{:S(2)}) async-start(f32[128,1,16]{2,1,0:T(1,128)} %bitcast.6), calls=%async_computation | async-start | bytes 131072 | tf_op jit(solution)/shard_map/all_to_all | solution.py:109
  22.7 2.8 %copy-start.7 = (bf16[1,2,512,512]{3,2,1,0:T(8,128)(2,1)S(1)}, bf16[1,2,512,512]{3,2,1,0:T(8,128)(2,1)}, u32[]{:S(2)}) copy-start(bf16[1,2,512,512]{3,2,1,0:T(8,128)(2,1)} %param.9) | copy-start | bytes 3145732
  22.7 2.8 %copy-start.8 = (bf16[1,2,512,512]{3,2,1,0:T(8,128)(2,1)S(1)}, bf16[1,2,512,512]{3,2,1,0:T(8,128)(2,1)}, u32[]{:S(2)}) copy-start(bf16[1,2,512,512]{3,2,1,0:T(8,128)(2,1)} %param.8) | copy-start | bytes 3145732
  26.0 1.0 copy-start.1
  27.0 1.5 %copy-start = (f32[1,2048,128]{2,1,0:T(8,128)S(1)}, f32[1,2048,128]{2,1,0:T(8,128)}, u32[]{:S(2)}) copy-start(f32[1,2048,128]{2,1,0:T(8,128)} %param.10) | copy-start | bytes 3145732
  32.0 13.9 %copy-start.4 = (s32[1,2]{1,0:T(1,128)S(1)}, s32[1,2]{1,0:T(1,128)}, u32[]{:S(2)}) copy-start(s32[1,2]{1,0:T(1,128)} %param.14) | copy-start | bytes 28
  34.0 12.5 %copy-start.5 = (s32[1,2,16]{2,1,0:T(2,128)S(1)}, s32[1,2,16]{2,1,0:T(2,128)}, u32[]{:S(2)}) copy-start(s32[1,2,16]{2,1,0:T(2,128)} %param.15) | copy-start | bytes 388
  34.0 42.8 %copy-start.3 = (f32[1,16,128]{2,1,0:T(8,128)S(1)}, f32[1,16,128]{2,1,0:T(8,128)}, u32[]{:S(2)}) copy-start(f32[1,16,128]{2,1,0:T(8,128)} %param.11) | copy-start | bytes 24580
  34.0 42.8 %all-to-all-start.1 = ((f32[128,16,128]{2,1,0:T(8,128)}), f32[128,16,128]{2,1,0:T(8,128)S(1)}, u32[]{:S(2)}, u32[]{:S(2)}) async-start(f32[128,16,128]{2,1,0:T(8,128)} %pad_maximum_fusion), calls=%async_computation.1 | async-start | bytes 2097152 | tf_op jit(solution)/shard_map/all_to_all | solution.py:106
  45.9 37.7 %copy-start.2 = (f32[512,512]{1,0:T(8,128)S(1)}, f32[512,512]{1,0:T(8,128)}, u32[]{:S(2)}) copy-start(f32[512,512]{1,0:T(8,128)} %copy-done.1) | copy-start | bytes 3145732
  79.5 8.5 %all-to-all-start.2 = ((f32[4,2,16,128]{3,2,1,0:T(8,128)}), f32[4,2,16,128]{3,2,1,0:T(8,128)S(1)}, u32[]{:S(2)}, u32[]{:S(2)}) async-start(f32[4,2,16,128]{3,2,1,0:T(8,128)} %broadcast_in_dim.79), calls=%async_computation.2 | async-start | bytes 131072 | tf_op jit(solution)/shard_map/all_to_all | solution.py:18
  88.8 17.9 %all-to-all-start.3 = ((bf16[64,16,128]{2,1,0:T(8,128)(2,1)}), bf16[64,16,128]{2,1,0:T(8,128)(2,1)S(1)}, u32[]{:S(2)}, u32[]{:S(2)}) async-start(bf16[64,16,128]{2,1,0:T(8,128)(2,1)} %broadcast_in_dim.80), calls=%async_computation.3 | async-start | bytes 524288 | tf_op jit(solution)/shard_map/all_to_all | solution.py:18
where the time goes:
time: 116 us; the launch traced here: 115 us
  waiting for transfers between devices  43.6 us (38%)
  starting transfers between devices  39.7 us (34%)
  local copies, waits for them, and re-layouts  10.3 us (9%)
  matrix products  7.6 us (7%)
  blocking collectives  7.37 us (6%)
  other arithmetic  5.97 us (5%)
    all_to_all x1, waiting for transfers between devices, per_device(): lax.all_to_all(jnp.concatenate(packs, axis=1), INNER, split_axis=0, conca...  28.7 us
    all_to_all x1, starting transfers between devices, per_device(): lax.all_to_all(jnp.concatenate(spots_all, axis=1), INNER, split_axis=0, c...  18.4 us
    all_to_all x2, waiting for transfers between devices, sent_to_all(): return lax.all_to_all(copies, axis, split_axis=0, concat_axis=0, tiled=True)  12.8 us
    all_to_all x1, starting transfers between devices, per_device(): lax.all_to_all(jnp.concatenate(packs, axis=1), INNER, split_axis=0, conca...  11.9 us
    all_to_all x2, starting transfers between devices, sent_to_all(): return lax.all_to_all(copies, axis, split_axis=0, concat_axis=0, tiled=True)  9.38 us
    all_to_all x1, blocking collectives, sent_to_all(): return lax.all_to_all(copies, axis, split_axis=0, concat_axis=0, tiled=True)  7.37 us
    dot_general x2, matrix products, per_device(): jnp.einsum('tr,tc->rc', acts[0, step], cotangent[0, step], preferred_elem...  3.26 us
    reshape x4, local copies, waits for them, and re-layouts, select_blocks(): accum = (resid + grad.reshape(blocks, width)).reshape(owners, region, width)  2.81 us
  transfers between devices with their start and end apart: 4, of which 4 were waited for; matrix products, arithmetic and copies ran while one was open for 13% of the time, Pallas kernels for 0%

commit v1 on v0

v1 whole, which is shorter than its diff:
```python
import math

import jax
import jax.numpy as jnp
import numpy as np
from jax import lax
from jax.experimental import pallas as pl
from jax.experimental.pallas import tpu as pltpu
from jax.sharding import Mesh
from jax.sharding import PartitionSpec as P

STEP_SIZE = 0.0625
NX, NZ, NY, NC = 4, 8, 8, 2
CHIPS = NZ * NY
REGION = 16
WIDTH = 128
BF = jnp.bfloat16
F32 = jnp.float32
VMEM_LIMIT = 48 * 1024 * 1024


def lines(axes0, axes1):
    ids = np.arange(NX * NZ * NY * NC).reshape(NX, NZ, NY, NC)
    out = []
    for core, axes in ((0, axes0), (1, axes1)):
        sub = ids[..., core]
        size = int(np.prod([sub.shape[a] for a in axes]))
        moved = np.moveaxis(sub, axes, range(3 - len(axes), 3))
        out += moved.reshape(-1, size).tolist()
    return out


def exchange(value, groups):
    return lax.all_to_all(
        value, "d", split_axis=0, concat_axis=0, tiled=True, axis_index_groups=groups
    )


def other_core(value):
    pairs = [(i, i ^ 1) for i in range(NX * NZ * NY * NC)]
    return lax.ppermute(value, "d", pairs)


def place_of(core, z, y):
    return z * NY + y if core == 0 else y * NZ + z


def local_kernel(scale, core_ref, acts_ref, cot_ref, resid_ref, count_ref, rank_ref,
                 resid_out, keep_ref, give_ref, acc_ref, ranks_ref, chosen_ref):
    step = pl.program_id(0)
    core = core_ref[0]
    rows = acts_ref.shape[3]
    cols = cot_ref.shape[3]
    tiles = cols // WIDTH
    groups = resid_ref.shape[1] // WIDTH

    @pl.when(step == 0)
    def _():
        resid_out[...] = resid_ref[...]

    @pl.when(step == 0)
    def _():
        per = WIDTH // groups
        row_id = lax.broadcasted_iota(jnp.int32, (groups, WIDTH), 0)
        lane_id = lax.broadcasted_iota(jnp.int32, (groups, WIDTH), 1)
        owner_id = lax.broadcasted_iota(jnp.int32, (WIDTH, WIDTH), 0) % per
        block_id = lax.broadcasted_iota(jnp.int32, (WIDTH, WIDTH), 1) // REGION
        place = jnp.where(owner_id == block_id, 1.0, 0.0).astype(BF)
        eye = jnp.where(row_id == lane_id, 1.0, 0.0).astype(BF)
        for s in range(chosen_ref.shape[0]):
            for r in range(groups):
                ranks_ref[r:r + 1, :] = rank_ref[0, s:s + 1, r * WIDTH:(r + 1) * WIDTH]
            count = jnp.broadcast_to(count_ref[0, s:s + 1, :].astype(F32), (groups, WIDTH))
            spread = jnp.where(lane_id // per == row_id, count, 0.0)
            limit = jnp.dot(spread.astype(BF), place, preferred_element_type=F32)
            chosen = jnp.where(ranks_ref[...].astype(F32) < limit, 1.0, 0.0)
            chosen_ref[s] = lax.dot_general(chosen.astype(BF), eye, (((0,), (0,)), ((), ())),
                                            preferred_element_type=F32)

    columns = chosen_ref[step]
    left = acts_ref[0, 0]
    half = 2 * WIDTH
    for h in range(cols // half):
        grad = lax.dot_general(left, cot_ref[0, 0, :, h * half:(h + 1) * half],
                               (((0,), (0,)), ((), ())), preferred_element_type=F32)
        grad = grad * scale
        for q in range(2):
            acc_ref[pl.ds(2 * h + q, rows, stride=tiles), :] = grad[:, q * WIDTH:(q + 1) * WIDTH]

    for r in range(groups):
        span = slice(r * WIDTH, (r + 1) * WIDTH)
        total = resid_out[0, span, :] + acc_ref[span, :]
        mask = jnp.broadcast_to(columns[:, r:r + 1], (WIDTH, WIDTH)) > 0.5
        resid_out[0, span, :] = jnp.where(mask, 0.0, total)
        sent = jnp.where(mask, total, 0.0).astype(BF)
        for me in range(NC):
            @pl.when(core == me)
            def _(me=me, r=r, sent=sent):
                for i in range(WIDTH // REGION):
                    owner = r * (WIDTH // REGION) + i
                    z, y, c = owner // (NY * NC), (owner // NC) % NY, owner % NC
                    to = keep_ref if c == me else give_ref
                    to[place_of(c, z, y), step] = sent[i * REGION:(i + 1) * REGION, :]


def owner_kernel(arrived_ref, oresid_ref, count_ref, rank_ref, out_ref, oresid_out):
    steps = rank_ref.shape[1]
    eye = (lax.broadcasted_iota(jnp.int32, (REGION, REGION), 0)
           == lax.broadcasted_iota(jnp.int32, (REGION, REGION), 1))
    oresid = oresid_ref[0]
    for s in range(steps):
        total = arrived_ref[0, s].astype(F32)
        for k in range(1, arrived_ref.shape[0]):
            total = total + arrived_ref[k, s].astype(F32)
        row = jnp.where(rank_ref[0, s:s + 1, :] < count_ref[0, s], 1.0, 0.0)
        square = jnp.where(eye, jnp.broadcast_to(row, (REGION, REGION)), 0.0)
        passed = jnp.broadcast_to(jnp.sum(square, axis=1, keepdims=True), (REGION, WIDTH)) > 0.5
        total = total + oresid
        going = jnp.where(passed, total, 0.0).astype(BF)
        oresid = jnp.where(passed, 0.0, total)
        for k in range(out_ref.shape[0]):
            out_ref[k, s] = going
    oresid_out[0] = oresid


def update_kernel(arrived_ref, out_ref):
    near = out_ref.shape[0]
    for a in range(near):
        total = jnp.zeros((REGION, WIDTH), F32)
        for s in range(arrived_ref.shape[1]):
            cross = arrived_ref[a, s].astype(F32)
            for x in range(1, NX):
                cross = cross + arrived_ref[x * near + a, s].astype(F32)
            total = total + cross.astype(BF).astype(F32)
        applied = (-STEP_SIZE * total).astype(BF)
        for k in range(near):
            out_ref[k, a] = applied


def assemble_kernel(core_ref, own_ref, got_ref, out_ref, flat_ref):
    core = core_ref[0]
    rows, cols = out_ref.shape
    tiles = cols // WIDTH
    for i in range(CHIPS):
        plain = NC * REGION * i
        swapped = NC * REGION * ((i % NZ) * NY + i // NZ) + REGION
        mine = pl.multiple_of(jnp.where(core == 0, plain, swapped), REGION)
        theirs = pl.multiple_of(jnp.where(core == 0, swapped, plain), REGION)
        flat_ref[pl.ds(mine, REGION), :] = own_ref[i].astype(F32)
        flat_ref[pl.ds(theirs, REGION), :] = got_ref[i].astype(F32)
    for t in range(tiles):
        out_ref[:, t * WIDTH:(t + 1) * WIDTH] = flat_ref[pl.ds(t, rows, stride=tiles), :].astype(BF)


def vmem():
    return pl.BlockSpec(memory_space=pltpu.VMEM)


def smem():
    return pl.BlockSpec(memory_space=pltpu.SMEM)


def per_device(acts, cotangent, residual, owner_residual, in_count, in_rank, out_count, out_rank):
    steps, tokens, rows = acts.shape[1:]
    cols = cotangent.shape[3]
    blocks = residual.shape[1]
    scale = 1.0 / math.sqrt(tokens * CHIPS * NC)
    core = (lax.axis_index("d") % NC).astype(jnp.int32).reshape(1)
    params = pltpu.CompilerParams(vmem_limit_bytes=VMEM_LIMIT)

    def local(*args):
        return local_kernel(scale, *args)

    whole3 = lambda s, c: (0, 0, 0)
    whole4 = lambda s, c: (0, 0, 0, 0)
    half = (CHIPS, steps, REGION, WIDTH)
    new_residual, keep, give = pl.pallas_call(
        local,
        grid_spec=pltpu.PrefetchScalarGridSpec(
            num_scalar_prefetch=1,
            grid=(steps,),
            in_specs=[
                pl.BlockSpec((1, 1, tokens, rows), lambda s, c: (0, s, 0, 0)),
                pl.BlockSpec((1, 1, tokens, cols), lambda s, c: (0, s, 0, 0)),
                pl.BlockSpec((1, blocks, WIDTH), whole3),
                pl.BlockSpec(in_count.shape, whole3),
                pl.BlockSpec(in_rank.shape, whole3),
            ],
            out_specs=[
                pl.BlockSpec((1, blocks, WIDTH), whole3),
                pl.BlockSpec(half, whole4),
                pl.BlockSpec(half, whole4),
            ],
            scratch_shapes=[
                pltpu.VMEM((blocks, WIDTH), F32),
                pltpu.VMEM((blocks // WIDTH, WIDTH), jnp.int32),
                pltpu.VMEM((steps, WIDTH, WIDTH), F32),
            ],
        ),
        out_shape=[
            jax.ShapeDtypeStruct(residual.shape, F32),
            jax.ShapeDtypeStruct(half, BF),
            jax.ShapeDtypeStruct(half, BF),
        ],
        compiler_params=params,
        name="local",
    )(core, acts, cotangent, residual, in_count, in_rank)

    got = other_core(give)
    pair = (keep.astype(F32) + got.astype(F32)).astype(BF)
    first = exchange(pair.reshape(NZ, NY, steps, REGION, WIDTH), lines((1,), (2,)))
    line = jnp.sum(first.astype(F32), axis=0).astype(BF)
    second = exchange(line, lines((2,), (1,)))

    outgoing, new_owner = pl.pallas_call(
        owner_kernel,
        in_specs=[vmem(), vmem(), smem(), vmem()],
        out_specs=[vmem(), vmem()],
        out_shape=[
            jax.ShapeDtypeStruct((NX * NY, steps, REGION, WIDTH), BF),
            jax.ShapeDtypeStruct(owner_residual.shape, F32),
        ],
        compiler_params=params,
        name="owner",
    )(second, owner_residual, out_count, out_rank)

    crossing = exchange(outgoing, lines((0, 2), (0, 1)))
    copies = pl.pallas_call(
        update_kernel,
        in_specs=[vmem()],
        out_specs=vmem(),
        out_shape=jax.ShapeDtypeStruct((NZ, NY, REGION, WIDTH), BF),
        compiler_params=params,
        name="update",
    )(crossing)
    own = exchange(copies, lines((1,), (2,))).reshape(CHIPS, REGION, WIDTH)
    theirs = other_core(own)
    applied = pl.pallas_call(
        assemble_kernel,
        in_specs=[smem(), vmem(), vmem()],
        out_specs=vmem(),
        out_shape=jax.ShapeDtypeStruct((rows, cols), BF),
        scratch_shapes=[pltpu.VMEM((blocks, WIDTH), F32)],
        compiler_params=params,
        name="assemble",
    )(core, own, theirs)
    return applied, new_residual, new_owner


def solution(mesh):
    flat = Mesh(mesh.devices.reshape(-1), ("d",))
    spec = P("d")
    return jax.shard_map(
        per_device,
        mesh=flat,
        in_specs=(spec,) * 8,
        out_specs=(P(), spec, spec),
        check_vma=False,
    )
```

time: 116 us -> 88.5 us (0.76)
  blocking collectives: 7.37 us -> 56.6 us
  waiting for transfers between devices: 43.6 us -> 2.65 us
  starting transfers between devices: 39.7 us -> 16 us
  matrix products: 7.6 us -> 0 us
  Pallas kernels: 0 us -> 7.45 us
  local copies, waits for them, and re-layouts: 10.3 us -> 4.39 us
  other arithmetic: 5.97 us -> 0.22 us
    all_to_all x1 -> x4, blocking collectives: 7.37 us -> 56.6 us  [exchange(): lax.all_to_all(value, 'd', split_axis=0, concat_axis=0, tiled=True, axis_...]
    all_to_all x4 -> x0, waiting for transfers between devices: 43.6 us -> none  [the longest x1 28.7 us: per_device(): lax.all_to_all(jnp.concatenate(packs, axis=1), INNER, split_axis=0, conca...]
    all_to_all x4 -> x0, starting transfers between devices: 39.7 us -> none  [the longest x1 18.4 us: per_device(): lax.all_to_all(jnp.concatenate(spots_all, axis=1), INNER, split_axis=0, c...]
    ppermute x0 -> x2, starting transfers between devices: none -> 16 us  [other_core(): return lax.ppermute(value, 'd', pairs)]
    dot_general x6 -> x0, matrix products: 7.6 us -> none  [the longest x2 3.26 us: per_device(): jnp.einsum('tr,tc->rc', acts[0, step], cotangent[0, step], preferred_elem...]
    pallas_call x0 -> x4, Pallas kernels: none -> 7.45 us  [the longest x1 5.14 us: per_device(): pl.pallas_call(local, grid_spec=pltpu.PrefetchScalarGridSpec(num_scalar_p...]
    reshape x4 -> x0, local copies, waits for them, and re-layouts: 2.81 us -> none  [select_blocks(): accum = (resid + grad.reshape(blocks, width)).reshape(owners, region, width)]
    ppermute x0 -> x2, waiting for transfers between devices: none -> 2.65 us  [other_core(): return lax.ppermute(value, 'd', pairs)]
  transfers between devices with their start and end apart: 4 -> 2, of which waited for: 4 -> 2; matrix products, arithmetic and copies ran while one was open for 13% -> 0% of each run, Pallas kernels for 0% -> 0%
where the time goes in v1:
time: 88.5 us; the launch traced here: 88 us
  blocking collectives  56.6 us (64%)
  starting transfers between devices  16 us (18%)
  Pallas kernels  7.45 us (8%)
  local copies, waits for them, and re-layouts  4.39 us (5%)
  waiting for transfers between devices  2.65 us (3%)
    all_to_all x4, blocking collectives, exchange(): lax.all_to_all(value, 'd', split_axis=0, concat_axis=0, tiled=True, axis_...  56.6 us
    ppermute x2, starting transfers between devices, other_core(): return lax.ppermute(value, 'd', pairs)  16 us
    pallas_call x1, Pallas kernels, per_device(): pl.pallas_call(local, grid_spec=pltpu.PrefetchScalarGridSpec(num_scalar_p...  5.14 us
    unnamed x16, local copies, waits for them, and re-layouts  4.39 us
    ppermute x2, waiting for transfers between devices, other_core(): return lax.ppermute(value, 'd', pairs)  2.65 us
  transfers between devices with their start and end apart: 2, of which 2 were waited for; matrix products, arithmetic and copies ran while one was open for 0% of the time, Pallas kernels for 0%

profile of v1, /device:TPU:1, one launch (start us, length us, event | category | flops | bytes accessed | tf_op | source)
XLA Modules:
  0.0 88.0 jit_solution(16606973900519864327)
XLA Ops:
  0.6 0.0 copy-start.3
  0.7 0.0 copy-start.5
  0.7 0.7 copy-done.3
  1.3 0.0 copy-done.5
  1.4 0.0 copy-start
  1.4 1.2 %copy-done = bf16[1,2,512,512]{3,2,1,0:T(8,128)(2,1)S(1)} copy-done((bf16[1,2,512,512]{3,2,1,0:T(8,128)(2,1)S(1)}, bf16[1,2,512,512]{3,2,1,0:T(8,128)(2,1)}, u32[]{:S(2)}) %copy-start) | copy-done | bytes 1048600
  2.6 0.0 copy-start.1
  2.6 1.2 %copy-done.1 = bf16[1,2,512,512]{3,2,1,0:T(8,128)(2,1)S(1)} copy-done((bf16[1,2,512,512]{3,2,1,0:T(8,128)(2,1)S(1)}, bf16[1,2,512,512]{3,2,1,0:T(8,128)(2,1)}, u32[]{:S(2)}) %copy-start.1) | copy-done | bytes 1048600
  3.8 0.0 copy-start.2
  3.8 1.2 %copy-done.2 = f32[1,2048,128]{2,1,0:T(8,128)S(1)} copy-done((f32[1,2048,128]{2,1,0:T(8,128)S(1)}, f32[1,2048,128]{2,1,0:T(8,128)}, u32[]{:S(2)}) %copy-start.2) | copy-done | bytes 1048600
  5.0 5.1 %local.1 = (f32[1,2048,128]{2,1,0:T(8,128)}, bf16[64,2,16,128]{3,2,1,0:T(8,128)(2,1)S(1)}, bf16[64,2,16,128]{3,2,1,0:T(8,128)(2,1)S(1)}) custom-call(s32[1]{0:T(128)} %bitcast.args_0_.core_ref, bf16[1,2,512,512]{3,2,1,0:T(8,128)(2,1)S(1)} %copy-done, bf16[1,2,512,512]{3,2,1,0:T(8,128)(2,1)S(1)} %copy-done.1, f32[1,2048,128]{2,1,0:T(8,128)S(1)} %copy-done.2, ...), custom_call_target="tpu_custom_call" | custom-call | tf_op jit(solution)/shard_map/local/pallas_call | solution.py:177
  10.2 8.7 %collective-permute-start = (bf16[64,2,16,128]{3,2,1,0:T(8,128)(2,1)S(1)}, bf16[64,2,16,128]{3,2,1,0:T(8,128)(2,1)S(1)}, u32[]{:S(2)}, u32[]{:S(2)}) collective-permute-start(bf16[64,2,16,128]{3,2,1,0:T(8,128)(2,1)S(1)} %get-tuple-element.9), channel_id=1, source_target_pairs={{0,1},{1,0},{2,3},{3,2},{4,5},{5,4},{6,7},{7,6},{8,9},{9,8},{10,11... | collective-permute-start | bytes 1572872 | tf_op jit(solution)/shard_map/ppermute | solution.py:41
  18.9 1.5 %collective-permute-done = bf16[64,2,16,128]{3,2,1,0:T(8,128)(2,1)S(1)} collective-permute-done((bf16[64,2,16,128]{3,2,1,0:T(8,128)(2,1)S(1)}, bf16[64,2,16,128]{3,2,1,0:T(8,128)(2,1)S(1)}, u32[]{:S(2)}, u32[]{:S(2)}) %collective-permute-start) | collective-permute-done | bytes 524320 | tf_op jit(solution)/shard_map/ppermute | solution.py:41
  20.4 0.1 add_convert_fusion
  20.5 14.8 %all_to_all.20 = bf16[8,8,2,16,128]{4,3,2,1,0:T(8,128)(2,1)S(1)} all-to-all(bf16[8,8,2,16,128]{4,3,2,1,0:T(8,128)(2,1)S(1)} %bitcast.5), channel_id=1, replica_groups={{0,16,32,48,64,80,96,112},{2,18,34,50,66,82,98,114},{4,20,36,52,68,84,1..., dimensions={0} | all-to-all | bytes 1048576 | tf_op jit(solution)/shard_map/all_to_all | solution.py:34
  35.4 0.1 reduce_sum.12
  35.5 0.0 copy-start.4
  35.5 0.0 copy-start.6
  35.5 0.0 copy-start.7
  35.5 15.7 %all_to_all.21.arrived_ref = bf16[8,2,16,128]{3,2,1,0:T(8,128)(2,1)S(1)} all-to-all(bf16[8,2,16,128]{3,2,1,0:T(8,128)(2,1)S(1)} %reduce_sum.12), channel_id=1, replica_groups={{0,2,4,6,8,10,12,14},{16,18,20,22,24,26,28,30},{32,34,36,38,40,42,44,46..., dimensions={0} | all-to-all | bytes 131072 | tf_op jit(solution)/shard_map/all_to_all | solution.py:34
  51.2 0.0 copy-done.4
  51.2 0.0 copy-done.6
  51.2 0.0 copy-done.7
  51.2 1.2 %owner.1 = (bf16[32,2,16,128]{3,2,1,0:T(8,128)(2,1)S(1)}, f32[1,16,128]{2,1,0:T(8,128)}) custom-call(bf16[8,2,16,128]{3,2,1,0:T(8,128)(2,1)S(1)} %all_to_all.21.arrived_ref, f32[1,16,128]{2,1,0:T(8,128)S(1)} %copy-done.4, s32[1,2]{1,0:T(1,128)S(1)} %copy-done.7, s32[1,2,16]{2,1,0:T(2,128)S(1)} %copy-done.6), custom_call_target="tpu_custom_call" | custom-call | tf_op jit(solution)/shard_map/owner/pallas_call | solution.py:215
  52.5 14.3 %all_to_all.22.arrived_ref = bf16[32,2,16,128]{3,2,1,0:T(8,128)(2,1)S(1)} all-to-all(bf16[32,2,16,128]{3,2,1,0:T(8,128)(2,1)S(1)} %get-tuple-element.10), channel_id=1, replica_groups={{0,2,4,6,8,10,12,14,128,130,132,134,136,138,140,142,256,258,260,262,264..., dimensions={0} | all-to-all | bytes 524288 | tf_op jit(solution)/shard_map/all_to_all | solution.py:34
  66.8 11.7 %all_to_all.23 = bf16[8,8,16,128]{3,2,1,0:T(8,128)(2,1)S(1)} all-to-all(bf16[8,8,16,128]{3,2,1,0:T(8,128)(2,1)S(1)} %update.1), channel_id=1, replica_groups={{0,16,32,48,64,80,96,112},{2,18,34,50,66,82,98,114},{4,20,36,52,68,84,1..., dimensions={0} | all-to-all | bytes 524288 | tf_op jit(solution)/shard_map/all_to_all | solution.py:34
  78.6 7.3 %collective-permute-start.1 = (bf16[64,16,128]{2,1,0:T(8,128)(2,1)S(1)}, bf16[64,16,128]{2,1,0:T(8,128)(2,1)S(1)}, u32[]{:S(2)}, u32[]{:S(2)}) collective-permute-start(bf16[64,16,128]{2,1,0:T(8,128)(2,1)S(1)} %bitcast.3), channel_id=1, source_target_pairs={{0,1},{1,0},{2,3},{3,2},{4,5},{5,4},{6,7},{7,6},{8,9},{9,8},{10,11... | collective-permute-start | bytes 786440 | tf_op jit(solution)/shard_map/ppermute | solution.py:41
  85.8 1.1 %collective-permute-done.1.got_ref = bf16[64,16,128]{2,1,0:T(8,128)(2,1)S(1)} collective-permute-done((bf16[64,16,128]{2,1,0:T(8,128)(2,1)S(1)}, bf16[64,16,128]{2,1,0:T(8,128)(2,1)S(1)}, u32[]{:S(2)}, u32[]{:S(2)}) %collective-permute-start.1) | collective-permute-done | bytes 262176 | tf_op jit(solution)/shard_map/ppermute | solution.py:41
  87.0 1.0 %assemble.1 = bf16[512,512]{1,0:T(8,128)(2,1)} custom-call(s32[1]{0:T(128)} %bitcast.args_0_.core_ref, bf16[64,16,128]{2,1,0:T(8,128)(2,1)S(1)} %bitcast.4, bf16[64,16,128]{2,1,0:T(8,128)(2,1)S(1)} %collective-permute-done.1.got_ref), custom_call_target="tpu_custom_call" | custom-call | tf_op jit(solution)/shard_map/assemble/pallas_call | solution.py:238
  (1 shorter events, 0.0 us)
Async XLA Ops:
  0.6 0.7 copy-start.3
  0.7 0.7 copy-start.5
  1.4 1.2 %copy-start = (bf16[1,2,512,512]{3,2,1,0:T(8,128)(2,1)S(1)}, bf16[1,2,512,512]{3,2,1,0:T(8,128)(2,1)}, u32[]{:S(2)}) copy-start(bf16[1,2,512,512]{3,2,1,0:T(8,128)(2,1)} %args_1_.4) | copy-start | bytes 3145732
  2.6 1.2 %copy-start.1 = (bf16[1,2,512,512]{3,2,1,0:T(8,128)(2,1)S(1)}, bf16[1,2,512,512]{3,2,1,0:T(8,128)(2,1)}, u32[]{:S(2)}) copy-start(bf16[1,2,512,512]{3,2,1,0:T(8,128)(2,1)} %args_2_.4) | copy-start | bytes 3145732
  3.8 1.2 %copy-start.2 = (f32[1,2048,128]{2,1,0:T(8,128)S(1)}, f32[1,2048,128]{2,1,0:T(8,128)}, u32[]{:S(2)}) copy-start(f32[1,2048,128]{2,1,0:T(8,128)} %args_3_.4) | copy-start | bytes 3145732
  10.2 10.2 %collective-permute-start = (bf16[64,2,16,128]{3,2,1,0:T(8,128)(2,1)S(1)}, bf16[64,2,16,128]{3,2,1,0:T(8,128)(2,1)S(1)}, u32[]{:S(2)}, u32[]{:S(2)}) collective-permute-start(bf16[64,2,16,128]{3,2,1,0:T(8,128)(2,1)S(1)} %get-tuple-element.9), channel_id=1, source_target_pairs={{0,1},{1,0},{2,3},{3,2},{4,5},{5,4},{6,7},{7,6},{8,9},{9,8},{10,11... | collective-permute-start | bytes 1572872 | tf_op jit(solution)/shard_map/ppermute | solution.py:41
  35.5 15.8 %copy-start.4 = (f32[1,16,128]{2,1,0:T(8,128)S(1)}, f32[1,16,128]{2,1,0:T(8,128)}, u32[]{:S(2)}) copy-start(f32[1,16,128]{2,1,0:T(8,128)} %oresid_ref.1) | copy-start | bytes 24580
  35.5 15.8 %copy-start.6 = (s32[1,2,16]{2,1,0:T(2,128)S(1)}, s32[1,2,16]{2,1,0:T(2,128)}, u32[]{:S(2)}) copy-start(s32[1,2,16]{2,1,0:T(2,128)} %rank_ref.1) | copy-start | bytes 388
  35.5 15.7 %copy-start.7 = (s32[1,2]{1,0:T(1,128)S(1)}, s32[1,2]{1,0:T(1,128)}, u32[]{:S(2)}) copy-start(s32[1,2]{1,0:T(1,128)} %count_ref.1) | copy-start | bytes 28
  78.6 8.4 %collective-permute-start.1 = (bf16[64,16,128]{2,1,0:T(8,128)(2,1)S(1)}, bf16[64,16,128]{2,1,0:T(8,128)(2,1)S(1)}, u32[]{:S(2)}, u32[]{:S(2)}) collective-permute-start(bf16[64,16,128]{2,1,0:T(8,128)(2,1)S(1)} %bitcast.3), channel_id=1, source_target_pairs={{0,1},{1,0},{2,3},{3,2},{4,5},{5,4},{6,7},{7,6},{8,9},{9,8},{10,11... | collective-permute-start | bytes 786440 | tf_op jit(solution)/shard_map/ppermute | solution.py:41

commit v2 on v1

v2 whole, which is shorter than its diff:
```python
import math

import jax
import jax.numpy as jnp
import numpy as np
from jax import lax
from jax.experimental import pallas as pl
from jax.experimental.pallas import tpu as pltpu
from jax.sharding import Mesh
from jax.sharding import PartitionSpec as P

STEP_SIZE = 0.0625
NX, NZ, NY, NC = 4, 8, 8, 2
CHIPS = NZ * NY
REGION = 16
WIDTH = 128
BF = jnp.bfloat16
F32 = jnp.float32
VMEM_LIMIT = 48 * 1024 * 1024


def groups_along(axes):
    ids = np.arange(NX * NZ * NY * NC).reshape(NX, NZ, NY, NC)
    size = int(np.prod([ids.shape[a] for a in axes]))
    return np.moveaxis(ids, axes, range(4 - len(axes), 4)).reshape(-1, size).tolist()


def exchange(value, axes):
    return lax.all_to_all(
        value, "d", split_axis=0, concat_axis=0, tiled=True, axis_index_groups=groups_along(axes)
    )


def other_core(value):
    pairs = [(i, i ^ 1) for i in range(NX * NZ * NY * NC)]
    return lax.ppermute(value, "d", pairs)


def of_both_cores(value):
    return lax.all_gather(value, "d", axis=0, axis_index_groups=groups_along((3,)))


def local_kernel(scale, core_ref, acts_hbm, cot_hbm, resid_hbm, count_hbm, rank_hbm,
                 resid_ref, keep_ref, give_ref,
                 acts_ref, cot_ref, acc_ref, count_ref, rank_ref, ranks_ref, chosen_ref, sems):
    core = core_ref[0]
    steps, _, rows = acts_ref.shape
    cols = cot_ref.shape[2]
    tiles = cols // WIDTH
    groups = resid_ref.shape[1] // WIDTH

    copies = [
        pltpu.make_async_copy(rank_hbm, rank_ref, sems.at[0]),
        pltpu.make_async_copy(count_hbm, count_ref, sems.at[1]),
        pltpu.make_async_copy(resid_hbm, resid_ref, sems.at[2]),
    ]
    for s in range(steps):
        copies.append(pltpu.make_async_copy(acts_hbm.at[0, s], acts_ref.at[s], sems.at[3 + 2 * s]))
        copies.append(pltpu.make_async_copy(cot_hbm.at[0, s], cot_ref.at[s], sems.at[4 + 2 * s]))
    for i in [0, 1, 3, 4, 2] + list(range(5, 3 + 2 * steps)):
        copies[i].start()

    per = WIDTH // groups
    row_id = lax.broadcasted_iota(jnp.int32, (groups, WIDTH), 0)
    lane_id = lax.broadcasted_iota(jnp.int32, (groups, WIDTH), 1)
    owner_id = lax.broadcasted_iota(jnp.int32, (WIDTH, WIDTH), 0) % per
    block_id = lax.broadcasted_iota(jnp.int32, (WIDTH, WIDTH), 1) // REGION
    place = jnp.where(owner_id == block_id, 1.0, 0.0).astype(BF)
    eye = jnp.where(row_id == lane_id, 1.0, 0.0).astype(BF)
    copies[0].wait()
    copies[1].wait()
    for s in range(steps):
        for r in range(groups):
            ranks_ref[s, r:r + 1, :] = rank_ref[0, s:s + 1, r * WIDTH:(r + 1) * WIDTH]
        count = jnp.broadcast_to(count_ref[0, s:s + 1, :].astype(F32), (groups, WIDTH))
        spread = jnp.where(lane_id // per == row_id, count, 0.0)
        limit = jnp.dot(spread.astype(BF), place, preferred_element_type=F32)
        chosen = jnp.where(ranks_ref[s].astype(F32) < limit, 1.0, 0.0)
        chosen_ref[s] = lax.dot_general(chosen.astype(BF), eye, (((0,), (0,)), ((), ())),
                                        preferred_element_type=F32)

    half = 2 * WIDTH
    for s in range(steps):
        copies[3 + 2 * s].wait()
        copies[4 + 2 * s].wait()
        left = acts_ref[s]
        for h in range(cols // half):
            grad = lax.dot_general(left, cot_ref[s, :, h * half:(h + 1) * half],
                                   (((0,), (0,)), ((), ())), preferred_element_type=F32)
            grad = grad * scale
            for q in range(2):
                acc_ref[pl.ds(2 * h + q, rows, stride=tiles), :] = grad[:, q * WIDTH:(q + 1) * WIDTH]
        if s == 0:
            copies[2].wait()
        columns = chosen_ref[s]
        for me in range(NC):
            @pl.when(core == me)
            def _(me=me, s=s, columns=columns):
                for r in range(groups):
                    span = slice(r * WIDTH, (r + 1) * WIDTH)
                    total = resid_ref[0, span, :] + acc_ref[span, :]
                    mask = jnp.broadcast_to(columns[:, r:r + 1], (WIDTH, WIDTH)) > 0.5
                    resid_ref[0, span, :] = jnp.where(mask, 0.0, total)
                    sent = jnp.where(mask, total, 0.0).astype(BF)
                    for i in range(WIDTH // REGION):
                        owner = r * (WIDTH // REGION) + i
                        to = keep_ref if owner % NC == me else give_ref
                        to[owner // NC, s] = sent[i * REGION:(i + 1) * REGION, :]


def owner_kernel(arrived_ref, oresid_ref, count_ref, rank_ref, out_ref, oresid_out):
    steps = rank_ref.shape[1]
    eye = (lax.broadcasted_iota(jnp.int32, (REGION, REGION), 0)
           == lax.broadcasted_iota(jnp.int32, (REGION, REGION), 1))
    oresid = oresid_ref[0]
    for s in range(steps):
        total = arrived_ref[0, s].astype(F32)
        for k in range(1, arrived_ref.shape[0]):
            total = total + arrived_ref[k, s].astype(F32)
        row = jnp.where(rank_ref[0, s:s + 1, :] < count_ref[0, s], 1.0, 0.0)
        square = jnp.where(eye, jnp.broadcast_to(row, (REGION, REGION)), 0.0)
        passed = jnp.broadcast_to(jnp.sum(square, axis=1, keepdims=True), (REGION, WIDTH)) > 0.5
        total = total + oresid
        going = jnp.where(passed, total, 0.0).astype(BF)
        oresid = jnp.where(passed, 0.0, total)
        for k in range(out_ref.shape[0]):
            out_ref[k, s] = going
    oresid_out[0] = oresid


def update_kernel(arrived_ref, out_ref):
    total = jnp.zeros((REGION, WIDTH), F32)
    for s in range(arrived_ref.shape[1]):
        cross = arrived_ref[0, s].astype(F32)
        for x in range(1, NX):
            cross = cross + arrived_ref[x, s].astype(F32)
        total = total + cross.astype(BF).astype(F32)
    applied = (-STEP_SIZE * total).astype(BF)
    for k in range(out_ref.shape[0]):
        out_ref[k] = applied


def assemble_kernel(halves_ref, out_ref, flat_ref):
    rows, cols = out_ref.shape
    tiles = cols // WIDTH
    for i in range(CHIPS):
        for c in range(NC):
            at = (i * NC + c) * REGION
            flat_ref[at:at + REGION, :] = halves_ref[c, i].astype(F32)
    for t in range(tiles):
        out_ref[:, t * WIDTH:(t + 1) * WIDTH] = flat_ref[pl.ds(t, rows, stride=tiles), :].astype(BF)


def vmem():
    return pl.BlockSpec(memory_space=pltpu.VMEM)


def hbm():
    return pl.BlockSpec(memory_space=pltpu.HBM)


def smem():
    return pl.BlockSpec(memory_space=pltpu.SMEM)


def per_device(acts, cotangent, residual, owner_residual, in_count, in_rank, out_count, out_rank):
    steps, tokens, rows = acts.shape[1:]
    cols = cotangent.shape[3]
    blocks = residual.shape[1]
    scale = 1.0 / math.sqrt(tokens * CHIPS * NC)
    core = (lax.axis_index("d") % NC).astype(jnp.int32).reshape(1)
    params = pltpu.CompilerParams(vmem_limit_bytes=VMEM_LIMIT)

    def local(*args):
        return local_kernel(scale, *args)

    half = (CHIPS, steps, REGION, WIDTH)
    new_residual, keep, give = pl.pallas_call(
        local,
        in_specs=[smem(), hbm(), hbm(), hbm(), hbm(), hbm()],
        out_specs=[vmem(), vmem(), vmem()],
        out_shape=[
            jax.ShapeDtypeStruct(residual.shape, F32),
            jax.ShapeDtypeStruct(half, BF),
            jax.ShapeDtypeStruct(half, BF),
        ],
        scratch_shapes=[
            pltpu.VMEM((steps, tokens, rows), BF),
            pltpu.VMEM((steps, tokens, cols), BF),
            pltpu.VMEM((blocks, WIDTH), F32),
            pltpu.VMEM(in_count.shape, jnp.int32),
            pltpu.VMEM(in_rank.shape, jnp.int32),
            pltpu.VMEM((steps, blocks // WIDTH, WIDTH), jnp.int32),
            pltpu.VMEM((steps, WIDTH, WIDTH), F32),
            pltpu.SemaphoreType.DMA((3 + 2 * steps,)),
        ],
        compiler_params=params,
        name="local",
    )(core, *[pltpu.with_memory_space_constraint(v, pltpu.HBM)
            for v in (acts, cotangent, residual, in_count, in_rank)])

    given = other_core(give)
    pair = (keep.astype(F32) + given.astype(F32)).astype(BF)
    arrived = exchange(pair, (1, 2))

    outgoing, new_owner = pl.pallas_call(
        owner_kernel,
        in_specs=[vmem(), vmem(), smem(), vmem()],
        out_specs=[vmem(), vmem()],
        out_shape=[
            jax.ShapeDtypeStruct((NX, steps, REGION, WIDTH), BF),
            jax.ShapeDtypeStruct(owner_residual.shape, F32),
        ],
        compiler_params=params,
        name="owner",
    )(arrived, owner_residual, out_count, out_rank)

    copies = pl.pallas_call(
        update_kernel,
        in_specs=[vmem()],
        out_specs=vmem(),
        out_shape=jax.ShapeDtypeStruct((CHIPS, REGION, WIDTH), BF),
        compiler_params=params,
        name="update",
    )(exchange(outgoing, (0,)))
    halves = of_both_cores(exchange(copies, (1, 2)))
    applied = pl.pallas_call(
        assemble_kernel,
        in_specs=[vmem()],
        out_specs=vmem(),
        out_shape=jax.ShapeDtypeStruct((rows, cols), BF),
        scratch_shapes=[pltpu.VMEM((blocks, WIDTH), F32)],
        compiler_params=params,
        name="assemble",
    )(halves)
    return applied, new_residual, new_owner


def solution(mesh):
    flat = Mesh(mesh.devices.reshape(-1), ("d",))
    spec = P("d")
    return jax.shard_map(
        per_device,
        mesh=flat,
        in_specs=(spec,) * 8,
        out_specs=(P(), spec, spec),
        check_vma=False,
    )
```

time: 88.5 us -> 79 us (0.89)
  starting transfers between devices: 16 us -> 8.77 us
  blocking collectives: 56.6 us -> 61.4 us
  local copies, waits for them, and re-layouts: 4.39 us -> 0.02 us
  Pallas kernels: 7.45 us -> 6.14 us
  waiting for transfers between devices: 2.65 us -> 1.51 us
    ppermute x2 -> x1, starting transfers between devices: 16 us -> 8.77 us  [other_core(): return lax.ppermute(value, 'd', pairs)]
    all_gather x0 -> x1, blocking collectives: none -> 5.78 us  [of_both_cores(): lax.all_gather(value, 'd', axis=0, axis_index_groups=groups_along((3,)))]
    unnamed x16 -> x6, local copies, waits for them, and re-layouts: 4.39 us -> 0.02 us
    pallas_call x2, Pallas kernels: 6.17 us -> 4.88 us  [the longest x1 3.92 us: per_device(): pl.pallas_call(local, in_specs=[smem(), hbm(), hbm(), hbm(), hbm(), hbm()...]
    ppermute x2 -> x1, waiting for transfers between devices: 2.65 us -> 1.51 us  [other_core(): return lax.ppermute(value, 'd', pairs)]
    all_to_all x4 -> x3, blocking collectives: 56.6 us -> 55.6 us  [exchange(): lax.all_to_all(value, 'd', split_axis=0, concat_axis=0, tiled=True, axis_...]
  transfers between devices with their start and end apart: 2 -> 1, of which waited for: 2 -> 1; matrix products, arithmetic and copies ran while one was open for 0% -> 0% of each run, Pallas kernels for 0% -> 0%
where the time goes in v2:
time: 79 us; the launch traced here: 78.6 us
  blocking collectives  61.4 us (78%)
  starting transfers between devices  8.77 us (11%)
  Pallas kernels  6.14 us (8%)
  waiting for transfers between devices  1.51 us (2%)
    all_to_all x3, blocking collectives, exchange(): lax.all_to_all(value, 'd', split_axis=0, concat_axis=0, tiled=True, axis_...  55.6 us
    ppermute x1, starting transfers between devices, other_core(): return lax.ppermute(value, 'd', pairs)  8.77 us
    all_gather x1, blocking collectives, of_both_cores(): lax.all_gather(value, 'd', axis=0, axis_index_groups=groups_along((3,)))  5.78 us
    pallas_call x1, Pallas kernels, per_device(): pl.pallas_call(local, in_specs=[smem(), hbm(), hbm(), hbm(), hbm(), hbm()...  3.92 us
  transfers between devices with their start and end apart: 1, of which 1 were waited for; matrix products, arithmetic and copies ran while one was open for 0% of the time, Pallas kernels for 0%

profile of v2, /device:TPU:1, one launch (start us, length us, event | category | flops | bytes accessed | tf_op | source)
XLA Modules:
  0.0 78.6 jit_solution(12917934482852659462)
XLA Ops:
  0.6 3.9 %local.1 = (f32[1,2048,128]{2,1,0:T(8,128)}, bf16[64,2,16,128]{3,2,1,0:T(8,128)(2,1)S(1)}, bf16[64,2,16,128]{3,2,1,0:T(8,128)(2,1)S(1)}) custom-call(s32[1]{0:T(128)} %bitcast.args_0_, bf16[1,2,512,512]{3,2,1,0:T(8,128)(2,1)} %args_1_.4, bf16[1,2,512,512]{3,2,1,0:T(8,128)(2,1)} %args_2_.4, f32[1,2048,128]{2,1,0:T(8,128)} %args_3_.4, s32[1,2,128]{2,1,0:T(2,128)} %args_4_.4, ...), custom_call_target="tpu_custom_call" | custom-call | tf_op jit(solution)/shard_map/local/pallas_call | solution.py:178
  4.6 8.8 %collective-permute-start = (bf16[64,2,16,128]{3,2,1,0:T(8,128)(2,1)S(1)}, bf16[64,2,16,128]{3,2,1,0:T(8,128)(2,1)S(1)}, u32[]{:S(2)}, u32[]{:S(2)}) collective-permute-start(bf16[64,2,16,128]{3,2,1,0:T(8,128)(2,1)S(1)} %get-tuple-element.9), channel_id=1, source_target_pairs={{0,1},{1,0},{2,3},{3,2},{4,5},{5,4},{6,7},{7,6},{8,9},{9,8},{10,11... | collective-permute-start | bytes 1572872 | tf_op jit(solution)/shard_map/ppermute | solution.py:36
  13.3 1.5 %collective-permute-done = bf16[64,2,16,128]{3,2,1,0:T(8,128)(2,1)S(1)} collective-permute-done((bf16[64,2,16,128]{3,2,1,0:T(8,128)(2,1)S(1)}, bf16[64,2,16,128]{3,2,1,0:T(8,128)(2,1)S(1)}, u32[]{:S(2)}, u32[]{:S(2)}) %collective-permute-start) | collective-permute-done | bytes 524320 | tf_op jit(solution)/shard_map/ppermute | solution.py:36
  14.9 0.1 add_convert_fusion
  15.0 0.0 copy-start
  15.0 0.0 copy-start.1
  15.0 0.0 copy-start.2
  15.0 28.5 %all_to_all.15.arrived_ref = bf16[64,2,16,128]{3,2,1,0:T(8,128)(2,1)S(1)} all-to-all(bf16[64,2,16,128]{3,2,1,0:T(8,128)(2,1)S(1)} %add_convert_fusion), channel_id=1, replica_groups={{0,2,4,6,8,10,12,14,16,18,20,22,24,26,28,30,32,34,36,38,40,42,44,46,48,..., dimensions={0} | all-to-all | bytes 1048576 | tf_op jit(solution)/shard_map/all_to_all | solution.py:29
  43.5 0.0 copy-done
  43.5 0.0 copy-done.1
  43.5 0.0 copy-done.2
  43.5 1.2 %owner.1 = (bf16[4,2,16,128]{3,2,1,0:T(8,128)(2,1)S(1)}, f32[1,16,128]{2,1,0:T(8,128)}) custom-call(bf16[64,2,16,128]{3,2,1,0:T(8,128)(2,1)S(1)} %all_to_all.15.arrived_ref, f32[1,16,128]{2,1,0:T(8,128)S(1)} %copy-done, s32[1,2]{1,0:T(1,128)S(1)} %copy-done.2, s32[1,2,16]{2,1,0:T(2,128)S(1)} %copy-done.1), custom_call_target="tpu_custom_call" | custom-call | tf_op jit(solution)/shard_map/owner/pallas_call | solution.py:206
  44.8 8.1 %all_to_all.16.arrived_ref = bf16[4,2,16,128]{3,2,1,0:T(8,128)(2,1)S(1)} all-to-all(bf16[4,2,16,128]{3,2,1,0:T(8,128)(2,1)S(1)} %get-tuple-element.10), channel_id=1, replica_groups={{0,128,256,384},{1,129,257,385},{2,130,258,386},{3,131,259,387},{4,132,..., dimensions={0} | all-to-all | bytes 65536 | tf_op jit(solution)/shard_map/all_to_all | solution.py:29
  52.9 19.0 %all_to_all.17 = bf16[64,16,128]{2,1,0:T(8,128)(2,1)S(1)} all-to-all(bf16[64,16,128]{2,1,0:T(8,128)(2,1)S(1)} %update.1), channel_id=1, replica_groups={{0,2,4,6,8,10,12,14,16,18,20,22,24,26,28,30,32,34,36,38,40,42,44,46,48,..., dimensions={0} | all-to-all | bytes 524288 | tf_op jit(solution)/shard_map/all_to_all | solution.py:29
  71.9 5.8 %all-gather = bf16[128,16,128]{2,1,0:T(8,128)(2,1)S(1)} all-gather(bf16[64,16,128]{2,1,0:T(8,128)(2,1)S(1)} %all_to_all.17), channel_id=2, replica_groups={{0,1},{2,3},{4,5},{6,7},{8,9},{10,11},{12,13},{14,15},{16,17},{18,19},{..., dimensions={0}, use_global_device_ids=true | all-gather | bytes 786432 | tf_op jit(solution)/shard_map/all_gather | solution.py:40
  77.7 1.0 %assemble.1 = bf16[512,512]{1,0:T(8,128)(2,1)} custom-call(bf16[2,64,16,128]{3,2,1,0:T(8,128)(2,1)S(1)} %bitcast.2), custom_call_target="tpu_custom_call" | custom-call | tf_op jit(solution)/shard_map/assemble/pallas_call | solution.py:227
  (1 shorter events, 0.0 us)
Async XLA Ops:
  4.6 10.3 %collective-permute-start = (bf16[64,2,16,128]{3,2,1,0:T(8,128)(2,1)S(1)}, bf16[64,2,16,128]{3,2,1,0:T(8,128)(2,1)S(1)}, u32[]{:S(2)}, u32[]{:S(2)}) collective-permute-start(bf16[64,2,16,128]{3,2,1,0:T(8,128)(2,1)S(1)} %get-tuple-element.9), channel_id=1, source_target_pairs={{0,1},{1,0},{2,3},{3,2},{4,5},{5,4},{6,7},{7,6},{8,9},{9,8},{10,11... | collective-permute-start | bytes 1572872 | tf_op jit(solution)/shard_map/ppermute | solution.py:36
  15.0 28.5 %copy-start = (f32[1,16,128]{2,1,0:T(8,128)S(1)}, f32[1,16,128]{2,1,0:T(8,128)}, u32[]{:S(2)}) copy-start(f32[1,16,128]{2,1,0:T(8,128)} %oresid_ref.1) | copy-start | bytes 24580
  15.0 28.5 %copy-start.1 = (s32[1,2,16]{2,1,0:T(2,128)S(1)}, s32[1,2,16]{2,1,0:T(2,128)}, u32[]{:S(2)}) copy-start(s32[1,2,16]{2,1,0:T(2,128)} %rank_ref.1) | copy-start | bytes 388
  15.0 28.5 %copy-start.2 = (s32[1,2]{1,0:T(1,128)S(1)}, s32[1,2]{1,0:T(1,128)}, u32[]{:S(2)}) copy-start(s32[1,2]{1,0:T(1,128)} %count_ref.1) | copy-start | bytes 28

commit v3 on v2

--- a/solution.py
+++ b/solution.py
@@ -25,10 +25,25 @@
     return np.moveaxis(ids, axes, range(4 - len(axes), 4)).reshape(-1, size).tolist()
 
 
-def exchange(value, axes):
+def lines(axes0, axes1):
+    return ([g for g in groups_along(axes0) if g[0] % NC == 0]
+            + [g for g in groups_along(axes1) if g[0] % NC == 1])
+
+
+def exchange(value, groups):
     return lax.all_to_all(
-        value, "d", split_axis=0, concat_axis=0, tiled=True, axis_index_groups=groups_along(axes)
+        value, "d", split_axis=0, concat_axis=0, tiled=True, axis_index_groups=groups
     )
+
+
+def from_pod(value, shift):
+    ids = np.arange(NX * NZ * NY * NC).reshape(NX, -1)
+    pairs = list(zip(ids.reshape(-1).tolist(), np.roll(ids, -shift, axis=0).reshape(-1).tolist()))
+    return lax.ppermute(value, "d", pairs)
+
+
+def place_of(core, z, y):
+    return z * NY + y if core == 0 else y * NZ + z
 
 
 def other_core(value):
@@ -104,40 +119,69 @@
                     sent = jnp.where(mask, total, 0.0).astype(BF)
                     for i in range(WIDTH // REGION):
                         owner = r * (WIDTH // REGION) + i
-                        to = keep_ref if owner % NC == me else give_ref
-                        to[owner // NC, s] = sent[i * REGION:(i + 1) * REGION, :]
-
-
-def owner_kernel(arrived_ref, oresid_ref, count_ref, rank_ref, out_ref, oresid_out):
-    steps = rank_ref.shape[1]
+                        z, y, c = owner // (NY * NC), (owner // NC) % NY, owner % NC
+                        at = (place_of(c, z, y) * steps + s) * REGION
+                        to = keep_ref if c == me else give_ref
+                        to[at:at + REGION, :] = sent[i * REGION:(i + 1) * REGION, :]
+
+
+def store_kernel(after_ref, value_ref, out_hbm, sem):
+    copy = pltpu.make_async_copy(value_ref, out_hbm, sem)
+    copy.start()
+    copy.wait()
+
+
+def facts_kernel(after_ref, oresid_ref, count_ref, rank_ref, out_ref):
     eye = (lax.broadcasted_iota(jnp.int32, (REGION, REGION), 0)
            == lax.broadcasted_iota(jnp.int32, (REGION, REGION), 1))
-    oresid = oresid_ref[0]
-    for s in range(steps):
-        total = arrived_ref[0, s].astype(F32)
-        for k in range(1, arrived_ref.shape[0]):
-            total = total + arrived_ref[k, s].astype(F32)
-        row = jnp.where(rank_ref[0, s:s + 1, :] < count_ref[0, s], 1.0, 0.0)
+    code = jnp.zeros((REGION, 1), F32)
+    for s in range(rank_ref.shape[1]):
+        count = jnp.broadcast_to(count_ref[0:1, s:s + 1], (1, REGION))
+        row = jnp.where(rank_ref[0, s:s + 1, :] < count, float(1 << s), 0.0)
         square = jnp.where(eye, jnp.broadcast_to(row, (REGION, REGION)), 0.0)
-        passed = jnp.broadcast_to(jnp.sum(square, axis=1, keepdims=True), (REGION, WIDTH)) > 0.5
-        total = total + oresid
-        going = jnp.where(passed, total, 0.0).astype(BF)
-        oresid = jnp.where(passed, 0.0, total)
-        for k in range(out_ref.shape[0]):
-            out_ref[k, s] = going
-    oresid_out[0] = oresid
-
-
-def update_kernel(arrived_ref, out_ref):
-    total = jnp.zeros((REGION, WIDTH), F32)
-    for s in range(arrived_ref.shape[1]):
-        cross = arrived_ref[0, s].astype(F32)
-        for x in range(1, NX):
-            cross = cross + arrived_ref[x, s].astype(F32)
-        total = total + cross.astype(BF).astype(F32)
+        code = code + jnp.sum(square, axis=1, keepdims=True)
+    out_ref[0] = oresid_ref[0]
+    out_ref[1] = jnp.broadcast_to(code, (REGION, WIDTH))
+
+
+def line_kernel(arrived_ref, out_ref):
+    peers, near, steps = arrived_ref.shape[:3]
+    for a in range(near):
+        for s in range(steps):
+            total = arrived_ref[0, a, s].astype(F32)
+            for k in range(1, peers):
+                total = total + arrived_ref[k, a, s].astype(F32)
+            part = total.astype(BF)
+            for x in range(NX):
+                out_ref[x * near + a, s] = part
+
+
+def owner_kernel(pod_ref, arrived_ref, *refs):
+    facts, (copies_ref, last_ref, keeps_ref, all_ref, lasts_ref) = refs[:NX], refs[NX:]
+    pod = pod_ref[0]
+    for k in range(NX):
+        all_ref[(pod + (NX - k)) % NX] = facts[k][...]
+    near = arrived_ref.shape[0] // NX
+    crosses = [jnp.zeros((REGION, WIDTH), F32) for _ in range(2)]
+    for x in range(NX):
+        oresid = all_ref[x, 0]
+        code = all_ref[x, 1]
+        passes = [(code == 1.0) | (code == 3.0), code >= 2.0]
+        for s in range(2):
+            total = arrived_ref[x * near, s].astype(F32)
+            for k in range(1, near):
+                total = total + arrived_ref[x * near + k, s].astype(F32)
+            total = total + oresid
+            crosses[s] = crosses[s] + jnp.where(passes[s], total, 0.0)
+            oresid = jnp.where(passes[s], 0.0, total)
+            if s == 1:
+                lasts_ref[x] = total
+    total = crosses[0].astype(BF).astype(F32) + crosses[1].astype(BF).astype(F32)
     applied = (-STEP_SIZE * total).astype(BF)
-    for k in range(out_ref.shape[0]):
-        out_ref[k] = applied
+    for k in range(copies_ref.shape[0]):
+        copies_ref[k] = applied
+    last_ref[...] = lasts_ref[pod]
+    keeps_ref[...] = jnp.where(all_ref[pod, 1] >= 2.0, 0.0, 1.0)
 
 
 def assemble_kernel(halves_ref, out_ref, flat_ref):
@@ -155,6 +199,10 @@
     return pl.BlockSpec(memory_space=pltpu.VMEM)
 
 
+def anywhere():
+    return pl.BlockSpec(memory_space=pl.ANY)
+
+
 def hbm():
     return pl.BlockSpec(memory_space=pltpu.HBM)
 
@@ -174,15 +222,16 @@
     def local(*args):
         return local_kernel(scale, *args)
 
-    half = (CHIPS, steps, REGION, WIDTH)
-    new_residual, keep, give = pl.pallas_call(
+    pod = (lax.axis_index("d") // (CHIPS * NC)).astype(jnp.int32).reshape(1)
+    size = CHIPS * steps * REGION
+    new_resid, keep, give = pl.pallas_call(
         local,
         in_specs=[smem(), hbm(), hbm(), hbm(), hbm(), hbm()],
         out_specs=[vmem(), vmem(), vmem()],
         out_shape=[
             jax.ShapeDtypeStruct(residual.shape, F32),
-            jax.ShapeDtypeStruct(half, BF),
-            jax.ShapeDtypeStruct(half, BF),
+            jax.ShapeDtypeStruct((size, WIDTH), BF),
+            jax.ShapeDtypeStruct((size, WIDTH), BF),
         ],
         scratch_shapes=[
             pltpu.VMEM((steps, tokens, rows), BF),
@@ -197,33 +246,57 @@
         compiler_params=params,
         name="local",
     )(core, *[pltpu.with_memory_space_constraint(v, pltpu.HBM)
-            for v in (acts, cotangent, residual, in_count, in_rank)])
+              for v in (acts, cotangent, residual, in_count, in_rank)])
 
     given = other_core(give)
     pair = (keep.astype(F32) + given.astype(F32)).astype(BF)
-    arrived = exchange(pair, (1, 2))
-
-    outgoing, new_owner = pl.pallas_call(
-        owner_kernel,
-        in_specs=[vmem(), vmem(), smem(), vmem()],
-        out_specs=[vmem(), vmem()],
-        out_shape=[
-            jax.ShapeDtypeStruct((NX, steps, REGION, WIDTH), BF),
-            jax.ShapeDtypeStruct(owner_residual.shape, F32),
-        ],
-        compiler_params=params,
-        name="owner",
-    )(arrived, owner_residual, out_count, out_rank)
-
-    copies = pl.pallas_call(
-        update_kernel,
+    first = exchange(pair.reshape(NZ, NY, steps, REGION, WIDTH), lines((1,), (2,)))
+
+    facts = pl.pallas_call(
+        facts_kernel,
+        in_specs=[anywhere(), vmem(), vmem(), vmem()],
+        out_specs=vmem(),
+        out_shape=jax.ShapeDtypeStruct((2, REGION, WIDTH), F32),
+        compiler_params=params,
+        name="facts",
+    )(pair, owner_residual, out_count, out_rank)
+    facts = [facts] + [from_pod(facts, k) for k in range(1, NX)]
+
+    line = pl.pallas_call(
+        line_kernel,
         in_specs=[vmem()],
         out_specs=vmem(),
-        out_shape=jax.ShapeDtypeStruct((CHIPS, REGION, WIDTH), BF),
-        compiler_params=params,
-        name="update",
-    )(exchange(outgoing, (0,)))
-    halves = of_both_cores(exchange(copies, (1, 2)))
+        out_shape=jax.ShapeDtypeStruct((NX * NY, steps, REGION, WIDTH), BF),
+        compiler_params=params,
+        name="line",
+    )(first)
+    second = exchange(line, lines((0, 2), (0, 1)))
+    new_residual = pl.pallas_call(
+        store_kernel,
+        in_specs=[anywhere(), vmem()],
+        out_specs=hbm(),
+        out_shape=jax.ShapeDtypeStruct(residual.shape, F32),
+        scratch_shapes=[pltpu.SemaphoreType.DMA],
+        compiler_params=params,
+        name="store",
+    )(line, new_resid)
+
+    tile = jax.ShapeDtypeStruct((REGION, WIDTH), F32)
+    copies, last, keeps = pl.pallas_call(
+        owner_kernel,
+        in_specs=[smem()] + [vmem()] * (1 + NX),
+        out_specs=[vmem(), vmem(), vmem()],
+        out_shape=[jax.ShapeDtypeStruct((CHIPS, REGION, WIDTH), BF), tile, tile],
+        scratch_shapes=[
+            pltpu.VMEM((NX, 2, REGION, WIDTH), F32),
+            pltpu.VMEM((NX, REGION, WIDTH), F32),
+        ],
+        compiler_params=params,
+        name="owner",
+    )(pod, second, *facts)
+    new_owner = jnp.where(keeps > 0.5, last, 0.0)[None]
+
+    halves = of_both_cores(exchange(copies, groups_along((1, 2))))
     applied = pl.pallas_call(
         assemble_kernel,
         in_specs=[vmem()],

time: 79 us -> 82.8 us (1.048)
  blocking collectives: 61.4 us -> 21.6 us
  starting transfers between devices: 8.77 us -> 38.5 us
  waiting for transfers between devices: 1.51 us -> 14.1 us
    all_to_all x3 -> x1, blocking collectives: 55.6 us -> 14.8 us  [exchange(): lax.all_to_all(value, 'd', split_axis=0, concat_axis=0, tiled=True, axis_...]
    all_to_all x0 -> x2, starting transfers between devices: none -> 19.2 us  [exchange(): lax.all_to_all(value, 'd', split_axis=0, concat_axis=0, tiled=True, axis_...]
    all_to_all x0 -> x2, waiting for transfers between devices: none -> 10.9 us  [exchange(): lax.all_to_all(value, 'd', split_axis=0, concat_axis=0, tiled=True, axis_...]
    ppermute x0 -> x3, starting transfers between devices: none -> 10.5 us  [from_pod(): return lax.ppermute(value, 'd', pairs)]
    ppermute x0 -> x3, waiting for transfers between devices: none -> 1.69 us  [from_pod(): return lax.ppermute(value, 'd', pairs)]
    pallas_call x2 -> x4, Pallas kernels: 1.26 us -> 2.68 us  [the longest x1 0.98 us: per_device(): pl.pallas_call(store_kernel, in_specs=[anywhere(), vmem()], out_specs=hbm...]
    pallas_call x1, Pallas kernels: 3.92 us -> 2.95 us  [per_device(): pl.pallas_call(local, in_specs=[smem(), hbm(), hbm(), hbm(), hbm(), hbm()...]
    all_gather x1, blocking collectives: 5.78 us -> 6.75 us  [of_both_cores(): lax.all_gather(value, 'd', axis=0, axis_index_groups=groups_along((3,)))]
  transfers between devices with their start and end apart: 1 -> 6, of which waited for: 1 -> 3; matrix products, arithmetic and copies ran while one was open for 0% -> 1% of each run, Pallas kernels for 0% -> 1%
where the time goes in v3:
time: 82.8 us; the launch traced here: 82.3 us
  starting transfers between devices  38.5 us (46%)
  blocking collectives  21.6 us (26%)
  waiting for transfers between devices  14.1 us (17%)
  Pallas kernels  6.58 us (8%)
    all_to_all x2, starting transfers between devices, exchange(): lax.all_to_all(value, 'd', split_axis=0, concat_axis=0, tiled=True, axis_...  19.2 us
    all_to_all x1, blocking collectives, exchange(): lax.all_to_all(value, 'd', split_axis=0, concat_axis=0, tiled=True, axis_...  14.8 us
    all_to_all x2, waiting for transfers between devices, exchange(): lax.all_to_all(value, 'd', split_axis=0, concat_axis=0, tiled=True, axis_...  10.9 us
    ppermute x3, starting transfers between devices, from_pod(): return lax.ppermute(value, 'd', pairs)  10.5 us
    ppermute x1, starting transfers between devices, other_core(): return lax.ppermute(value, 'd', pairs)  8.78 us
    all_gather x1, blocking collectives, of_both_cores(): lax.all_gather(value, 'd', axis=0, axis_index_groups=groups_along((3,)))  6.75 us
    pallas_call x1, Pallas kernels, per_device(): pl.pallas_call(local, in_specs=[smem(), hbm(), hbm(), hbm(), hbm(), hbm()...  2.95 us
    ppermute x3, waiting for transfers between devices, from_pod(): return lax.ppermute(value, 'd', pairs)  1.69 us
  transfers between devices with their start and end apart: 6, of which 3 were waited for; matrix products, arithmetic and copies ran while one was open for 1% of the time, Pallas kernels for 1%

profile of v3, /device:TPU:1, one launch (start us, length us, event | category | flops | bytes accessed | tf_op | source)
XLA Modules:
  0.0 82.3 jit_solution(10479262682013088450)
XLA Ops:
  0.6 3.0 %local.1 = (f32[1,2048,128]{2,1,0:T(8,128)S(1)}, bf16[2048,128]{1,0:T(8,128)(2,1)S(1)}, bf16[2048,128]{1,0:T(8,128)(2,1)S(1)}) custom-call(s32[1]{0:T(128)} %bitcast.1.args_0_, bf16[1,2,512,512]{3,2,1,0:T(8,128)(2,1)} %args_1_.4, bf16[1,2,512,512]{3,2,1,0:T(8,128)(2,1)} %args_2_.4, f32[1,2048,128]{2,1,0:T(8,128)} %args_3_.4, s32[1,2,128]{2,1,0:T(2,128)} %args_4_.4, ...), custom_call_target="tpu_custom_call" | custom-call | tf_op jit(solution)/shard_map/local/pallas_call | solution.py:227
  3.6 8.8 %collective-permute-start = (bf16[2048,128]{1,0:T(8,128)(2,1)S(1)}, bf16[2048,128]{1,0:T(8,128)(2,1)S(1)}, u32[]{:S(2)}, u32[]{:S(2)}) collective-permute-start(bf16[2048,128]{1,0:T(8,128)(2,1)S(1)} %get-tuple-element.10), channel_id=1, source_target_pairs={{0,1},{1,0},{2,3},{3,2},{4,5},{5,4},{6,7},{7,6},{8,9},{9,8},{10,11... | collective-permute-start | bytes 1572872 | tf_op jit(solution)/shard_map/ppermute | solution.py:51
  12.4 1.5 %collective-permute-done = bf16[2048,128]{1,0:T(8,128)(2,1)S(1)} collective-permute-done((bf16[2048,128]{1,0:T(8,128)(2,1)S(1)}, bf16[2048,128]{1,0:T(8,128)(2,1)S(1)}, u32[]{:S(2)}, u32[]{:S(2)}) %collective-permute-start) | collective-permute-done | bytes 524320 | tf_op jit(solution)/shard_map/ppermute | solution.py:51
  13.9 0.1 add_convert_fusion.after_ref
  14.0 14.8 %all_to_all.15.arrived_ref = bf16[8,8,2,16,128]{4,3,2,1,0:T(8,128)(2,1)S(1)} all-to-all(bf16[8,8,2,16,128]{4,3,2,1,0:T(8,128)(2,1)S(1)} %bitcast.6), channel_id=1, replica_groups={{0,16,32,48,64,80,96,112},{2,18,34,50,66,82,98,114},{4,20,36,52,68,84,1..., dimensions={0} | all-to-all | bytes 1048576 | tf_op jit(solution)/shard_map/all_to_all | solution.py:34
  28.9 0.8 line.1.after_ref
  29.7 0.0 copy-start
  29.7 0.0 copy-start.1
  29.7 0.0 copy-start.2
  29.7 11.6 %all-to-all-start.1 = ((bf16[32,2,16,128]{3,2,1,0:T(8,128)(2,1)}), bf16[32,2,16,128]{3,2,1,0:T(8,128)(2,1)S(1)}, u32[]{:S(2)}, u32[]{:S(2)}) async-start(bf16[32,2,16,128]{3,2,1,0:T(8,128)(2,1)} %line.1.after_ref), calls=%async_computation.1 | async-start | bytes 524288 | tf_op jit(solution)/shard_map/all_to_all | solution.py:34
  41.2 0.0 copy-done
  41.3 0.0 copy-done.1
  41.3 0.0 copy-done.2
  41.3 0.1 facts.1.refs_0_
  41.4 3.1 %collective-permute-start.1 = (f32[2,16,128]{2,1,0:T(8,128)S(1)}, f32[2,16,128]{2,1,0:T(8,128)S(1)}, u32[]{:S(2)}, u32[]{:S(2)}) collective-permute-start(f32[2,16,128]{2,1,0:T(8,128)S(1)} %facts.1.refs_0_), channel_id=1, source_target_pairs={{0,128},{1,129},{2,130},{3,131},{4,132},{5,133},{6,134},{7,135},{8... | collective-permute-start | bytes 49160 | tf_op jit(solution)/shard_map/ppermute | solution.py:42
  44.6 4.3 %collective-permute-start.2 = (f32[2,16,128]{2,1,0:T(8,128)S(1)}, f32[2,16,128]{2,1,0:T(8,128)S(1)}, u32[]{:S(2)}, u32[]{:S(2)}) collective-permute-start(f32[2,16,128]{2,1,0:T(8,128)S(1)} %facts.1.refs_0_), channel_id=1, source_target_pairs={{0,256},{1,257},{2,258},{3,259},{4,260},{5,261},{6,262},{7,263},{8... | collective-permute-start | bytes 49160 | tf_op jit(solution)/shard_map/ppermute | solution.py:42
  48.9 3.1 %collective-permute-start.3 = (f32[2,16,128]{2,1,0:T(8,128)S(1)}, f32[2,16,128]{2,1,0:T(8,128)S(1)}, u32[]{:S(2)}, u32[]{:S(2)}) collective-permute-start(f32[2,16,128]{2,1,0:T(8,128)S(1)} %facts.1.refs_0_), channel_id=1, source_target_pairs={{0,384},{1,385},{2,386},{3,387},{4,388},{5,389},{6,390},{7,391},{8... | collective-permute-start | bytes 49160 | tf_op jit(solution)/shard_map/ppermute | solution.py:42
  52.0 0.0 collective-permute-done.1.refs_1_
  52.0 0.0 collective-permute-done.2.refs_2_
  52.0 1.7 %collective-permute-done.3.refs_3_ = f32[2,16,128]{2,1,0:T(8,128)S(1)} collective-permute-done((f32[2,16,128]{2,1,0:T(8,128)S(1)}, f32[2,16,128]{2,1,0:T(8,128)S(1)}, u32[]{:S(2)}, u32[]{:S(2)}) %collective-permute-start.3) | collective-permute-done | bytes 16416 | tf_op jit(solution)/shard_map/ppermute | solution.py:42
  53.7 0.0 all-to-all-done.1.arrived_ref
  53.7 0.8 owner.1
  54.5 7.6 %all-to-all-start.2 = ((bf16[64,16,128]{2,1,0:T(8,128)(2,1)}), bf16[64,16,128]{2,1,0:T(8,128)(2,1)S(1)}, u32[]{:S(2)}, u32[]{:S(2)}) async-start(bf16[64,16,128]{2,1,0:T(8,128)(2,1)} %get-tuple-element.11), calls=%async_computation.2 | async-start | bytes 524288 | tf_op jit(solution)/shard_map/all_to_all | solution.py:34
  62.1 1.0 %store.1 = f32[1,2048,128]{2,1,0:T(8,128)} custom-call(bf16[32,2,16,128]{3,2,1,0:T(8,128)(2,1)} %line.1.after_ref, f32[1,2048,128]{2,1,0:T(8,128)S(1)} %get-tuple-element.12.value_ref), custom_call_target="tpu_custom_call" | custom-call | tf_op jit(solution)/shard_map/store/pallas_call | solution.py:274
  63.1 0.6 select_bitcast_fusion
  63.7 10.9 %all-to-all-done.2 = bf16[64,16,128]{2,1,0:T(8,128)(2,1)S(1)} async-done(((bf16[64,16,128]{2,1,0:T(8,128)(2,1)}), bf16[64,16,128]{2,1,0:T(8,128)(2,1)S(1)}, u32[]{:S(2)}, u32[]{:S(2)}) %all-to-all-start.2) | async-done | bytes 262176 | tf_op jit(solution)/shard_map/all_to_all | solution.py:34
  74.6 6.8 %all-gather = bf16[128,16,128]{2,1,0:T(8,128)(2,1)S(1)} all-gather(bf16[64,16,128]{2,1,0:T(8,128)(2,1)S(1)} %all-to-all-done.2), channel_id=2, replica_groups={{0,1},{2,3},{4,5},{6,7},{8,9},{10,11},{12,13},{14,15},{16,17},{18,19},{..., dimensions={0}, use_global_device_ids=true | all-gather | bytes 786432 | tf_op jit(solution)/shard_map/all_gather | solution.py:55
  81.3 1.0 %assemble.1 = bf16[512,512]{1,0:T(8,128)(2,1)} custom-call(bf16[2,64,16,128]{3,2,1,0:T(8,128)(2,1)S(1)} %bitcast.7), custom_call_target="tpu_custom_call" | custom-call | tf_op jit(solution)/shard_map/assemble/pallas_call | solution.py:300
Async XLA Ops:
  3.6 10.3 %collective-permute-start = (bf16[2048,128]{1,0:T(8,128)(2,1)S(1)}, bf16[2048,128]{1,0:T(8,128)(2,1)S(1)}, u32[]{:S(2)}, u32[]{:S(2)}) collective-permute-start(bf16[2048,128]{1,0:T(8,128)(2,1)S(1)} %get-tuple-element.10), channel_id=1, source_target_pairs={{0,1},{1,0},{2,3},{3,2},{4,5},{5,4},{6,7},{7,6},{8,9},{9,8},{10,11... | collective-permute-start | bytes 1572872 | tf_op jit(solution)/shard_map/ppermute | solution.py:51
  29.7 11.6 %copy-start = (f32[1,16,128]{2,1,0:T(8,128)S(1)}, f32[1,16,128]{2,1,0:T(8,128)}, u32[]{:S(2)}) copy-start(f32[1,16,128]{2,1,0:T(8,128)} %oresid_ref.1) | copy-start | bytes 24580
  29.7 11.6 %copy-start.1 = (s32[1,2,16]{2,1,0:T(2,128)S(1)}, s32[1,2,16]{2,1,0:T(2,128)}, u32[]{:S(2)}) copy-start(s32[1,2,16]{2,1,0:T(2,128)} %rank_ref.1) | copy-start | bytes 388
  29.7 11.6 %copy-start.2 = (s32[1,2]{1,0:T(1,128)S(1)}, s32[1,2]{1,0:T(1,128)}, u32[]{:S(2)}) copy-start(s32[1,2]{1,0:T(1,128)} %count_ref.1) | copy-start | bytes 28
  29.7 24.0 %all-to-all-start.1 = ((bf16[32,2,16,128]{3,2,1,0:T(8,128)(2,1)}), bf16[32,2,16,128]{3,2,1,0:T(8,128)(2,1)S(1)}, u32[]{:S(2)}, u32[]{:S(2)}) async-start(bf16[32,2,16,128]{3,2,1,0:T(8,128)(2,1)} %line.1.after_ref), calls=%async_computation.1 | async-start | bytes 524288 | tf_op jit(solution)/shard_map/all_to_all | solution.py:34
  41.4 10.6 %collective-permute-start.1 = (f32[2,16,128]{2,1,0:T(8,128)S(1)}, f32[2,16,128]{2,1,0:T(8,128)S(1)}, u32[]{:S(2)}, u32[]{:S(2)}) collective-permute-start(f32[2,16,128]{2,1,0:T(8,128)S(1)} %facts.1.refs_0_), channel_id=1, source_target_pairs={{0,128},{1,129},{2,130},{3,131},{4,132},{5,133},{6,134},{7,135},{8... | collective-permute-start | bytes 49160 | tf_op jit(solution)/shard_map/ppermute | solution.py:42
  44.6 7.4 %collective-permute-start.2 = (f32[2,16,128]{2,1,0:T(8,128)S(1)}, f32[2,16,128]{2,1,0:T(8,128)S(1)}, u32[]{:S(2)}, u32[]{:S(2)}) collective-permute-start(f32[2,16,128]{2,1,0:T(8,128)S(1)} %facts.1.refs_0_), channel_id=1, source_target_pairs={{0,256},{1,257},{2,258},{3,259},{4,260},{5,261},{6,262},{7,263},{8... | collective-permute-start | bytes 49160 | tf_op jit(solution)/shard_map/ppermute | solution.py:42
  48.9 4.8 %collective-permute-start.3 = (f32[2,16,128]{2,1,0:T(8,128)S(1)}, f32[2,16,128]{2,1,0:T(8,128)S(1)}, u32[]{:S(2)}, u32[]{:S(2)}) collective-permute-start(f32[2,16,128]{2,1,0:T(8,128)S(1)} %facts.1.refs_0_), channel_id=1, source_target_pairs={{0,384},{1,385},{2,386},{3,387},{4,388},{5,389},{6,390},{7,391},{8... | collective-permute-start | bytes 49160 | tf_op jit(solution)/shard_map/ppermute | solution.py:42
  54.5 20.1 %all-to-all-start.2 = ((bf16[64,16,128]{2,1,0:T(8,128)(2,1)}), bf16[64,16,128]{2,1,0:T(8,128)(2,1)S(1)}, u32[]{:S(2)}, u32[]{:S(2)}) async-start(bf16[64,16,128]{2,1,0:T(8,128)(2,1)} %get-tuple-element.11), calls=%async_computation.2 | async-start | bytes 524288 | tf_op jit(solution)/shard_map/all_to_all | solution.py:34

commit v4 on v2

--- a/solution.py
+++ b/solution.py
@@ -48,17 +48,32 @@
     cols = cot_ref.shape[2]
     tiles = cols // WIDTH
     groups = resid_ref.shape[1] // WIDTH
-
-    copies = [
-        pltpu.make_async_copy(rank_hbm, rank_ref, sems.at[0]),
-        pltpu.make_async_copy(count_hbm, count_ref, sems.at[1]),
-        pltpu.make_async_copy(resid_hbm, resid_ref, sems.at[2]),
-    ]
-    for s in range(steps):
-        copies.append(pltpu.make_async_copy(acts_hbm.at[0, s], acts_ref.at[s], sems.at[3 + 2 * s]))
-        copies.append(pltpu.make_async_copy(cot_hbm.at[0, s], cot_ref.at[s], sems.at[4 + 2 * s]))
-    for i in [0, 1, 3, 4, 2] + list(range(5, 3 + 2 * steps)):
-        copies[i].start()
+    parts = 2
+    part = rows // parts
+
+    def copy(source, target, at):
+        return pltpu.make_async_copy(source, target, sems.at[at])
+
+    rank_copy = copy(rank_hbm, rank_ref, 0)
+    count_copy = copy(count_hbm, count_ref, 1)
+    resid_copy = copy(resid_hbm, resid_ref, 2)
+    cot_copy, acts_copy = [], []
+    for s in range(steps):
+        base = 3 + s * (1 + parts)
+        cot_copy.append(copy(cot_hbm.at[0, s], cot_ref.at[s], base))
+        acts_copy.append([
+            copy(acts_hbm.at[0, s, :, m * part:(m + 1) * part],
+                 acts_ref.at[s, :, m * part:(m + 1) * part], base + 1 + m)
+            for m in range(parts)
+        ])
+    rank_copy.start()
+    count_copy.start()
+    for s in range(steps):
+        cot_copy[s].start()
+        for m in range(parts):
+            acts_copy[s][m].start()
+        if s == 0:
+            resid_copy.start()
 
     per = WIDTH // groups
     row_id = lax.broadcasted_iota(jnp.int32, (groups, WIDTH), 0)
@@ -67,8 +82,8 @@
     block_id = lax.broadcasted_iota(jnp.int32, (WIDTH, WIDTH), 1) // REGION
     place = jnp.where(owner_id == block_id, 1.0, 0.0).astype(BF)
     eye = jnp.where(row_id == lane_id, 1.0, 0.0).astype(BF)
-    copies[0].wait()
-    copies[1].wait()
+    rank_copy.wait()
+    count_copy.wait()
     for s in range(steps):
         for r in range(groups):
             ranks_ref[s, r:r + 1, :] = rank_ref[0, s:s + 1, r * WIDTH:(r + 1) * WIDTH]
@@ -81,43 +96,51 @@
 
     half = 2 * WIDTH
     for s in range(steps):
-        copies[3 + 2 * s].wait()
-        copies[4 + 2 * s].wait()
-        left = acts_ref[s]
-        for h in range(cols // half):
-            grad = lax.dot_general(left, cot_ref[s, :, h * half:(h + 1) * half],
-                                   (((0,), (0,)), ((), ())), preferred_element_type=F32)
-            grad = grad * scale
-            for q in range(2):
-                acc_ref[pl.ds(2 * h + q, rows, stride=tiles), :] = grad[:, q * WIDTH:(q + 1) * WIDTH]
-        if s == 0:
-            copies[2].wait()
-        columns = chosen_ref[s]
-        for me in range(NC):
-            @pl.when(core == me)
-            def _(me=me, s=s, columns=columns):
-                for r in range(groups):
-                    span = slice(r * WIDTH, (r + 1) * WIDTH)
-                    total = resid_ref[0, span, :] + acc_ref[span, :]
-                    mask = jnp.broadcast_to(columns[:, r:r + 1], (WIDTH, WIDTH)) > 0.5
-                    resid_ref[0, span, :] = jnp.where(mask, 0.0, total)
-                    sent = jnp.where(mask, total, 0.0).astype(BF)
-                    for i in range(WIDTH // REGION):
-                        owner = r * (WIDTH // REGION) + i
-                        to = keep_ref if owner % NC == me else give_ref
-                        to[owner // NC, s] = sent[i * REGION:(i + 1) * REGION, :]
-
-
-def owner_kernel(arrived_ref, oresid_ref, count_ref, rank_ref, out_ref, oresid_out):
-    steps = rank_ref.shape[1]
+        cot_copy[s].wait()
+        for m in range(parts):
+            acts_copy[s][m].wait()
+            left = acts_ref[s, :, m * part:(m + 1) * part]
+            for h in range(cols // half):
+                grad = lax.dot_general(left, cot_ref[s, :, h * half:(h + 1) * half],
+                                       (((0,), (0,)), ((), ())), preferred_element_type=F32)
+                grad = grad * scale
+                for q in range(2):
+                    to = pl.ds(m * part * tiles + 2 * h + q, part, stride=tiles)
+                    acc_ref[to, :] = grad[:, q * WIDTH:(q + 1) * WIDTH]
+            if s == 0 and m == 0:
+                resid_copy.wait()
+            columns = chosen_ref[s]
+            for me in range(NC):
+                @pl.when(core == me)
+                def _(me=me, s=s, m=m, columns=columns):
+                    for r in range(m * groups // parts, (m + 1) * groups // parts):
+                        span = slice(r * WIDTH, (r + 1) * WIDTH)
+                        total = resid_ref[0, span, :] + acc_ref[span, :]
+                        mask = jnp.broadcast_to(columns[:, r:r + 1], (WIDTH, WIDTH)) > 0.5
+                        resid_ref[0, span, :] = jnp.where(mask, 0.0, total)
+                        sent = jnp.where(mask, total, 0.0).astype(BF)
+                        for i in range(WIDTH // REGION):
+                            owner = r * (WIDTH // REGION) + i
+                            to = keep_ref if owner % NC == me else give_ref
+                            to[owner // NC, s] = sent[i * REGION:(i + 1) * REGION, :]
+
+
+def store_kernel(value_ref, out_hbm, sem):
+    copy = pltpu.make_async_copy(value_ref, out_hbm, sem)
+    copy.start()
+    copy.wait()
+
+
+def owner_kernel(arrived_ref, oresid_ref, count_ref, rank_ref, out_ref, last_ref, kept_ref):
     eye = (lax.broadcasted_iota(jnp.int32, (REGION, REGION), 0)
            == lax.broadcasted_iota(jnp.int32, (REGION, REGION), 1))
     oresid = oresid_ref[0]
-    for s in range(steps):
+    for s in range(rank_ref.shape[1]):
         total = arrived_ref[0, s].astype(F32)
         for k in range(1, arrived_ref.shape[0]):
             total = total + arrived_ref[k, s].astype(F32)
-        row = jnp.where(rank_ref[0, s:s + 1, :] < count_ref[0, s], 1.0, 0.0)
+        count = jnp.broadcast_to(count_ref[0:1, s:s + 1], (1, REGION))
+        row = jnp.where(rank_ref[0, s:s + 1, :] < count, 1.0, 0.0)
         square = jnp.where(eye, jnp.broadcast_to(row, (REGION, REGION)), 0.0)
         passed = jnp.broadcast_to(jnp.sum(square, axis=1, keepdims=True), (REGION, WIDTH)) > 0.5
         total = total + oresid
@@ -125,7 +148,8 @@
         oresid = jnp.where(passed, 0.0, total)
         for k in range(out_ref.shape[0]):
             out_ref[k, s] = going
-    oresid_out[0] = oresid
+    last_ref[...] = total
+    kept_ref[...] = jnp.where(passed, 0.0, 1.0)
 
 
 def update_kernel(arrived_ref, out_ref):
@@ -140,15 +164,26 @@
         out_ref[k] = applied
 
 
-def assemble_kernel(halves_ref, out_ref, flat_ref):
-    rows, cols = out_ref.shape
+def assemble_kernel(halves_ref, last_ref, kept_ref, out_hbm, oresid_ref, flat_ref, rows_ref, sems):
+    oresid_ref[0] = jnp.where(kept_ref[...] > 0.5, last_ref[...], 0.0)
+    rows, cols = rows_ref.shape
     tiles = cols // WIDTH
-    for i in range(CHIPS):
-        for c in range(NC):
-            at = (i * NC + c) * REGION
-            flat_ref[at:at + REGION, :] = halves_ref[c, i].astype(F32)
-    for t in range(tiles):
-        out_ref[:, t * WIDTH:(t + 1) * WIDTH] = flat_ref[pl.ds(t, rows, stride=tiles), :].astype(BF)
+    parts = sems.shape[0]
+    part = rows // parts
+    sends = []
+    for p in range(parts):
+        for i in range(p * CHIPS // parts, (p + 1) * CHIPS // parts):
+            for c in range(NC):
+                at = (i * NC + c) * REGION
+                flat_ref[at:at + REGION, :] = halves_ref[c, i].astype(F32)
+        span = slice(p * part, (p + 1) * part)
+        for t in range(tiles):
+            value = flat_ref[pl.ds(p * part * tiles + t, part, stride=tiles), :]
+            rows_ref[span, t * WIDTH:(t + 1) * WIDTH] = value.astype(BF)
+        sends.append(pltpu.make_async_copy(rows_ref.at[span], out_hbm.at[span], sems.at[p]))
+        sends[-1].start()
+    for send in sends:
+        send.wait()
 
 
 def vmem():
@@ -175,7 +210,7 @@
         return local_kernel(scale, *args)
 
     half = (CHIPS, steps, REGION, WIDTH)
-    new_residual, keep, give = pl.pallas_call(
+    new_resid, keep, give = pl.pallas_call(
         local,
         in_specs=[smem(), hbm(), hbm(), hbm(), hbm(), hbm()],
         out_specs=[vmem(), vmem(), vmem()],
@@ -192,7 +227,7 @@
             pltpu.VMEM(in_rank.shape, jnp.int32),
             pltpu.VMEM((steps, blocks // WIDTH, WIDTH), jnp.int32),
             pltpu.VMEM((steps, WIDTH, WIDTH), F32),
-            pltpu.SemaphoreType.DMA((3 + 2 * steps,)),
+            pltpu.SemaphoreType.DMA((3 + 3 * steps,)),
         ],
         compiler_params=params,
         name="local",
@@ -200,17 +235,25 @@
             for v in (acts, cotangent, residual, in_count, in_rank)])
 
     given = other_core(give)
+    new_residual = pl.pallas_call(
+        store_kernel,
+        in_specs=[vmem()],
+        out_specs=hbm(),
+        out_shape=jax.ShapeDtypeStruct(residual.shape, F32),
+        scratch_shapes=[pltpu.SemaphoreType.DMA],
+        compiler_params=params,
+        name="store",
+    )(new_resid)
     pair = (keep.astype(F32) + given.astype(F32)).astype(BF)
+    pair, new_residual = lax.optimization_barrier((pair, new_residual))
     arrived = exchange(pair, (1, 2))
 
-    outgoing, new_owner = pl.pallas_call(
+    tile = jax.ShapeDtypeStruct((REGION, WIDTH), F32)
+    outgoing, last, kept = pl.pallas_call(
         owner_kernel,
-        in_specs=[vmem(), vmem(), smem(), vmem()],
-        out_specs=[vmem(), vmem()],
-        out_shape=[
-            jax.ShapeDtypeStruct((NX, steps, REGION, WIDTH), BF),
-            jax.ShapeDtypeStruct(owner_residual.shape, F32),
-        ],
+        in_specs=[vmem(), vmem(), vmem(), vmem()],
+        out_specs=[vmem(), vmem(), vmem()],
+        out_shape=[jax.ShapeDtypeStruct((NX, steps, REGION, WIDTH), BF), tile, tile],
         compiler_params=params,
         name="owner",
     )(arrived, owner_residual, out_count, out_rank)
@@ -224,15 +267,22 @@
         name="update",
     )(exchange(outgoing, (0,)))
     halves = of_both_cores(exchange(copies, (1, 2)))
-    applied = pl.pallas_call(
+    applied, new_owner = pl.pallas_call(
         assemble_kernel,
-        in_specs=[vmem()],
-        out_specs=vmem(),
-        out_shape=jax.ShapeDtypeStruct((rows, cols), BF),
-        scratch_shapes=[pltpu.VMEM((blocks, WIDTH), F32)],
+        in_specs=[vmem(), vmem(), vmem()],
+        out_specs=[hbm(), vmem()],
+        out_shape=[
+            jax.ShapeDtypeStruct((rows, cols), BF),
+            jax.ShapeDtypeStruct(owner_residual.shape, F32),
+        ],
+        scratch_shapes=[
+            pltpu.VMEM((blocks, WIDTH), F32),
+            pltpu.VMEM((rows, cols), BF),
+            pltpu.SemaphoreType.DMA((4,)),
+        ],
         compiler_params=params,
         name="assemble",
-    )(halves)
+    )(halves, last, kept)
     return applied, new_residual, new_owner
 
 

time: 79 us -> 78 us (0.987)
  waiting for transfers between devices: 1.51 us -> 0.53 us
    ppermute x1, waiting for transfers between devices: 1.51 us -> 0.53 us  [other_core(): return lax.ppermute(value, 'd', pairs)]
    pallas_call x2 -> x3, Pallas kernels: 2.18 us -> 2.59 us  [the longest x1 1.46 us: per_device(): pl.pallas_call(assemble_kernel, in_specs=[vmem(), vmem(), vmem()], out_sp...]
  transfers between devices with their start and end apart: 1 -> 1, of which waited for: 1 -> 1; matrix products, arithmetic and copies ran while one was open for 0% -> 0% of each run, Pallas kernels for 0% -> 1%
where the time goes in v4:
time: 78 us; the launch traced here: 77.6 us
  blocking collectives  61.4 us (79%)
  starting transfers between devices  8.75 us (11%)
  Pallas kernels  6.14 us (8%)
    all_to_all x3, blocking collectives, exchange(): lax.all_to_all(value, 'd', split_axis=0, concat_axis=0, tiled=True, axis_...  55.6 us
    ppermute x1, starting transfers between devices, other_core(): return lax.ppermute(value, 'd', pairs)  8.75 us
    all_gather x1, blocking collectives, of_both_cores(): lax.all_gather(value, 'd', axis=0, axis_index_groups=groups_along((3,)))  5.78 us
    pallas_call x1, Pallas kernels, per_device(): pl.pallas_call(local, in_specs=[smem(), hbm(), hbm(), hbm(), hbm(), hbm()...  3.51 us
  transfers between devices with their start and end apart: 1, of which 1 were waited for; matrix products, arithmetic and copies ran while one was open for 0% of the time, Pallas kernels for 1%

profile of v4, /device:TPU:1, one launch (start us, length us, event | category | flops | bytes accessed | tf_op | source)
XLA Modules:
  0.0 77.6 jit_solution(13153394038670924224)
XLA Ops:
  0.6 3.5 %local.1 = (f32[1,2048,128]{2,1,0:T(8,128)S(1)}, bf16[64,2,16,128]{3,2,1,0:T(8,128)(2,1)S(1)}, bf16[64,2,16,128]{3,2,1,0:T(8,128)(2,1)S(1)}) custom-call(s32[1]{0:T(128)} %bitcast.args_0_, bf16[1,2,512,512]{3,2,1,0:T(8,128)(2,1)} %args_1_.4, bf16[1,2,512,512]{3,2,1,0:T(8,128)(2,1)} %args_2_.4, f32[1,2048,128]{2,1,0:T(8,128)} %args_3_.4, ...), custom_call_target="tpu_custom_call" | custom-call | tf_op jit(solution)/shard_map/local/pallas_call | solution.py:213
  4.2 8.8 %collective-permute-start = (bf16[64,2,16,128]{3,2,1,0:T(8,128)(2,1)S(1)}, bf16[64,2,16,128]{3,2,1,0:T(8,128)(2,1)S(1)}, u32[]{:S(2)}, u32[]{:S(2)}) collective-permute-start(bf16[64,2,16,128]{3,2,1,0:T(8,128)(2,1)S(1)} %get-tuple-element.14), channel_id=1, source_target_pairs={{0,1},{1,0},{2,3},{3,2},{4,5},{5,4},{6,7},{7,6},{8,9},{9,8},{10,11... | collective-permute-start | bytes 1572872 | tf_op jit(solution)/shard_map/ppermute | solution.py:36
  12.9 1.0 %store.1 = f32[1,2048,128]{2,1,0:T(8,128)} custom-call(f32[1,2048,128]{2,1,0:T(8,128)S(1)} %get-tuple-element.15.value_ref), custom_call_target="tpu_custom_call" | custom-call | tf_op jit(solution)/shard_map/store/pallas_call | solution.py:238
  13.9 0.5 collective-permute-done
  14.4 0.1 add_convert_fusion
  14.6 0.0 copy-start
  14.6 0.0 copy-start.1
  14.6 0.0 copy-start.2
  14.6 28.5 %all_to_all.15.arrived_ref = bf16[64,2,16,128]{3,2,1,0:T(8,128)(2,1)S(1)} all-to-all(bf16[64,2,16,128]{3,2,1,0:T(8,128)(2,1)S(1)} %add_convert_fusion), channel_id=1, replica_groups={{0,2,4,6,8,10,12,14,16,18,20,22,24,26,28,30,32,34,36,38,40,42,44,46,48,..., dimensions={0} | all-to-all | bytes 1048576 | tf_op jit(solution)/shard_map/all_to_all | solution.py:29
  43.1 0.0 copy-done
  43.1 0.0 copy-done.1
  43.1 0.0 copy-done.2
  43.1 0.2 owner.1
  43.2 8.1 %all_to_all.16.arrived_ref = bf16[4,2,16,128]{3,2,1,0:T(8,128)(2,1)S(1)} all-to-all(bf16[4,2,16,128]{3,2,1,0:T(8,128)(2,1)S(1)} %get-tuple-element.17), channel_id=1, replica_groups={{0,128,256,384},{1,129,257,385},{2,130,258,386},{3,131,259,387},{4,132,..., dimensions={0} | all-to-all | bytes 65536 | tf_op jit(solution)/shard_map/all_to_all | solution.py:29
  51.4 19.0 %all_to_all.17 = bf16[64,16,128]{2,1,0:T(8,128)(2,1)S(1)} all-to-all(bf16[64,16,128]{2,1,0:T(8,128)(2,1)S(1)} %update.1), channel_id=1, replica_groups={{0,2,4,6,8,10,12,14,16,18,20,22,24,26,28,30,32,34,36,38,40,42,44,46,48,..., dimensions={0} | all-to-all | bytes 524288 | tf_op jit(solution)/shard_map/all_to_all | solution.py:29
  70.4 5.8 %all-gather = bf16[128,16,128]{2,1,0:T(8,128)(2,1)S(1)} all-gather(bf16[64,16,128]{2,1,0:T(8,128)(2,1)S(1)} %all_to_all.17), channel_id=2, replica_groups={{0,1},{2,3},{4,5},{6,7},{8,9},{10,11},{12,13},{14,15},{16,17},{18,19},{..., dimensions={0}, use_global_device_ids=true | all-gather | bytes 786432 | tf_op jit(solution)/shard_map/all_gather | solution.py:40
  76.2 1.5 %assemble.1 = (bf16[512,512]{1,0:T(8,128)(2,1)}, f32[1,16,128]{2,1,0:T(8,128)}) custom-call(bf16[2,64,16,128]{3,2,1,0:T(8,128)(2,1)S(1)} %bitcast.2, f32[16,128]{1,0:T(8,128)S(1)} %get-tuple-element.18.last_ref, f32[16,128]{1,0:T(8,128)S(1)} %get-tuple-element.19.kept_ref), custom_call_target="tpu_custom_call" | custom-call | tf_op jit(solution)/shard_map/assemble/pallas_call | solution.py:270
  (1 shorter events, 0.0 us)
Async XLA Ops:
  4.2 10.3 %collective-permute-start = (bf16[64,2,16,128]{3,2,1,0:T(8,128)(2,1)S(1)}, bf16[64,2,16,128]{3,2,1,0:T(8,128)(2,1)S(1)}, u32[]{:S(2)}, u32[]{:S(2)}) collective-permute-start(bf16[64,2,16,128]{3,2,1,0:T(8,128)(2,1)S(1)} %get-tuple-element.14), channel_id=1, source_target_pairs={{0,1},{1,0},{2,3},{3,2},{4,5},{5,4},{6,7},{7,6},{8,9},{9,8},{10,11... | collective-permute-start | bytes 1572872 | tf_op jit(solution)/shard_map/ppermute | solution.py:36
  14.6 28.5 %copy-start = (f32[1,16,128]{2,1,0:T(8,128)S(1)}, f32[1,16,128]{2,1,0:T(8,128)}, u32[]{:S(2)}) copy-start(f32[1,16,128]{2,1,0:T(8,128)} %oresid_ref.1) | copy-start | bytes 24580
  14.6 28.5 %copy-start.1 = (s32[1,2,16]{2,1,0:T(2,128)S(1)}, s32[1,2,16]{2,1,0:T(2,128)}, u32[]{:S(2)}) copy-start(s32[1,2,16]{2,1,0:T(2,128)} %rank_ref.1) | copy-start | bytes 388
  14.6 28.5 %copy-start.2 = (s32[1,2]{1,0:T(1,128)S(1)}, s32[1,2]{1,0:T(1,128)}, u32[]{:S(2)}) copy-start(s32[1,2]{1,0:T(1,128)} %count_ref.1) | copy-start | bytes 28

commit v5 on v4

--- a/solution.py
+++ b/solution.py
@@ -16,6 +16,7 @@
 WIDTH = 128
 BF = jnp.bfloat16
 F32 = jnp.float32
+PART = 512
 VMEM_LIMIT = 48 * 1024 * 1024
 
 
@@ -25,10 +26,19 @@
     return np.moveaxis(ids, axes, range(4 - len(axes), 4)).reshape(-1, size).tolist()
 
 
-def exchange(value, axes):
+def lines(axes0, axes1):
+    return ([g for g in groups_along(axes0) if g[0] % NC == 0]
+            + [g for g in groups_along(axes1) if g[0] % NC == 1])
+
+
+def exchange(value, groups):
     return lax.all_to_all(
-        value, "d", split_axis=0, concat_axis=0, tiled=True, axis_index_groups=groups_along(axes)
+        value, "d", split_axis=0, concat_axis=0, tiled=True, axis_index_groups=groups
     )
+
+
+def place_of(core, z, y):
+    return z * NY + y if core == 0 else y * NZ + z
 
 
 def other_core(value):
@@ -48,32 +58,27 @@
     cols = cot_ref.shape[2]
     tiles = cols // WIDTH
     groups = resid_ref.shape[1] // WIDTH
-    parts = 2
-    part = rows // parts
+    parts = resid_ref.shape[1] // PART
 
     def copy(source, target, at):
         return pltpu.make_async_copy(source, target, sems.at[at])
 
     rank_copy = copy(rank_hbm, rank_ref, 0)
     count_copy = copy(count_hbm, count_ref, 1)
-    resid_copy = copy(resid_hbm, resid_ref, 2)
-    cot_copy, acts_copy = [], []
-    for s in range(steps):
-        base = 3 + s * (1 + parts)
-        cot_copy.append(copy(cot_hbm.at[0, s], cot_ref.at[s], base))
-        acts_copy.append([
-            copy(acts_hbm.at[0, s, :, m * part:(m + 1) * part],
-                 acts_ref.at[s, :, m * part:(m + 1) * part], base + 1 + m)
-            for m in range(parts)
-        ])
+    acts_copy = [copy(acts_hbm.at[0, s], acts_ref.at[s], 2 + 2 * s) for s in range(steps)]
+    cot_copy = [copy(cot_hbm.at[0, s], cot_ref.at[s], 3 + 2 * s) for s in range(steps)]
+    resid_copy = [
+        copy(resid_hbm.at[:, p * PART:(p + 1) * PART], resid_ref.at[:, p * PART:(p + 1) * PART],
+             2 + 2 * steps + p)
+        for p in range(parts)
+    ]
     rank_copy.start()
     count_copy.start()
     for s in range(steps):
+        acts_copy[s].start()
         cot_copy[s].start()
-        for m in range(parts):
-            acts_copy[s][m].start()
-        if s == 0:
-            resid_copy.start()
+    for p in range(parts):
+        resid_copy[p].start()
 
     per = WIDTH // groups
     row_id = lax.broadcasted_iota(jnp.int32, (groups, WIDTH), 0)
@@ -96,33 +101,37 @@
 
     half = 2 * WIDTH
     for s in range(steps):
+        acts_copy[s].wait()
         cot_copy[s].wait()
-        for m in range(parts):
-            acts_copy[s][m].wait()
-            left = acts_ref[s, :, m * part:(m + 1) * part]
-            for h in range(cols // half):
-                grad = lax.dot_general(left, cot_ref[s, :, h * half:(h + 1) * half],
-                                       (((0,), (0,)), ((), ())), preferred_element_type=F32)
-                grad = grad * scale
-                for q in range(2):
-                    to = pl.ds(m * part * tiles + 2 * h + q, part, stride=tiles)
-                    acc_ref[to, :] = grad[:, q * WIDTH:(q + 1) * WIDTH]
-            if s == 0 and m == 0:
-                resid_copy.wait()
-            columns = chosen_ref[s]
-            for me in range(NC):
-                @pl.when(core == me)
-                def _(me=me, s=s, m=m, columns=columns):
-                    for r in range(m * groups // parts, (m + 1) * groups // parts):
-                        span = slice(r * WIDTH, (r + 1) * WIDTH)
-                        total = resid_ref[0, span, :] + acc_ref[span, :]
-                        mask = jnp.broadcast_to(columns[:, r:r + 1], (WIDTH, WIDTH)) > 0.5
-                        resid_ref[0, span, :] = jnp.where(mask, 0.0, total)
+        left = acts_ref[s]
+        for h in range(cols // half):
+            grad = lax.dot_general(left, cot_ref[s, :, h * half:(h + 1) * half],
+                                   (((0,), (0,)), ((), ())), preferred_element_type=F32)
+            grad = grad * scale
+            for q in range(2):
+                to = pl.ds(2 * h + q, rows, stride=tiles)
+                acc_ref[s, to, :] = grad[:, q * WIDTH:(q + 1) * WIDTH]
+
+    columns = [chosen_ref[s] for s in range(steps)]
+    for p in range(parts):
+        resid_copy[p].wait()
+        for me in range(NC):
+            @pl.when(core == me)
+            def _(me=me, p=p):
+                for r in range(p * groups // parts, (p + 1) * groups // parts):
+                    span = slice(r * WIDTH, (r + 1) * WIDTH)
+                    total = resid_ref[0, span, :]
+                    for s in range(steps):
+                        total = total + acc_ref[s, span, :]
+                        mask = jnp.broadcast_to(columns[s][:, r:r + 1], (WIDTH, WIDTH)) > 0.5
                         sent = jnp.where(mask, total, 0.0).astype(BF)
+                        total = jnp.where(mask, 0.0, total)
                         for i in range(WIDTH // REGION):
                             owner = r * (WIDTH // REGION) + i
-                            to = keep_ref if owner % NC == me else give_ref
-                            to[owner // NC, s] = sent[i * REGION:(i + 1) * REGION, :]
+                            z, y, c = owner // (NY * NC), (owner // NC) % NY, owner % NC
+                            to = keep_ref if c == me else give_ref
+                            to[place_of(c, z, y), s] = sent[i * REGION:(i + 1) * REGION, :]
+                    resid_ref[0, span, :] = total
 
 
 def store_kernel(value_ref, out_hbm, sem):
@@ -164,26 +173,16 @@
         out_ref[k] = applied
 
 
-def assemble_kernel(halves_ref, last_ref, kept_ref, out_hbm, oresid_ref, flat_ref, rows_ref, sems):
+def assemble_kernel(halves_ref, last_ref, kept_ref, out_ref, oresid_ref, flat_ref):
     oresid_ref[0] = jnp.where(kept_ref[...] > 0.5, last_ref[...], 0.0)
-    rows, cols = rows_ref.shape
+    rows, cols = out_ref.shape
     tiles = cols // WIDTH
-    parts = sems.shape[0]
-    part = rows // parts
-    sends = []
-    for p in range(parts):
-        for i in range(p * CHIPS // parts, (p + 1) * CHIPS // parts):
-            for c in range(NC):
-                at = (i * NC + c) * REGION
-                flat_ref[at:at + REGION, :] = halves_ref[c, i].astype(F32)
-        span = slice(p * part, (p + 1) * part)
-        for t in range(tiles):
-            value = flat_ref[pl.ds(p * part * tiles + t, part, stride=tiles), :]
-            rows_ref[span, t * WIDTH:(t + 1) * WIDTH] = value.astype(BF)
-        sends.append(pltpu.make_async_copy(rows_ref.at[span], out_hbm.at[span], sems.at[p]))
-        sends[-1].start()
-    for send in sends:
-        send.wait()
+    for i in range(CHIPS):
+        for c in range(NC):
+            at = (i * NC + c) * REGION
+            flat_ref[at:at + REGION, :] = halves_ref[c, i].astype(F32)
+    for t in range(tiles):
+        out_ref[:, t * WIDTH:(t + 1) * WIDTH] = flat_ref[pl.ds(t, rows, stride=tiles), :].astype(BF)
 
 
 def vmem():
@@ -222,12 +221,12 @@
         scratch_shapes=[
             pltpu.VMEM((steps, tokens, rows), BF),
             pltpu.VMEM((steps, tokens, cols), BF),
-            pltpu.VMEM((blocks, WIDTH), F32),
+            pltpu.VMEM((steps, blocks, WIDTH), F32),
             pltpu.VMEM(in_count.shape, jnp.int32),
             pltpu.VMEM(in_rank.shape, jnp.int32),
             pltpu.VMEM((steps, blocks // WIDTH, WIDTH), jnp.int32),
             pltpu.VMEM((steps, WIDTH, WIDTH), F32),
-            pltpu.SemaphoreType.DMA((3 + 3 * steps,)),
+            pltpu.SemaphoreType.DMA((2 + 2 * steps + blocks // PART,)),
         ],
         compiler_params=params,
         name="local",
@@ -246,7 +245,9 @@
     )(new_resid)
     pair = (keep.astype(F32) + given.astype(F32)).astype(BF)
     pair, new_residual = lax.optimization_barrier((pair, new_residual))
-    arrived = exchange(pair, (1, 2))
+    first = exchange(pair.reshape(NZ, NY, steps, REGION, WIDTH), lines((1,), (2,)))
+    line = jnp.sum(first.astype(F32), axis=0).astype(BF)
+    arrived = exchange(line, lines((2,), (1,)))
 
     tile = jax.ShapeDtypeStruct((REGION, WIDTH), F32)
     outgoing, last, kept = pl.pallas_call(
@@ -265,20 +266,18 @@
         out_shape=jax.ShapeDtypeStruct((CHIPS, REGION, WIDTH), BF),
         compiler_params=params,
         name="update",
-    )(exchange(outgoing, (0,)))
-    halves = of_both_cores(exchange(copies, (1, 2)))
+    )(exchange(outgoing, groups_along((0,))))
+    halves = of_both_cores(exchange(copies, groups_along((1, 2))))
     applied, new_owner = pl.pallas_call(
         assemble_kernel,
         in_specs=[vmem(), vmem(), vmem()],
-        out_specs=[hbm(), vmem()],
+        out_specs=[vmem(), vmem()],
         out_shape=[
             jax.ShapeDtypeStruct((rows, cols), BF),
             jax.ShapeDtypeStruct(owner_residual.shape, F32),
         ],
         scratch_shapes=[
             pltpu.VMEM((blocks, WIDTH), F32),
-            pltpu.VMEM((rows, cols), BF),
-            pltpu.SemaphoreType.DMA((4,)),
         ],
         compiler_params=params,
         name="assemble",

time: 78 us -> 78.4 us (level)
  blocking collectives: 61.4 us -> 62.5 us
  Pallas kernels: 6.14 us -> 5.24 us
    all_gather x1, blocking collectives: 5.78 us -> 7.56 us  [of_both_cores(): lax.all_gather(value, 'd', axis=0, axis_index_groups=groups_along((3,)))]
    all_to_all x3 -> x4, blocking collectives: 55.6 us -> 55 us  [exchange(): lax.all_to_all(value, 'd', split_axis=0, concat_axis=0, tiled=True, axis_...]
where the time goes in v5:
time: 78.4 us; the launch traced here: 78 us
  blocking collectives  62.5 us (80%)
  starting transfers between devices  8.79 us (11%)
  Pallas kernels  5.24 us (7%)
    all_to_all x4, blocking collectives, exchange(): lax.all_to_all(value, 'd', split_axis=0, concat_axis=0, tiled=True, axis_...  55 us
    ppermute x1, starting transfers between devices, other_core(): return lax.ppermute(value, 'd', pairs)  8.79 us
    all_gather x1, blocking collectives, of_both_cores(): lax.all_gather(value, 'd', axis=0, axis_index_groups=groups_along((3,)))  7.56 us
    pallas_call x1, Pallas kernels, per_device(): pl.pallas_call(local, in_specs=[smem(), hbm(), hbm(), hbm(), hbm(), hbm()...  3.11 us
  transfers between devices with their start and end apart: 1, of which 1 were waited for; matrix products, arithmetic and copies ran while one was open for 0% of the time, Pallas kernels for 1%

profile of v5, /device:TPU:1, one launch (start us, length us, event | category | flops | bytes accessed | tf_op | source)
XLA Modules:
  0.0 78.0 jit_solution(16830540741656701867)
XLA Ops:
  0.6 3.1 %local.1 = (f32[1,2048,128]{2,1,0:T(8,128)S(1)}, bf16[64,2,16,128]{3,2,1,0:T(8,128)(2,1)S(1)}, bf16[64,2,16,128]{3,2,1,0:T(8,128)(2,1)S(1)}) custom-call(s32[1]{0:T(128)} %bitcast.args_0_, bf16[1,2,512,512]{3,2,1,0:T(8,128)(2,1)} %args_1_.4, bf16[1,2,512,512]{3,2,1,0:T(8,128)(2,1)} %args_2_.4, f32[1,2048,128]{2,1,0:T(8,128)} %args_3_.4, ...), custom_call_target="tpu_custom_call" | custom-call | tf_op jit(solution)/shard_map/local/pallas_call | solution.py:212
  3.8 8.8 %collective-permute-start = (bf16[64,2,16,128]{3,2,1,0:T(8,128)(2,1)S(1)}, bf16[64,2,16,128]{3,2,1,0:T(8,128)(2,1)S(1)}, u32[]{:S(2)}, u32[]{:S(2)}) collective-permute-start(bf16[64,2,16,128]{3,2,1,0:T(8,128)(2,1)S(1)} %get-tuple-element.14), channel_id=1, source_target_pairs={{0,1},{1,0},{2,3},{3,2},{4,5},{5,4},{6,7},{7,6},{8,9},{9,8},{10,11... | collective-permute-start | bytes 1572872 | tf_op jit(solution)/shard_map/ppermute | solution.py:46
  12.6 1.0 %store.1 = f32[1,2048,128]{2,1,0:T(8,128)} custom-call(f32[1,2048,128]{2,1,0:T(8,128)S(1)} %get-tuple-element.15.value_ref), custom_call_target="tpu_custom_call" | custom-call | tf_op jit(solution)/shard_map/store/pallas_call | solution.py:237
  13.5 0.5 collective-permute-done
  14.1 0.1 add_convert_fusion
  14.2 14.8 %all_to_all.20 = bf16[8,8,2,16,128]{4,3,2,1,0:T(8,128)(2,1)S(1)} all-to-all(bf16[8,8,2,16,128]{4,3,2,1,0:T(8,128)(2,1)S(1)} %bitcast.4), channel_id=1, replica_groups={{0,16,32,48,64,80,96,112},{2,18,34,50,66,82,98,114},{4,20,36,52,68,84,1..., dimensions={0} | all-to-all | bytes 1048576 | tf_op jit(solution)/shard_map/all_to_all | solution.py:35
  29.1 0.1 reduce_sum.12
  29.1 0.0 copy-start
  29.2 0.0 copy-start.1
  29.2 0.0 copy-start.2
  29.2 15.7 %all_to_all.21.arrived_ref = bf16[8,2,16,128]{3,2,1,0:T(8,128)(2,1)S(1)} all-to-all(bf16[8,2,16,128]{3,2,1,0:T(8,128)(2,1)S(1)} %reduce_sum.12), channel_id=1, replica_groups={{0,2,4,6,8,10,12,14},{16,18,20,22,24,26,28,30},{32,34,36,38,40,42,44,46..., dimensions={0} | all-to-all | bytes 131072 | tf_op jit(solution)/shard_map/all_to_all | solution.py:35
  44.9 0.0 copy-done
  44.9 0.0 copy-done.1
  44.9 0.0 copy-done.2
  44.9 0.2 owner.1
  45.1 8.1 %all_to_all.22.arrived_ref = bf16[4,2,16,128]{3,2,1,0:T(8,128)(2,1)S(1)} all-to-all(bf16[4,2,16,128]{3,2,1,0:T(8,128)(2,1)S(1)} %get-tuple-element.17), channel_id=1, replica_groups={{0,128,256,384},{1,129,257,385},{2,130,258,386},{3,131,259,387},{4,132,..., dimensions={0} | all-to-all | bytes 65536 | tf_op jit(solution)/shard_map/all_to_all | solution.py:35
  53.2 16.3 %all_to_all.23 = bf16[64,16,128]{2,1,0:T(8,128)(2,1)S(1)} all-to-all(bf16[64,16,128]{2,1,0:T(8,128)(2,1)S(1)} %update.1), channel_id=1, replica_groups={{0,2,4,6,8,10,12,14,16,18,20,22,24,26,28,30,32,34,36,38,40,42,44,46,48,..., dimensions={0} | all-to-all | bytes 524288 | tf_op jit(solution)/shard_map/all_to_all | solution.py:35
  69.5 7.6 %all-gather = bf16[128,16,128]{2,1,0:T(8,128)(2,1)S(1)} all-gather(bf16[64,16,128]{2,1,0:T(8,128)(2,1)S(1)} %all_to_all.23), channel_id=2, replica_groups={{0,1},{2,3},{4,5},{6,7},{8,9},{10,11},{12,13},{14,15},{16,17},{18,19},{..., dimensions={0}, use_global_device_ids=true | all-gather | bytes 786432 | tf_op jit(solution)/shard_map/all_gather | solution.py:50
  77.1 1.0 %assemble.1 = (bf16[512,512]{1,0:T(8,128)(2,1)}, f32[1,16,128]{2,1,0:T(8,128)}) custom-call(bf16[2,64,16,128]{3,2,1,0:T(8,128)(2,1)S(1)} %bitcast.3, f32[16,128]{1,0:T(8,128)S(1)} %get-tuple-element.18.last_ref, f32[16,128]{1,0:T(8,128)S(1)} %get-tuple-element.19.kept_ref), custom_call_target="tpu_custom_call" | custom-call | tf_op jit(solution)/shard_map/assemble/pallas_call | solution.py:271
  (1 shorter events, 0.0 us)
Async XLA Ops:
  3.8 10.3 %collective-permute-start = (bf16[64,2,16,128]{3,2,1,0:T(8,128)(2,1)S(1)}, bf16[64,2,16,128]{3,2,1,0:T(8,128)(2,1)S(1)}, u32[]{:S(2)}, u32[]{:S(2)}) collective-permute-start(bf16[64,2,16,128]{3,2,1,0:T(8,128)(2,1)S(1)} %get-tuple-element.14), channel_id=1, source_target_pairs={{0,1},{1,0},{2,3},{3,2},{4,5},{5,4},{6,7},{7,6},{8,9},{9,8},{10,11... | collective-permute-start | bytes 1572872 | tf_op jit(solution)/shard_map/ppermute | solution.py:46
  29.1 15.8 %copy-start = (f32[1,16,128]{2,1,0:T(8,128)S(1)}, f32[1,16,128]{2,1,0:T(8,128)}, u32[]{:S(2)}) copy-start(f32[1,16,128]{2,1,0:T(8,128)} %oresid_ref.1) | copy-start | bytes 24580
  29.2 15.8 %copy-start.1 = (s32[1,2,16]{2,1,0:T(2,128)S(1)}, s32[1,2,16]{2,1,0:T(2,128)}, u32[]{:S(2)}) copy-start(s32[1,2,16]{2,1,0:T(2,128)} %rank_ref.1) | copy-start | bytes 388
  29.2 15.8 %copy-start.2 = (s32[1,2]{1,0:T(1,128)S(1)}, s32[1,2]{1,0:T(1,128)}, u32[]{:S(2)}) copy-start(s32[1,2]{1,0:T(1,128)} %count_ref.1) | copy-start | bytes 28

commit v6 on v2

--- a/solution.py
+++ b/solution.py
@@ -108,16 +108,22 @@
                         to[owner // NC, s] = sent[i * REGION:(i + 1) * REGION, :]
 
 
-def owner_kernel(arrived_ref, oresid_ref, count_ref, rank_ref, out_ref, oresid_out):
-    steps = rank_ref.shape[1]
+def store_kernel(value_ref, out_hbm, sem):
+    copy = pltpu.make_async_copy(value_ref, out_hbm, sem)
+    copy.start()
+    copy.wait()
+
+
+def owner_kernel(arrived_ref, oresid_ref, count_ref, rank_ref, out_ref, last_ref, kept_ref):
     eye = (lax.broadcasted_iota(jnp.int32, (REGION, REGION), 0)
            == lax.broadcasted_iota(jnp.int32, (REGION, REGION), 1))
     oresid = oresid_ref[0]
-    for s in range(steps):
+    for s in range(rank_ref.shape[1]):
         total = arrived_ref[0, s].astype(F32)
         for k in range(1, arrived_ref.shape[0]):
             total = total + arrived_ref[k, s].astype(F32)
-        row = jnp.where(rank_ref[0, s:s + 1, :] < count_ref[0, s], 1.0, 0.0)
+        count = jnp.broadcast_to(count_ref[0:1, s:s + 1], (1, REGION))
+        row = jnp.where(rank_ref[0, s:s + 1, :] < count, 1.0, 0.0)
         square = jnp.where(eye, jnp.broadcast_to(row, (REGION, REGION)), 0.0)
         passed = jnp.broadcast_to(jnp.sum(square, axis=1, keepdims=True), (REGION, WIDTH)) > 0.5
         total = total + oresid
@@ -125,7 +131,8 @@
         oresid = jnp.where(passed, 0.0, total)
         for k in range(out_ref.shape[0]):
             out_ref[k, s] = going
-    oresid_out[0] = oresid
+    last_ref[...] = total
+    kept_ref[...] = jnp.where(passed, 0.0, 1.0)
 
 
 def update_kernel(arrived_ref, out_ref):
@@ -140,7 +147,8 @@
         out_ref[k] = applied
 
 
-def assemble_kernel(halves_ref, out_ref, flat_ref):
+def assemble_kernel(halves_ref, last_ref, kept_ref, out_ref, oresid_ref, flat_ref):
+    oresid_ref[0] = jnp.where(kept_ref[...] > 0.5, last_ref[...], 0.0)
     rows, cols = out_ref.shape
     tiles = cols // WIDTH
     for i in range(CHIPS):
@@ -175,7 +183,7 @@
         return local_kernel(scale, *args)
 
     half = (CHIPS, steps, REGION, WIDTH)
-    new_residual, keep, give = pl.pallas_call(
+    new_resid, keep, give = pl.pallas_call(
         local,
         in_specs=[smem(), hbm(), hbm(), hbm(), hbm(), hbm()],
         out_specs=[vmem(), vmem(), vmem()],
@@ -200,17 +208,25 @@
             for v in (acts, cotangent, residual, in_count, in_rank)])
 
     given = other_core(give)
+    new_residual = pl.pallas_call(
+        store_kernel,
+        in_specs=[vmem()],
+        out_specs=hbm(),
+        out_shape=jax.ShapeDtypeStruct(residual.shape, F32),
+        scratch_shapes=[pltpu.SemaphoreType.DMA],
+        compiler_params=params,
+        name="store",
+    )(new_resid)
     pair = (keep.astype(F32) + given.astype(F32)).astype(BF)
+    pair, new_residual = lax.optimization_barrier((pair, new_residual))
     arrived = exchange(pair, (1, 2))
 
-    outgoing, new_owner = pl.pallas_call(
+    tile = jax.ShapeDtypeStruct((REGION, WIDTH), F32)
+    outgoing, last, kept = pl.pallas_call(
         owner_kernel,
-        in_specs=[vmem(), vmem(), smem(), vmem()],
-        out_specs=[vmem(), vmem()],
-        out_shape=[
-            jax.ShapeDtypeStruct((NX, steps, REGION, WIDTH), BF),
-            jax.ShapeDtypeStruct(owner_residual.shape, F32),
-        ],
+        in_specs=[vmem(), vmem(), vmem(), vmem()],
+        out_specs=[vmem(), vmem(), vmem()],
+        out_shape=[jax.ShapeDtypeStruct((NX, steps, REGION, WIDTH), BF), tile, tile],
         compiler_params=params,
         name="owner",
     )(arrived, owner_residual, out_count, out_rank)
@@ -224,15 +240,20 @@
         name="update",
     )(exchange(outgoing, (0,)))
     halves = of_both_cores(exchange(copies, (1, 2)))
-    applied = pl.pallas_call(
+    applied, new_owner = pl.pallas_call(
         assemble_kernel,
-        in_specs=[vmem()],
-        out_specs=vmem(),
-        out_shape=jax.ShapeDtypeStruct((rows, cols), BF),
-        scratch_shapes=[pltpu.VMEM((blocks, WIDTH), F32)],
+        in_specs=[vmem(), vmem(), vmem()],
+        out_specs=[vmem(), vmem()],
+        out_shape=[
+            jax.ShapeDtypeStruct((rows, cols), BF),
+            jax.ShapeDtypeStruct(owner_residual.shape, F32),
+        ],
+        scratch_shapes=[
+            pltpu.VMEM((blocks, WIDTH), F32),
+        ],
         compiler_params=params,
         name="assemble",
-    )(halves)
+    )(halves, last, kept)
     return applied, new_residual, new_owner
 
 

time: 79 us -> 77 us (0.975)
  Pallas kernels: 6.14 us -> 5.1 us
  waiting for transfers between devices: 1.51 us -> 0.53 us
    ppermute x1, waiting for transfers between devices: 1.51 us -> 0.53 us  [other_core(): return lax.ppermute(value, 'd', pairs)]
    pallas_call x1, Pallas kernels: 3.92 us -> 2.97 us  [per_device(): pl.pallas_call(local, in_specs=[smem(), hbm(), hbm(), hbm(), hbm(), hbm()...]
    pallas_call x2 -> x3, Pallas kernels: 2.18 us -> 2.09 us  [the longest x1 0.98 us: per_device(): pl.pallas_call(store_kernel, in_specs=[vmem()], out_specs=hbm(), out_shap...]
  transfers between devices with their start and end apart: 1 -> 1, of which waited for: 1 -> 1; matrix products, arithmetic and copies ran while one was open for 0% -> 0% of each run, Pallas kernels for 0% -> 1%
where the time goes in v6:
time: 77 us; the launch traced here: 76.6 us
  blocking collectives  61.4 us (80%)
  starting transfers between devices  8.77 us (11%)
  Pallas kernels  5.1 us (7%)
    all_to_all x3, blocking collectives, exchange(): lax.all_to_all(value, 'd', split_axis=0, concat_axis=0, tiled=True, axis_...  55.6 us
    ppermute x1, starting transfers between devices, other_core(): return lax.ppermute(value, 'd', pairs)  8.77 us
    all_gather x1, blocking collectives, of_both_cores(): lax.all_gather(value, 'd', axis=0, axis_index_groups=groups_along((3,)))  5.78 us
    pallas_call x1, Pallas kernels, per_device(): pl.pallas_call(local, in_specs=[smem(), hbm(), hbm(), hbm(), hbm(), hbm()...  2.97 us
  transfers between devices with their start and end apart: 1, of which 1 were waited for; matrix products, arithmetic and copies ran while one was open for 0% of the time, Pallas kernels for 1%

profile of v6, /device:TPU:1, one launch (start us, length us, event | category | flops | bytes accessed | tf_op | source)
XLA Modules:
  0.0 76.6 jit_solution(8826674080670022293)
XLA Ops:
  0.6 3.0 %local.1 = (f32[1,2048,128]{2,1,0:T(8,128)S(1)}, bf16[64,2,16,128]{3,2,1,0:T(8,128)(2,1)S(1)}, bf16[64,2,16,128]{3,2,1,0:T(8,128)(2,1)S(1)}) custom-call(s32[1]{0:T(128)} %bitcast.args_0_, bf16[1,2,512,512]{3,2,1,0:T(8,128)(2,1)} %args_1_.4, bf16[1,2,512,512]{3,2,1,0:T(8,128)(2,1)} %args_2_.4, f32[1,2048,128]{2,1,0:T(8,128)} %args_3_.4, ...), custom_call_target="tpu_custom_call" | custom-call | tf_op jit(solution)/shard_map/local/pallas_call | solution.py:186
  3.6 8.8 %collective-permute-start = (bf16[64,2,16,128]{3,2,1,0:T(8,128)(2,1)S(1)}, bf16[64,2,16,128]{3,2,1,0:T(8,128)(2,1)S(1)}, u32[]{:S(2)}, u32[]{:S(2)}) collective-permute-start(bf16[64,2,16,128]{3,2,1,0:T(8,128)(2,1)S(1)} %get-tuple-element.14), channel_id=1, source_target_pairs={{0,1},{1,0},{2,3},{3,2},{4,5},{5,4},{6,7},{7,6},{8,9},{9,8},{10,11... | collective-permute-start | bytes 1572872 | tf_op jit(solution)/shard_map/ppermute | solution.py:36
  12.4 1.0 %store.1 = f32[1,2048,128]{2,1,0:T(8,128)} custom-call(f32[1,2048,128]{2,1,0:T(8,128)S(1)} %get-tuple-element.15.value_ref), custom_call_target="tpu_custom_call" | custom-call | tf_op jit(solution)/shard_map/store/pallas_call | solution.py:211
  13.4 0.5 collective-permute-done
  13.9 0.1 add_convert_fusion
  14.1 0.0 copy-start
  14.1 0.0 copy-start.1
  14.1 0.0 copy-start.2
  14.1 28.5 %all_to_all.15.arrived_ref = bf16[64,2,16,128]{3,2,1,0:T(8,128)(2,1)S(1)} all-to-all(bf16[64,2,16,128]{3,2,1,0:T(8,128)(2,1)S(1)} %add_convert_fusion), channel_id=1, replica_groups={{0,2,4,6,8,10,12,14,16,18,20,22,24,26,28,30,32,34,36,38,40,42,44,46,48,..., dimensions={0} | all-to-all | bytes 1048576 | tf_op jit(solution)/shard_map/all_to_all | solution.py:29
  42.6 0.0 copy-done
  42.6 0.0 copy-done.1
  42.6 0.0 copy-done.2
  42.6 0.2 owner.1
  42.7 8.1 %all_to_all.16.arrived_ref = bf16[4,2,16,128]{3,2,1,0:T(8,128)(2,1)S(1)} all-to-all(bf16[4,2,16,128]{3,2,1,0:T(8,128)(2,1)S(1)} %get-tuple-element.17), channel_id=1, replica_groups={{0,128,256,384},{1,129,257,385},{2,130,258,386},{3,131,259,387},{4,132,..., dimensions={0} | all-to-all | bytes 65536 | tf_op jit(solution)/shard_map/all_to_all | solution.py:29
  50.9 19.0 %all_to_all.17 = bf16[64,16,128]{2,1,0:T(8,128)(2,1)S(1)} all-to-all(bf16[64,16,128]{2,1,0:T(8,128)(2,1)S(1)} %update.1), channel_id=1, replica_groups={{0,2,4,6,8,10,12,14,16,18,20,22,24,26,28,30,32,34,36,38,40,42,44,46,48,..., dimensions={0} | all-to-all | bytes 524288 | tf_op jit(solution)/shard_map/all_to_all | solution.py:29
  69.9 5.8 %all-gather = bf16[128,16,128]{2,1,0:T(8,128)(2,1)S(1)} all-gather(bf16[64,16,128]{2,1,0:T(8,128)(2,1)S(1)} %all_to_all.17), channel_id=2, replica_groups={{0,1},{2,3},{4,5},{6,7},{8,9},{10,11},{12,13},{14,15},{16,17},{18,19},{..., dimensions={0}, use_global_device_ids=true | all-gather | bytes 786432 | tf_op jit(solution)/shard_map/all_gather | solution.py:40
  75.7 1.0 %assemble.1 = (bf16[512,512]{1,0:T(8,128)(2,1)}, f32[1,16,128]{2,1,0:T(8,128)}) custom-call(bf16[2,64,16,128]{3,2,1,0:T(8,128)(2,1)S(1)} %bitcast.2, f32[16,128]{1,0:T(8,128)S(1)} %get-tuple-element.18.last_ref, f32[16,128]{1,0:T(8,128)S(1)} %get-tuple-element.19.kept_ref), custom_call_target="tpu_custom_call" | custom-call | tf_op jit(solution)/shard_map/assemble/pallas_call | solution.py:243
  (1 shorter events, 0.0 us)
Async XLA Ops:
  3.6 10.3 %collective-permute-start = (bf16[64,2,16,128]{3,2,1,0:T(8,128)(2,1)S(1)}, bf16[64,2,16,128]{3,2,1,0:T(8,128)(2,1)S(1)}, u32[]{:S(2)}, u32[]{:S(2)}) collective-permute-start(bf16[64,2,16,128]{3,2,1,0:T(8,128)(2,1)S(1)} %get-tuple-element.14), channel_id=1, source_target_pairs={{0,1},{1,0},{2,3},{3,2},{4,5},{5,4},{6,7},{7,6},{8,9},{9,8},{10,11... | collective-permute-start | bytes 1572872 | tf_op jit(solution)/shard_map/ppermute | solution.py:36
  14.1 28.5 %copy-start = (f32[1,16,128]{2,1,0:T(8,128)S(1)}, f32[1,16,128]{2,1,0:T(8,128)}, u32[]{:S(2)}) copy-start(f32[1,16,128]{2,1,0:T(8,128)} %oresid_ref.1) | copy-start | bytes 24580
  14.1 28.5 %copy-start.1 = (s32[1,2,16]{2,1,0:T(2,128)S(1)}, s32[1,2,16]{2,1,0:T(2,128)}, u32[]{:S(2)}) copy-start(s32[1,2,16]{2,1,0:T(2,128)} %rank_ref.1) | copy-start | bytes 388
  14.1 28.5 %copy-start.2 = (s32[1,2]{1,0:T(1,128)S(1)}, s32[1,2]{1,0:T(1,128)}, u32[]{:S(2)}) copy-start(s32[1,2]{1,0:T(1,128)} %count_ref.1) | copy-start | bytes 28

commit v7 on v6

--- a/solution.py
+++ b/solution.py
@@ -13,6 +13,7 @@
 NX, NZ, NY, NC = 4, 8, 8, 2
 CHIPS = NZ * NY
 REGION = 16
+ROWS = 4
 WIDTH = 128
 BF = jnp.bfloat16
 F32 = jnp.float32
@@ -114,7 +115,7 @@
     copy.wait()
 
 
-def owner_kernel(arrived_ref, oresid_ref, count_ref, rank_ref, out_ref, last_ref, kept_ref):
+def owner_kernel(arrived_ref, oresid_ref, count_ref, rank_ref, out_ref, last_ref, kept_ref, going_ref):
     eye = (lax.broadcasted_iota(jnp.int32, (REGION, REGION), 0)
            == lax.broadcasted_iota(jnp.int32, (REGION, REGION), 1))
     oresid = oresid_ref[0]
@@ -127,36 +128,44 @@
         square = jnp.where(eye, jnp.broadcast_to(row, (REGION, REGION)), 0.0)
         passed = jnp.broadcast_to(jnp.sum(square, axis=1, keepdims=True), (REGION, WIDTH)) > 0.5
         total = total + oresid
-        going = jnp.where(passed, total, 0.0).astype(BF)
+        going_ref[s] = jnp.where(passed, total, 0.0)
         oresid = jnp.where(passed, 0.0, total)
-        for k in range(out_ref.shape[0]):
-            out_ref[k, s] = going
+        for c in range(NC):
+            tiles = [going_ref[s, pl.ds(NC * c + j, ROWS, stride=REGION // ROWS), :] for j in range(2)]
+            both = jnp.concatenate(tiles, axis=0).astype(BF)
+            for x in range(NX):
+                out_ref[x * NC + c, s] = both
     last_ref[...] = total
     kept_ref[...] = jnp.where(passed, 0.0, 1.0)
 
 
 def update_kernel(arrived_ref, out_ref):
-    total = jnp.zeros((REGION, WIDTH), F32)
-    for s in range(arrived_ref.shape[1]):
-        cross = arrived_ref[0, s].astype(F32)
-        for x in range(1, NX):
-            cross = cross + arrived_ref[x, s].astype(F32)
-        total = total + cross.astype(BF).astype(F32)
-    applied = (-STEP_SIZE * total).astype(BF)
-    for k in range(out_ref.shape[0]):
-        out_ref[k] = applied
-
-
-def assemble_kernel(halves_ref, last_ref, kept_ref, out_ref, oresid_ref, flat_ref):
+    parts = []
+    for c in range(NC):
+        total = jnp.zeros(arrived_ref.shape[2:], F32)
+        for s in range(arrived_ref.shape[1]):
+            cross = arrived_ref[c, s].astype(F32)
+            for x in range(1, NX):
+                cross = cross + arrived_ref[x * NC + c, s].astype(F32)
+            total = total + cross.astype(BF).astype(F32)
+        parts.append(-STEP_SIZE * total)
+    for j in range(2):
+        tile = jnp.concatenate([part[j * ROWS:(j + 1) * ROWS] for part in parts], axis=0).astype(BF)
+        for k in range(out_ref.shape[0]):
+            out_ref[k, j] = tile
+
+
+def assemble_kernel(halves_ref, last_ref, kept_ref, out_hbm, oresid_ref, sems):
+    sends = []
+    for c in range(NC):
+        for j in range(2):
+            t = 2 * c + j
+            sends.append(pltpu.make_async_copy(
+                halves_ref.at[c, :, j], out_hbm.at[:, :, t * WIDTH:(t + 1) * WIDTH], sems.at[t]))
+            sends[-1].start()
     oresid_ref[0] = jnp.where(kept_ref[...] > 0.5, last_ref[...], 0.0)
-    rows, cols = out_ref.shape
-    tiles = cols // WIDTH
-    for i in range(CHIPS):
-        for c in range(NC):
-            at = (i * NC + c) * REGION
-            flat_ref[at:at + REGION, :] = halves_ref[c, i].astype(F32)
-    for t in range(tiles):
-        out_ref[:, t * WIDTH:(t + 1) * WIDTH] = flat_ref[pl.ds(t, rows, stride=tiles), :].astype(BF)
+    for send in sends:
+        send.wait()
 
 
 def vmem():
@@ -226,7 +235,8 @@
         owner_kernel,
         in_specs=[vmem(), vmem(), vmem(), vmem()],
         out_specs=[vmem(), vmem(), vmem()],
-        out_shape=[jax.ShapeDtypeStruct((NX, steps, REGION, WIDTH), BF), tile, tile],
+        out_shape=[jax.ShapeDtypeStruct((NX * NC, steps, NC * ROWS, WIDTH), BF), tile, tile],
+        scratch_shapes=[pltpu.VMEM((steps, REGION, WIDTH), F32)],
         compiler_params=params,
         name="owner",
     )(arrived, owner_residual, out_count, out_rank)
@@ -235,26 +245,24 @@
         update_kernel,
         in_specs=[vmem()],
         out_specs=vmem(),
-        out_shape=jax.ShapeDtypeStruct((CHIPS, REGION, WIDTH), BF),
+        out_shape=jax.ShapeDtypeStruct((CHIPS, 2, NC * ROWS, WIDTH), BF),
         compiler_params=params,
         name="update",
-    )(exchange(outgoing, (0,)))
+    )(exchange(outgoing, (0, 3)))
     halves = of_both_cores(exchange(copies, (1, 2)))
     applied, new_owner = pl.pallas_call(
         assemble_kernel,
         in_specs=[vmem(), vmem(), vmem()],
-        out_specs=[vmem(), vmem()],
+        out_specs=[hbm(), vmem()],
         out_shape=[
-            jax.ShapeDtypeStruct((rows, cols), BF),
+            jax.ShapeDtypeStruct((CHIPS, NC * ROWS, cols), BF),
             jax.ShapeDtypeStruct(owner_residual.shape, F32),
         ],
-        scratch_shapes=[
-            pltpu.VMEM((blocks, WIDTH), F32),
-        ],
+        scratch_shapes=[pltpu.SemaphoreType.DMA((4,))],
         compiler_params=params,
         name="assemble",
     )(halves, last, kept)
-    return applied, new_residual, new_owner
+    return applied.reshape(rows, cols), new_residual, new_owner
 
 
 def solution(mesh):

time: 77 us -> 78.6 us (1.021)
  blocking collectives: 61.4 us -> 62.6 us
    all_to_all x3, blocking collectives: 55.6 us -> 57.5 us  [exchange(): lax.all_to_all(value, 'd', split_axis=0, concat_axis=0, tiled=True, axis_...]
where the time goes in v7:
time: 78.6 us; the launch traced here: 78.3 us
  blocking collectives  62.6 us (80%)
  starting transfers between devices  8.77 us (11%)
  Pallas kernels  5.58 us (7%)
    all_to_all x3, blocking collectives, exchange(): lax.all_to_all(value, 'd', split_axis=0, concat_axis=0, tiled=True, axis_...  57.5 us
    ppermute x1, starting transfers between devices, other_core(): return lax.ppermute(value, 'd', pairs)  8.77 us
    all_gather x1, blocking collectives, of_both_cores(): lax.all_gather(value, 'd', axis=0, axis_index_groups=groups_along((3,)))  5.05 us
    pallas_call x1, Pallas kernels, per_device(): pl.pallas_call(local, in_specs=[smem(), hbm(), hbm(), hbm(), hbm(), hbm()...  2.97 us
  transfers between devices with their start and end apart: 1, of which 1 were waited for; matrix products, arithmetic and copies ran while one was open for 0% of the time, Pallas kernels for 1%

profile of v7, /device:TPU:1, one launch (start us, length us, event | category | flops | bytes accessed | tf_op | source)
XLA Modules:
  0.0 78.3 jit_solution(6025510231465198578)
XLA Ops:
  0.6 3.0 %local.1 = (f32[1,2048,128]{2,1,0:T(8,128)S(1)}, bf16[64,2,16,128]{3,2,1,0:T(8,128)(2,1)S(1)}, bf16[64,2,16,128]{3,2,1,0:T(8,128)(2,1)S(1)}) custom-call(s32[1]{0:T(128)} %bitcast.args_0_, bf16[1,2,512,512]{3,2,1,0:T(8,128)(2,1)} %args_1_.4, bf16[1,2,512,512]{3,2,1,0:T(8,128)(2,1)} %args_2_.4, f32[1,2048,128]{2,1,0:T(8,128)} %args_3_.4, ...), custom_call_target="tpu_custom_call" | custom-call | tf_op jit(solution)/shard_map/local/pallas_call | solution.py:195
  3.6 8.8 %collective-permute-start = (bf16[64,2,16,128]{3,2,1,0:T(8,128)(2,1)S(1)}, bf16[64,2,16,128]{3,2,1,0:T(8,128)(2,1)S(1)}, u32[]{:S(2)}, u32[]{:S(2)}) collective-permute-start(bf16[64,2,16,128]{3,2,1,0:T(8,128)(2,1)S(1)} %get-tuple-element.14), channel_id=1, source_target_pairs={{0,1},{1,0},{2,3},{3,2},{4,5},{5,4},{6,7},{7,6},{8,9},{9,8},{10,11... | collective-permute-start | bytes 1572872 | tf_op jit(solution)/shard_map/ppermute | solution.py:37
  12.4 1.0 %store.1 = f32[1,2048,128]{2,1,0:T(8,128)} custom-call(f32[1,2048,128]{2,1,0:T(8,128)S(1)} %get-tuple-element.15.value_ref), custom_call_target="tpu_custom_call" | custom-call | tf_op jit(solution)/shard_map/store/pallas_call | solution.py:220
  13.4 0.5 collective-permute-done
  13.9 0.1 add_convert_fusion
  14.1 0.0 copy-start
  14.1 0.0 copy-start.1
  14.1 0.0 copy-start.2
  14.1 28.5 %all_to_all.15.arrived_ref = bf16[64,2,16,128]{3,2,1,0:T(8,128)(2,1)S(1)} all-to-all(bf16[64,2,16,128]{3,2,1,0:T(8,128)(2,1)S(1)} %add_convert_fusion), channel_id=1, replica_groups={{0,2,4,6,8,10,12,14,16,18,20,22,24,26,28,30,32,34,36,38,40,42,44,46,48,..., dimensions={0} | all-to-all | bytes 1048576 | tf_op jit(solution)/shard_map/all_to_all | solution.py:30
  42.6 0.0 copy-done
  42.6 0.0 copy-done.1
  42.6 0.0 copy-done.2
  42.6 0.2 owner.1
  42.7 11.7 %all_to_all.16.arrived_ref = bf16[8,2,8,128]{3,2,1,0:T(8,128)(2,1)S(1)} all-to-all(bf16[8,2,8,128]{3,2,1,0:T(8,128)(2,1)S(1)} %get-tuple-element.17), channel_id=1, replica_groups={{0,1,128,129,256,257,384,385},{2,3,130,131,258,259,386,387},{4,5,132,13..., dimensions={0} | all-to-all | bytes 65536 | tf_op jit(solution)/shard_map/all_to_all | solution.py:30
  54.5 17.3 %all_to_all.17 = bf16[64,2,8,128]{3,2,1,0:T(8,128)(2,1)S(1)} all-to-all(bf16[64,2,8,128]{3,2,1,0:T(8,128)(2,1)S(1)} %update.1), channel_id=1, replica_groups={{0,2,4,6,8,10,12,14,16,18,20,22,24,26,28,30,32,34,36,38,40,42,44,46,48,..., dimensions={0} | all-to-all | bytes 524288 | tf_op jit(solution)/shard_map/all_to_all | solution.py:30
  71.9 5.0 %all-gather = bf16[128,2,8,128]{3,2,1,0:T(8,128)(2,1)S(1)} all-gather(bf16[64,2,8,128]{3,2,1,0:T(8,128)(2,1)S(1)} %all_to_all.17), channel_id=2, replica_groups={{0,1},{2,3},{4,5},{6,7},{8,9},{10,11},{12,13},{14,15},{16,17},{18,19},{..., dimensions={0}, use_global_device_ids=true | all-gather | bytes 786432 | tf_op jit(solution)/shard_map/all_gather | solution.py:41
  76.9 1.4 %assemble.1 = (bf16[64,8,512]{2,1,0:T(8,128)(2,1)}, f32[1,16,128]{2,1,0:T(8,128)}) custom-call(bf16[2,64,2,8,128]{4,3,2,1,0:T(8,128)(2,1)S(1)} %bitcast.3, f32[16,128]{1,0:T(8,128)S(1)} %get-tuple-element.18.last_ref, f32[16,128]{1,0:T(8,128)S(1)} %get-tuple-element.19.kept_ref), custom_call_target="tpu_custom_call" | custom-call | tf_op jit(solution)/shard_map/assemble/pallas_call | solution.py:253
  (1 shorter events, 0.0 us)
Async XLA Ops:
  3.6 10.3 %collective-permute-start = (bf16[64,2,16,128]{3,2,1,0:T(8,128)(2,1)S(1)}, bf16[64,2,16,128]{3,2,1,0:T(8,128)(2,1)S(1)}, u32[]{:S(2)}, u32[]{:S(2)}) collective-permute-start(bf16[64,2,16,128]{3,2,1,0:T(8,128)(2,1)S(1)} %get-tuple-element.14), channel_id=1, source_target_pairs={{0,1},{1,0},{2,3},{3,2},{4,5},{5,4},{6,7},{7,6},{8,9},{9,8},{10,11... | collective-permute-start | bytes 1572872 | tf_op jit(solution)/shard_map/ppermute | solution.py:37
  14.1 28.5 %copy-start = (f32[1,16,128]{2,1,0:T(8,128)S(1)}, f32[1,16,128]{2,1,0:T(8,128)}, u32[]{:S(2)}) copy-start(f32[1,16,128]{2,1,0:T(8,128)} %oresid_ref.1) | copy-start | bytes 24580
  14.1 28.5 %copy-start.1 = (s32[1,2,16]{2,1,0:T(2,128)S(1)}, s32[1,2,16]{2,1,0:T(2,128)}, u32[]{:S(2)}) copy-start(s32[1,2,16]{2,1,0:T(2,128)} %rank_ref.1) | copy-start | bytes 388
  14.1 28.5 %copy-start.2 = (s32[1,2]{1,0:T(1,128)S(1)}, s32[1,2]{1,0:T(1,128)}, u32[]{:S(2)}) copy-start(s32[1,2]{1,0:T(1,128)} %count_ref.1) | copy-start | bytes 28

commit v8 on v6

--- a/solution.py
+++ b/solution.py
@@ -13,6 +13,9 @@
 NX, NZ, NY, NC = 4, 8, 8, 2
 CHIPS = NZ * NY
 REGION = 16
+CAP = 8
+NONE = 31.0
+WHOLE = (NZ * NY * 2 - 1) * REGION
 WIDTH = 128
 BF = jnp.bfloat16
 F32 = jnp.float32
@@ -31,18 +34,13 @@
     )
 
 
-def other_core(value):
-    pairs = [(i, i ^ 1) for i in range(NX * NZ * NY * NC)]
-    return lax.ppermute(value, "d", pairs)
-
-
 def of_both_cores(value):
     return lax.all_gather(value, "d", axis=0, axis_index_groups=groups_along((3,)))
 
 
 def local_kernel(scale, core_ref, acts_hbm, cot_hbm, resid_hbm, count_hbm, rank_hbm,
                  resid_ref, keep_ref, give_ref,
-                 acts_ref, cot_ref, acc_ref, count_ref, rank_ref, ranks_ref, chosen_ref, sems):
+                 acts_ref, cot_ref, acc_ref, count_ref, rank_ref, ranks_ref, chosen_ref, last_ref, pack_ref, sems):
     core = core_ref[0]
     steps, _, rows = acts_ref.shape
     cols = cot_ref.shape[2]
@@ -76,6 +74,8 @@
         spread = jnp.where(lane_id // per == row_id, count, 0.0)
         limit = jnp.dot(spread.astype(BF), place, preferred_element_type=F32)
         chosen = jnp.where(ranks_ref[s].astype(F32) < limit, 1.0, 0.0)
+        if s == steps - 1:
+            last_ref[...] = jnp.where(chosen > 0.5, ranks_ref[s].astype(F32), NONE)
         chosen_ref[s] = lax.dot_general(chosen.astype(BF), eye, (((0,), (0,)), ((), ())),
                                         preferred_element_type=F32)
 
@@ -104,14 +104,41 @@
                     sent = jnp.where(mask, total, 0.0).astype(BF)
                     for i in range(WIDTH // REGION):
                         owner = r * (WIDTH // REGION) + i
-                        to = keep_ref if owner % NC == me else give_ref
-                        to[owner // NC, s] = sent[i * REGION:(i + 1) * REGION, :]
-
-
-def store_kernel(value_ref, out_hbm, sem):
-    copy = pltpu.make_async_copy(value_ref, out_hbm, sem)
-    copy.start()
-    copy.wait()
+                        at = ((owner // NC) * steps + s) * REGION
+                        tile = sent[i * REGION:(i + 1) * REGION, :]
+                        if owner % NC == me:
+                            keep_ref[at:at + REGION, :] = tile
+                        elif at < WHOLE:
+                            give_ref[at:at + REGION, :] = tile
+                        else:
+                            slots = last_ref[r:r + 1, :]
+                            wide = jnp.broadcast_to(slots, (REGION, WIDTH))
+                            slot = lax.broadcasted_iota(jnp.int32, (REGION, WIDTH), 0).astype(F32)
+                            lane = lax.broadcasted_iota(jnp.int32, (REGION, WIDTH), 1)
+                            pick = jnp.where((wide == slot) & (lane // REGION == i), 1.0, 0.0)
+                            packed = jnp.dot(pick.astype(BF), sent, preferred_element_type=F32)
+                            pack_ref[0:CAP, :] = packed[0:CAP, :]
+                            pack_ref[CAP:2 * CAP, :] = jnp.broadcast_to(slots, (CAP, WIDTH))
+                            give_ref[at:at + CAP + 2, :] = pack_ref[0:CAP + 2, :].astype(BF)
+
+
+def pair_kernel(core_ref, keep_ref, both_ref, out_ref, tile_ref):
+    core = core_ref[0]
+    other = 1 - core
+    chunk = 8 * REGION
+    for at in range(0, WHOLE, chunk):
+        span = slice(at, min(at + chunk, WHOLE))
+        total = keep_ref[span, :].astype(F32) + both_ref[other, span, :].astype(F32)
+        out_ref[span, :] = total.astype(BF)
+    packed = both_ref[other, WHOLE:WHOLE + CAP, :].astype(F32)
+    packed = jnp.concatenate([packed, jnp.zeros_like(packed)], axis=0).astype(BF)
+    slots = both_ref[other, WHOLE + CAP:WHOLE + CAP + 2, :].astype(F32)[0:1, :]
+    slot = lax.broadcasted_iota(jnp.int32, (REGION, WIDTH), 0).astype(F32)
+    pick = jnp.where(jnp.broadcast_to(slots, (REGION, WIDTH)) == slot, 1.0, 0.0).astype(BF)
+    tile_ref[...] = lax.dot_general(pick, packed, (((0,), (0,)), ((), ())), preferred_element_type=F32)
+    at = pl.multiple_of(WIDTH - NC * REGION + core * REGION, REGION)
+    total = keep_ref[WHOLE:WHOLE + REGION, :].astype(F32) + tile_ref[pl.ds(at, REGION), :]
+    out_ref[WHOLE:WHOLE + REGION, :] = total.astype(BF)
 
 
 def owner_kernel(arrived_ref, oresid_ref, count_ref, rank_ref, out_ref, last_ref, kept_ref):
@@ -182,15 +209,15 @@
     def local(*args):
         return local_kernel(scale, *args)
 
-    half = (CHIPS, steps, REGION, WIDTH)
+    size = CHIPS * steps * REGION
     new_resid, keep, give = pl.pallas_call(
         local,
         in_specs=[smem(), hbm(), hbm(), hbm(), hbm(), hbm()],
         out_specs=[vmem(), vmem(), vmem()],
         out_shape=[
-            jax.ShapeDtypeStruct(residual.shape, F32),
-            jax.ShapeDtypeStruct(half, BF),
-            jax.ShapeDtypeStruct(half, BF),
+            pltpu.VMEM(residual.shape, F32),
+            jax.ShapeDtypeStruct((size, WIDTH), BF),
+            jax.ShapeDtypeStruct((WHOLE + CAP + 2, WIDTH), BF),
         ],
         scratch_shapes=[
             pltpu.VMEM((steps, tokens, rows), BF),
@@ -200,6 +227,8 @@
             pltpu.VMEM(in_rank.shape, jnp.int32),
             pltpu.VMEM((steps, blocks // WIDTH, WIDTH), jnp.int32),
             pltpu.VMEM((steps, WIDTH, WIDTH), F32),
+            pltpu.VMEM((blocks // WIDTH, WIDTH), F32),
+            pltpu.VMEM((2 * CAP, WIDTH), F32),
             pltpu.SemaphoreType.DMA((3 + 2 * steps,)),
         ],
         compiler_params=params,
@@ -207,18 +236,17 @@
     )(core, *[pltpu.with_memory_space_constraint(v, pltpu.HBM)
             for v in (acts, cotangent, residual, in_count, in_rank)])
 
-    given = other_core(give)
-    new_residual = pl.pallas_call(
-        store_kernel,
-        in_specs=[vmem()],
-        out_specs=hbm(),
-        out_shape=jax.ShapeDtypeStruct(residual.shape, F32),
-        scratch_shapes=[pltpu.SemaphoreType.DMA],
-        compiler_params=params,
-        name="store",
-    )(new_resid)
-    pair = (keep.astype(F32) + given.astype(F32)).astype(BF)
-    pair, new_residual = lax.optimization_barrier((pair, new_residual))
+    pair = pl.pallas_call(
+        pair_kernel,
+        in_specs=[smem(), vmem(), vmem()],
+        out_specs=vmem(),
+        out_shape=jax.ShapeDtypeStruct((size, WIDTH), BF),
+        scratch_shapes=[pltpu.VMEM((WIDTH, WIDTH), F32)],
+        compiler_params=params,
+        name="pair",
+    )(core, keep, of_both_cores(give))
+    new_residual = new_resid
+    pair = pair.reshape(CHIPS, steps, REGION, WIDTH)
     arrived = exchange(pair, (1, 2))
 
     tile = jax.ShapeDtypeStruct((REGION, WIDTH), F32)
@@ -235,7 +263,7 @@
         update_kernel,
         in_specs=[vmem()],
         out_specs=vmem(),
-        out_shape=jax.ShapeDtypeStruct((CHIPS, REGION, WIDTH), BF),
+        out_shape=pltpu.VMEM((CHIPS, REGION, WIDTH), BF),
         compiler_params=params,
         name="update",
     )(exchange(outgoing, (0,)))

time: 77 us -> 76.8 us (level)
  waiting for transfers between devices: 0.53 us -> 11.6 us
  blocking collectives: 61.4 us -> 51.4 us
  starting transfers between devices: 8.77 us -> 6.62 us
  local copies, waits for them, and re-layouts: 0.02 us -> 0.99 us
    all_to_all x3 -> x2, blocking collectives: 55.6 us -> 36.6 us  [exchange(): lax.all_to_all(value, 'd', split_axis=0, concat_axis=0, tiled=True, axis_...]
    all_to_all x0 -> x1, waiting for transfers between devices: none -> 11.6 us  [exchange(): lax.all_to_all(value, 'd', split_axis=0, concat_axis=0, tiled=True, axis_...]
    all_gather x1 -> x2, blocking collectives: 5.78 us -> 14.8 us  [of_both_cores(): lax.all_gather(value, 'd', axis=0, axis_index_groups=groups_along((3,)))]
    ppermute x1 -> x0, starting transfers between devices: 8.77 us -> none  [other_core(): return lax.ppermute(value, 'd', pairs)]
    all_to_all x0 -> x1, starting transfers between devices: none -> 6.62 us  [exchange(): lax.all_to_all(value, 'd', split_axis=0, concat_axis=0, tiled=True, axis_...]
    unnamed x6 -> x7, local copies, waits for them, and re-layouts: 0.02 us -> 0.99 us
  transfers between devices with their start and end apart: 1 -> 1, of which waited for: 1 -> 1; matrix products, arithmetic and copies ran while one was open for 0% -> 1% of each run, Pallas kernels for 1% -> 0%
where the time goes in v8:
time: 76.8 us; the launch traced here: 76.4 us
  blocking collectives  51.4 us (67%)
  waiting for transfers between devices  11.6 us (15%)
  starting transfers between devices  6.62 us (9%)
  Pallas kernels  5.07 us (7%)
  local copies, waits for them, and re-layouts  0.99 us (1%)
    all_to_all x2, blocking collectives, exchange(): lax.all_to_all(value, 'd', split_axis=0, concat_axis=0, tiled=True, axis_...  36.6 us
    all_gather x2, blocking collectives, of_both_cores(): lax.all_gather(value, 'd', axis=0, axis_index_groups=groups_along((3,)))  14.8 us
    all_to_all x1, waiting for transfers between devices, exchange(): lax.all_to_all(value, 'd', split_axis=0, concat_axis=0, tiled=True, axis_...  11.6 us
    all_to_all x1, starting transfers between devices, exchange(): lax.all_to_all(value, 'd', split_axis=0, concat_axis=0, tiled=True, axis_...  6.62 us
    pallas_call x1, Pallas kernels, per_device(): pl.pallas_call(local, in_specs=[smem(), hbm(), hbm(), hbm(), hbm(), hbm()...  3 us
  transfers between devices with their start and end apart: 1, of which 1 were waited for; matrix products, arithmetic and copies ran while one was open for 1% of the time, Pallas kernels for 0%

profile of v8, /device:TPU:1, one launch (start us, length us, event | category | flops | bytes accessed | tf_op | source)
XLA Modules:
  0.0 76.4 jit_solution(2814663707273057244)
XLA Ops:
  0.6 3.0 %local.1 = (f32[1,2048,128]{2,1,0:T(8,128)S(1)}, bf16[2048,128]{1,0:T(8,128)(2,1)S(1)}, bf16[2042,128]{1,0:T(8,128)(2,1)S(1)}) custom-call(s32[1]{0:T(128)} %bitcast.args_0_.core_ref, bf16[1,2,512,512]{3,2,1,0:T(8,128)(2,1)} %args_1_.4, bf16[1,2,512,512]{3,2,1,0:T(8,128)(2,1)} %args_2_.4, f32[1,2048,128]{2,1,0:T(8,128)} %args_3_.4, s32[1,2,128]{2,1,0:T(2,128)} %args_4_.4, ...), custom_call_target="tpu_custom_call" | custom-call | tf_op jit(solution)/shard_map/local/pallas_call | solution.py:213
  3.7 9.0 %all-gather.2.both_ref = bf16[2,2042,128]{2,1,0:T(8,128)(2,1)S(1)} all-gather(bf16[1,2042,128]{2,1,0:T(8,128)(2,1)S(1)} %bitcast.6), channel_id=2, replica_groups={{0,1},{2,3},{4,5},{6,7},{8,9},{10,11},{12,13},{14,15},{16,17},{18,19},{..., dimensions={0}, use_global_device_ids=true | all-gather | bytes 1568256 | tf_op jit(solution)/shard_map/all_gather | solution.py:38
  12.7 0.2 pair.1
  12.9 0.0 copy-start
  12.9 0.0 copy-start.1
  13.0 0.0 copy-start.2
  13.0 28.5 %all_to_all.15.arrived_ref = bf16[64,2,16,128]{3,2,1,0:T(8,128)(2,1)S(1)} all-to-all(bf16[64,2,16,128]{3,2,1,0:T(8,128)(2,1)S(1)} %bitcast.4), channel_id=1, replica_groups={{0,2,4,6,8,10,12,14,16,18,20,22,24,26,28,30,32,34,36,38,40,42,44,46,48,..., dimensions={0} | all-to-all | bytes 1048576 | tf_op jit(solution)/shard_map/all_to_all | solution.py:32
  41.4 0.0 copy-done
  41.4 0.0 copy-done.1
  41.4 0.0 copy-done.2
  41.4 0.2 owner.1
  41.6 8.1 %all_to_all.16.arrived_ref = bf16[4,2,16,128]{3,2,1,0:T(8,128)(2,1)S(1)} all-to-all(bf16[4,2,16,128]{3,2,1,0:T(8,128)(2,1)S(1)} %get-tuple-element.13), channel_id=1, replica_groups={{0,128,256,384},{1,129,257,385},{2,130,258,386},{3,131,259,387},{4,132,..., dimensions={0} | all-to-all | bytes 65536 | tf_op jit(solution)/shard_map/all_to_all | solution.py:32
  49.7 0.7 update.1
  50.4 6.6 %all-to-all-start.2 = ((bf16[64,16,128]{2,1,0:T(8,128)(2,1)}), bf16[64,16,128]{2,1,0:T(8,128)(2,1)S(1)}, u32[]{:S(2)}, u32[]{:S(2)}) async-start(bf16[64,16,128]{2,1,0:T(8,128)(2,1)} %update.1), calls=%async_computation.2 | async-start | bytes 524288 | tf_op jit(solution)/shard_map/all_to_all | solution.py:32
  57.1 1.0 %copy.11 = f32[1,2048,128]{2,1,0:T(8,128)} copy(f32[1,2048,128]{2,1,0:T(8,128)S(1)} %get-tuple-element.20) | data formatting | bytes 2097152
  58.0 11.6 %all-to-all-done.2 = bf16[64,16,128]{2,1,0:T(8,128)(2,1)S(1)} async-done(((bf16[64,16,128]{2,1,0:T(8,128)(2,1)}), bf16[64,16,128]{2,1,0:T(8,128)(2,1)S(1)}, u32[]{:S(2)}, u32[]{:S(2)}) %all-to-all-start.2) | async-done | bytes 262176 | tf_op jit(solution)/shard_map/all_to_all | solution.py:32
  69.7 5.8 %all-gather.1 = bf16[128,16,128]{2,1,0:T(8,128)(2,1)S(1)} all-gather(bf16[64,16,128]{2,1,0:T(8,128)(2,1)S(1)} %all-to-all-done.2), channel_id=3, replica_groups={{0,1},{2,3},{4,5},{6,7},{8,9},{10,11},{12,13},{14,15},{16,17},{18,19},{..., dimensions={0}, use_global_device_ids=true | all-gather | bytes 786432 | tf_op jit(solution)/shard_map/all_gather | solution.py:38
  75.5 1.0 %assemble.1 = (bf16[512,512]{1,0:T(8,128)(2,1)}, f32[1,16,128]{2,1,0:T(8,128)}) custom-call(bf16[2,64,16,128]{3,2,1,0:T(8,128)(2,1)S(1)} %bitcast.5, f32[16,128]{1,0:T(8,128)S(1)} %get-tuple-element.14.last_ref, f32[16,128]{1,0:T(8,128)S(1)} %get-tuple-element.15.kept_ref), custom_call_target="tpu_custom_call" | custom-call | tf_op jit(solution)/shard_map/assemble/pallas_call | solution.py:271
Async XLA Ops:
  12.9 28.5 %copy-start = (f32[1,16,128]{2,1,0:T(8,128)S(1)}, f32[1,16,128]{2,1,0:T(8,128)}, u32[]{:S(2)}) copy-start(f32[1,16,128]{2,1,0:T(8,128)} %oresid_ref.1) | copy-start | bytes 24580
  12.9 28.5 %copy-start.1 = (s32[1,2,16]{2,1,0:T(2,128)S(1)}, s32[1,2,16]{2,1,0:T(2,128)}, u32[]{:S(2)}) copy-start(s32[1,2,16]{2,1,0:T(2,128)} %rank_ref.1) | copy-start | bytes 388
  13.0 28.5 %copy-start.2 = (s32[1,2]{1,0:T(1,128)S(1)}, s32[1,2]{1,0:T(1,128)}, u32[]{:S(2)}) copy-start(s32[1,2]{1,0:T(1,128)} %count_ref.1) | copy-start | bytes 28
  50.4 19.2 %all-to-all-start.2 = ((bf16[64,16,128]{2,1,0:T(8,128)(2,1)}), bf16[64,16,128]{2,1,0:T(8,128)(2,1)S(1)}, u32[]{:S(2)}, u32[]{:S(2)}) async-start(bf16[64,16,128]{2,1,0:T(8,128)(2,1)} %update.1), calls=%async_computation.2 | async-start | bytes 524288 | tf_op jit(solution)/shard_map/all_to_all | solution.py:32

commit v9 on v8

--- a/solution.py
+++ b/solution.py
@@ -122,7 +122,16 @@
                             give_ref[at:at + CAP + 2, :] = pack_ref[0:CAP + 2, :].astype(BF)
 
 
-def pair_kernel(core_ref, keep_ref, both_ref, out_ref, tile_ref):
+def stored(resid_ref, store_hbm, sem, part):
+    quarter = resid_ref.shape[1] // 4
+    span = slice(part[0] * quarter, part[1] * quarter)
+    copy = pltpu.make_async_copy(resid_ref.at[:, span], store_hbm.at[:, span], sem)
+    copy.start()
+    return copy
+
+
+def pair_kernel(core_ref, keep_ref, both_ref, resid_ref, out_ref, store_hbm, tile_ref, sem):
+    store = stored(resid_ref, store_hbm, sem, (0, 1))
     core = core_ref[0]
     other = 1 - core
     chunk = 8 * REGION
@@ -139,9 +148,12 @@
     at = pl.multiple_of(WIDTH - NC * REGION + core * REGION, REGION)
     total = keep_ref[WHOLE:WHOLE + REGION, :].astype(F32) + tile_ref[pl.ds(at, REGION), :]
     out_ref[WHOLE:WHOLE + REGION, :] = total.astype(BF)
-
-
-def owner_kernel(arrived_ref, oresid_ref, count_ref, rank_ref, out_ref, last_ref, kept_ref):
+    store.wait()
+
+
+def owner_kernel(arrived_ref, oresid_ref, count_ref, rank_ref, resid_ref, begun_hbm,
+                 out_ref, last_ref, kept_ref, store_hbm, sem):
+    store = stored(resid_ref, store_hbm, sem, (1, 2))
     eye = (lax.broadcasted_iota(jnp.int32, (REGION, REGION), 0)
            == lax.broadcasted_iota(jnp.int32, (REGION, REGION), 1))
     oresid = oresid_ref[0]
@@ -160,6 +172,7 @@
             out_ref[k, s] = going
     last_ref[...] = total
     kept_ref[...] = jnp.where(passed, 0.0, 1.0)
+    store.wait()
 
 
 def update_kernel(arrived_ref, out_ref):
@@ -174,7 +187,9 @@
         out_ref[k] = applied
 
 
-def assemble_kernel(halves_ref, last_ref, kept_ref, out_ref, oresid_ref, flat_ref):
+def assemble_kernel(halves_ref, last_ref, kept_ref, resid_ref, begun_hbm,
+                    out_ref, oresid_ref, store_hbm, flat_ref, sem):
+    store = stored(resid_ref, store_hbm, sem, (2, 4))
     oresid_ref[0] = jnp.where(kept_ref[...] > 0.5, last_ref[...], 0.0)
     rows, cols = out_ref.shape
     tiles = cols // WIDTH
@@ -184,6 +199,7 @@
             flat_ref[at:at + REGION, :] = halves_ref[c, i].astype(F32)
     for t in range(tiles):
         out_ref[:, t * WIDTH:(t + 1) * WIDTH] = flat_ref[pl.ds(t, rows, stride=tiles), :].astype(BF)
+    store.wait()
 
 
 def vmem():
@@ -236,52 +252,53 @@
     )(core, *[pltpu.with_memory_space_constraint(v, pltpu.HBM)
             for v in (acts, cotangent, residual, in_count, in_rank)])
 
-    pair = pl.pallas_call(
+    placed = jax.ShapeDtypeStruct(residual.shape, F32)
+    pair, store = pl.pallas_call(
         pair_kernel,
-        in_specs=[smem(), vmem(), vmem()],
-        out_specs=vmem(),
-        out_shape=jax.ShapeDtypeStruct((size, WIDTH), BF),
-        scratch_shapes=[pltpu.VMEM((WIDTH, WIDTH), F32)],
+        in_specs=[smem(), vmem(), vmem(), vmem()],
+        out_specs=[vmem(), hbm()],
+        out_shape=[jax.ShapeDtypeStruct((size, WIDTH), BF), placed],
+        scratch_shapes=[pltpu.VMEM((WIDTH, WIDTH), F32), pltpu.SemaphoreType.DMA],
         compiler_params=params,
         name="pair",
-    )(core, keep, of_both_cores(give))
-    new_residual = new_resid
-    pair = pair.reshape(CHIPS, steps, REGION, WIDTH)
-    arrived = exchange(pair, (1, 2))
+    )(core, keep, of_both_cores(give), new_resid)
+    arrived = exchange(pair.reshape(CHIPS, steps, REGION, WIDTH), (1, 2))
 
     tile = jax.ShapeDtypeStruct((REGION, WIDTH), F32)
-    outgoing, last, kept = pl.pallas_call(
+    outgoing, last, kept, store = pl.pallas_call(
         owner_kernel,
-        in_specs=[vmem(), vmem(), vmem(), vmem()],
-        out_specs=[vmem(), vmem(), vmem()],
-        out_shape=[jax.ShapeDtypeStruct((NX, steps, REGION, WIDTH), BF), tile, tile],
+        in_specs=[vmem(), vmem(), vmem(), vmem(), vmem(), hbm()],
+        out_specs=[vmem(), vmem(), vmem(), hbm()],
+        out_shape=[jax.ShapeDtypeStruct((NX, steps, REGION, WIDTH), BF), tile, tile, placed],
+        scratch_shapes=[pltpu.SemaphoreType.DMA],
+        input_output_aliases={5: 3},
         compiler_params=params,
         name="owner",
-    )(arrived, owner_residual, out_count, out_rank)
+    )(arrived, owner_residual, out_count, out_rank, new_resid, store)
 
     copies = pl.pallas_call(
         update_kernel,
         in_specs=[vmem()],
         out_specs=vmem(),
-        out_shape=pltpu.VMEM((CHIPS, REGION, WIDTH), BF),
+        out_shape=jax.ShapeDtypeStruct((CHIPS, REGION, WIDTH), BF),
         compiler_params=params,
         name="update",
     )(exchange(outgoing, (0,)))
     halves = of_both_cores(exchange(copies, (1, 2)))
-    applied, new_owner = pl.pallas_call(
+    applied, new_owner, new_residual = pl.pallas_call(
         assemble_kernel,
-        in_specs=[vmem(), vmem(), vmem()],
-        out_specs=[vmem(), vmem()],
+        in_specs=[vmem(), vmem(), vmem(), vmem(), hbm()],
+        out_specs=[vmem(), vmem(), hbm()],
         out_shape=[
             jax.ShapeDtypeStruct((rows, cols), BF),
             jax.ShapeDtypeStruct(owner_residual.shape, F32),
+            placed,
         ],
-        scratch_shapes=[
-            pltpu.VMEM((blocks, WIDTH), F32),
-        ],
+        scratch_shapes=[pltpu.VMEM((blocks, WIDTH), F32), pltpu.SemaphoreType.DMA],
+        input_output_aliases={4: 2},
         compiler_params=params,
         name="assemble",
-    )(halves, last, kept)
+    )(halves, last, kept, new_resid, store)
     return applied, new_residual, new_owner
 
 

time: 76.8 us -> 78.1 us (1.017)
  blocking collectives: 51.4 us -> 70.3 us
  waiting for transfers between devices: 11.6 us -> 0 us
  starting transfers between devices: 6.62 us -> 0 us
  Pallas kernels: 5.07 us -> 6.07 us
    all_to_all x2 -> x3, blocking collectives: 36.6 us -> 55.5 us  [exchange(): lax.all_to_all(value, 'd', split_axis=0, concat_axis=0, tiled=True, axis_...]
    all_to_all x1 -> x0, waiting for transfers between devices: 11.6 us -> none  [exchange(): lax.all_to_all(value, 'd', split_axis=0, concat_axis=0, tiled=True, axis_...]
    all_to_all x1 -> x0, starting transfers between devices: 6.62 us -> none  [exchange(): lax.all_to_all(value, 'd', split_axis=0, concat_axis=0, tiled=True, axis_...]
    pallas_call x3, Pallas kernels: 1.34 us -> 3.02 us  [the longest x1 1.6 us: per_device(): pl.pallas_call(assemble_kernel, in_specs=[vmem(), vmem(), vmem(), vmem(),...]
  transfers between devices with their start and end apart: 1 -> 0, of which waited for: 1 -> 0; matrix products, arithmetic and copies ran while one was open for 1% -> 0% of each run, Pallas kernels for 0% -> 0%
where the time goes in v9:
time: 78.1 us; the launch traced here: 77.7 us
  blocking collectives  70.3 us (90%)
  Pallas kernels  6.07 us (8%)
    all_to_all x3, blocking collectives, exchange(): lax.all_to_all(value, 'd', split_axis=0, concat_axis=0, tiled=True, axis_...  55.5 us
    all_gather x2, blocking collectives, of_both_cores(): lax.all_gather(value, 'd', axis=0, axis_index_groups=groups_along((3,)))  14.8 us
    pallas_call x1, Pallas kernels, per_device(): pl.pallas_call(local, in_specs=[smem(), hbm(), hbm(), hbm(), hbm(), hbm()...  3.02 us
    pallas_call x1, Pallas kernels, per_device(): pl.pallas_call(assemble_kernel, in_specs=[vmem(), vmem(), vmem(), vmem(),...  1.6 us

profile of v9, /device:TPU:1, one launch (start us, length us, event | category | flops | bytes accessed | tf_op | source)
XLA Modules:
  0.0 77.7 jit_solution(8517695784871436196)
XLA Ops:
  0.6 3.0 %local.1 = (f32[1,2048,128]{2,1,0:T(8,128)S(1)}, bf16[2048,128]{1,0:T(8,128)(2,1)S(1)}, bf16[2042,128]{1,0:T(8,128)(2,1)S(1)}) custom-call(s32[1]{0:T(128)} %bitcast.args_0_.core_ref, bf16[1,2,512,512]{3,2,1,0:T(8,128)(2,1)} %args_1_.4, bf16[1,2,512,512]{3,2,1,0:T(8,128)(2,1)} %args_2_.4, f32[1,2048,128]{2,1,0:T(8,128)} %args_3_.4, s32[1,2,128]{2,1,0:T(2,128)} %args_4_.4, ...), custom_call_target="tpu_custom_call" | custom-call | tf_op jit(solution)/shard_map/local/pallas_call | solution.py:229
  3.7 9.0 %all-gather.2.both_ref = bf16[2,2042,128]{2,1,0:T(8,128)(2,1)S(1)} all-gather(bf16[1,2042,128]{2,1,0:T(8,128)(2,1)S(1)} %bitcast.5), channel_id=2, replica_groups={{0,1},{2,3},{4,5},{6,7},{8,9},{10,11},{12,13},{14,15},{16,17},{18,19},{..., dimensions={0}, use_global_device_ids=true | all-gather | bytes 1568256 | tf_op jit(solution)/shard_map/all_gather | solution.py:38
  12.7 0.7 pair.1
  13.4 0.0 copy-start
  13.4 28.3 %all_to_all.15.arrived_ref = bf16[64,2,16,128]{3,2,1,0:T(8,128)(2,1)S(1)} all-to-all(bf16[64,2,16,128]{3,2,1,0:T(8,128)(2,1)S(1)} %bitcast.6), channel_id=1, replica_groups={{0,2,4,6,8,10,12,14,16,18,20,22,24,26,28,30,32,34,36,38,40,42,44,46,48,..., dimensions={0} | all-to-all | bytes 1048576 | tf_op jit(solution)/shard_map/all_to_all | solution.py:32
  41.8 0.0 copy-start.1
  41.8 0.0 copy-start.2
  41.8 0.0 copy-done
  41.8 0.7 copy-done.1
  42.5 0.0 copy-done.2
  42.5 0.7 owner.1
  43.2 8.1 %all_to_all.16.arrived_ref = bf16[4,2,16,128]{3,2,1,0:T(8,128)(2,1)S(1)} all-to-all(bf16[4,2,16,128]{3,2,1,0:T(8,128)(2,1)S(1)} %get-tuple-element.20), channel_id=1, replica_groups={{0,128,256,384},{1,129,257,385},{2,130,258,386},{3,131,259,387},{4,132,..., dimensions={0} | all-to-all | bytes 65536 | tf_op jit(solution)/shard_map/all_to_all | solution.py:32
  51.3 19.0 %all_to_all.17 = bf16[64,16,128]{2,1,0:T(8,128)(2,1)S(1)} all-to-all(bf16[64,16,128]{2,1,0:T(8,128)(2,1)S(1)} %update.1), channel_id=1, replica_groups={{0,2,4,6,8,10,12,14,16,18,20,22,24,26,28,30,32,34,36,38,40,42,44,46,48,..., dimensions={0} | all-to-all | bytes 524288 | tf_op jit(solution)/shard_map/all_to_all | solution.py:32
  70.4 5.8 %all-gather.1 = bf16[128,16,128]{2,1,0:T(8,128)(2,1)S(1)} all-gather(bf16[64,16,128]{2,1,0:T(8,128)(2,1)S(1)} %all_to_all.17), channel_id=3, replica_groups={{0,1},{2,3},{4,5},{6,7},{8,9},{10,11},{12,13},{14,15},{16,17},{18,19},{..., dimensions={0}, use_global_device_ids=true | all-gather | bytes 786432 | tf_op jit(solution)/shard_map/all_gather | solution.py:38
  76.1 1.6 %assemble.1 = (bf16[512,512]{1,0:T(8,128)(2,1)}, f32[1,16,128]{2,1,0:T(8,128)}, f32[1,2048,128]{2,1,0:T(8,128)}) custom-call(bf16[2,64,16,128]{3,2,1,0:T(8,128)(2,1)S(1)} %bitcast.4, f32[16,128]{1,0:T(8,128)S(1)} %get-tuple-element.21.last_ref, f32[16,128]{1,0:T(8,128)S(1)} %get-tuple-element.22.kept_ref, ...), custom_call_target="tpu_custom_call", output_to_operand_aliasing={{2}: (4, {})} | custom-call | tf_op jit(solution)/shard_map/assemble/pallas_call | solution.py:288
  (1 shorter events, 0.0 us)
Async XLA Ops:
  13.4 28.3 %copy-start = (f32[1,16,128]{2,1,0:T(8,128)S(1)}, f32[1,16,128]{2,1,0:T(8,128)}, u32[]{:S(2)}) copy-start(f32[1,16,128]{2,1,0:T(8,128)} %oresid_ref.1) | copy-start | bytes 24580
  41.8 0.7 copy-start.1
  41.8 0.7 copy-start.2

commit v10 on v8

--- a/solution.py
+++ b/solution.py
@@ -79,47 +79,61 @@
         chosen_ref[s] = lax.dot_general(chosen.astype(BF), eye, (((0,), (0,)), ((), ())),
                                         preferred_element_type=F32)
 
-    half = 2 * WIDTH
-    for s in range(steps):
+    def multiply(s):
         copies[3 + 2 * s].wait()
         copies[4 + 2 * s].wait()
         left = acts_ref[s]
+        half = 2 * WIDTH
         for h in range(cols // half):
             grad = lax.dot_general(left, cot_ref[s, :, h * half:(h + 1) * half],
                                    (((0,), (0,)), ((), ())), preferred_element_type=F32)
             grad = grad * scale
             for q in range(2):
-                acc_ref[pl.ds(2 * h + q, rows, stride=tiles), :] = grad[:, q * WIDTH:(q + 1) * WIDTH]
-        if s == 0:
-            copies[2].wait()
+                to = pl.ds(2 * h + q, rows, stride=tiles)
+                acc_ref[s, to, :] = grad[:, q * WIDTH:(q + 1) * WIDTH]
+
+    def select(s, me):
         columns = chosen_ref[s]
-        for me in range(NC):
-            @pl.when(core == me)
-            def _(me=me, s=s, columns=columns):
-                for r in range(groups):
-                    span = slice(r * WIDTH, (r + 1) * WIDTH)
-                    total = resid_ref[0, span, :] + acc_ref[span, :]
-                    mask = jnp.broadcast_to(columns[:, r:r + 1], (WIDTH, WIDTH)) > 0.5
-                    resid_ref[0, span, :] = jnp.where(mask, 0.0, total)
-                    sent = jnp.where(mask, total, 0.0).astype(BF)
-                    for i in range(WIDTH // REGION):
-                        owner = r * (WIDTH // REGION) + i
-                        at = ((owner // NC) * steps + s) * REGION
-                        tile = sent[i * REGION:(i + 1) * REGION, :]
-                        if owner % NC == me:
-                            keep_ref[at:at + REGION, :] = tile
-                        elif at < WHOLE:
-                            give_ref[at:at + REGION, :] = tile
-                        else:
-                            slots = last_ref[r:r + 1, :]
-                            wide = jnp.broadcast_to(slots, (REGION, WIDTH))
-                            slot = lax.broadcasted_iota(jnp.int32, (REGION, WIDTH), 0).astype(F32)
-                            lane = lax.broadcasted_iota(jnp.int32, (REGION, WIDTH), 1)
-                            pick = jnp.where((wide == slot) & (lane // REGION == i), 1.0, 0.0)
-                            packed = jnp.dot(pick.astype(BF), sent, preferred_element_type=F32)
-                            pack_ref[0:CAP, :] = packed[0:CAP, :]
-                            pack_ref[CAP:2 * CAP, :] = jnp.broadcast_to(slots, (CAP, WIDTH))
-                            give_ref[at:at + CAP + 2, :] = pack_ref[0:CAP + 2, :].astype(BF)
+        for r in range(groups):
+            span = slice(r * WIDTH, (r + 1) * WIDTH)
+            total = resid_ref[0, span, :] + acc_ref[s, span, :]
+            mask = jnp.broadcast_to(columns[:, r:r + 1], (WIDTH, WIDTH)) > 0.5
+            resid_ref[0, span, :] = jnp.where(mask, 0.0, total)
+            sent = jnp.where(mask, total, 0.0).astype(BF)
+            for i in range(WIDTH // REGION):
+                owner = r * (WIDTH // REGION) + i
+                at = ((owner // NC) * steps + s) * REGION
+                tile = sent[i * REGION:(i + 1) * REGION, :]
+                if owner % NC == me:
+                    keep_ref[at:at + REGION, :] = tile
+                elif at < WHOLE:
+                    give_ref[at:at + REGION, :] = tile
+                else:
+                    slots = last_ref[r:r + 1, :]
+                    wide = jnp.broadcast_to(slots, (REGION, WIDTH))
+                    slot = lax.broadcasted_iota(jnp.int32, (REGION, WIDTH), 0).astype(F32)
+                    lane = lax.broadcasted_iota(jnp.int32, (REGION, WIDTH), 1)
+                    pick = jnp.where((wide == slot) & (lane // REGION == i), 1.0, 0.0)
+                    packed = jnp.dot(pick.astype(BF), sent, preferred_element_type=F32)
+                    pack_ref[0:CAP, :] = packed[0:CAP, :]
+                    pack_ref[CAP:2 * CAP, :] = jnp.broadcast_to(slots, (CAP, WIDTH))
+                    give_ref[at:at + CAP + 2, :] = pack_ref[0:CAP + 2, :].astype(BF)
+
+    multiply(0)
+    copies[2].wait()
+    for me in range(NC):
+        @pl.when(core == me)
+        def _(me=me):
+            select(0, me)
+            for s in range(1, steps):
+                multiply(s)
+                select(s, me)
+
+
+def store_kernel(after_ref, value_ref, out_hbm, sem):
+    copy = pltpu.make_async_copy(value_ref, out_hbm, sem)
+    copy.start()
+    copy.wait()
 
 
 def pair_kernel(core_ref, keep_ref, both_ref, out_ref, tile_ref):
@@ -222,7 +236,7 @@
         scratch_shapes=[
             pltpu.VMEM((steps, tokens, rows), BF),
             pltpu.VMEM((steps, tokens, cols), BF),
-            pltpu.VMEM((blocks, WIDTH), F32),
+            pltpu.VMEM((steps, blocks, WIDTH), F32),
             pltpu.VMEM(in_count.shape, jnp.int32),
             pltpu.VMEM(in_rank.shape, jnp.int32),
             pltpu.VMEM((steps, blocks // WIDTH, WIDTH), jnp.int32),
@@ -245,7 +259,6 @@
         compiler_params=params,
         name="pair",
     )(core, keep, of_both_cores(give))
-    new_residual = new_resid
     pair = pair.reshape(CHIPS, steps, REGION, WIDTH)
     arrived = exchange(pair, (1, 2))
 
@@ -259,14 +272,24 @@
         name="owner",
     )(arrived, owner_residual, out_count, out_rank)
 
+    new_residual = pl.pallas_call(
+        store_kernel,
+        in_specs=[pl.BlockSpec(memory_space=pl.ANY), vmem()],
+        out_specs=hbm(),
+        out_shape=jax.ShapeDtypeStruct(residual.shape, F32),
+        scratch_shapes=[pltpu.SemaphoreType.DMA],
+        compiler_params=params,
+        name="store",
+    )(last, new_resid)
     copies = pl.pallas_call(
         update_kernel,
         in_specs=[vmem()],
         out_specs=vmem(),
-        out_shape=pltpu.VMEM((CHIPS, REGION, WIDTH), BF),
+        out_shape=jax.ShapeDtypeStruct((CHIPS, REGION, WIDTH), BF),
         compiler_params=params,
         name="update",
     )(exchange(outgoing, (0,)))
+    copies, new_residual = lax.optimization_barrier((copies, new_residual))
     halves = of_both_cores(exchange(copies, (1, 2)))
     applied, new_owner = pl.pallas_call(
         assemble_kernel,

time: 76.8 us -> 76.6 us (level)
  blocking collectives: 51.4 us -> 62.3 us
  waiting for transfers between devices: 11.6 us -> 3.32 us
  starting transfers between devices: 6.62 us -> 4.02 us
  local copies, waits for them, and re-layouts: 0.99 us -> 0.02 us
  Pallas kernels: 5.07 us -> 5.85 us
    all_to_all x2, blocking collectives: 36.6 us -> 47.5 us  [exchange(): lax.all_to_all(value, 'd', split_axis=0, concat_axis=0, tiled=True, axis_...]
    all_to_all x1, waiting for transfers between devices: 11.6 us -> 3.32 us  [exchange(): lax.all_to_all(value, 'd', split_axis=0, concat_axis=0, tiled=True, axis_...]
    all_to_all x1, starting transfers between devices: 6.62 us -> 4.02 us  [exchange(): lax.all_to_all(value, 'd', split_axis=0, concat_axis=0, tiled=True, axis_...]
    pallas_call x0 -> x1, Pallas kernels: none -> 0.98 us  [per_device(): pl.pallas_call(store_kernel, in_specs=[pl.BlockSpec(memory_space=pl.ANY),...]
    unnamed x7 -> x6, local copies, waits for them, and re-layouts: 0.99 us -> 0.02 us
  transfers between devices with their start and end apart: 1 -> 1, of which waited for: 1 -> 1; matrix products, arithmetic and copies ran while one was open for 1% -> 0% of each run, Pallas kernels for 0% -> 1%
where the time goes in v10:
time: 76.6 us; the launch traced here: 76.2 us
  blocking collectives  62.3 us (81%)
  Pallas kernels  5.85 us (8%)
  starting transfers between devices  4.02 us (5%)
  waiting for transfers between devices  3.32 us (4%)
    all_to_all x2, blocking collectives, exchange(): lax.all_to_all(value, 'd', split_axis=0, concat_axis=0, tiled=True, axis_...  47.5 us
    all_gather x2, blocking collectives, of_both_cores(): lax.all_gather(value, 'd', axis=0, axis_index_groups=groups_along((3,)))  14.8 us
    all_to_all x1, starting transfers between devices, exchange(): lax.all_to_all(value, 'd', split_axis=0, concat_axis=0, tiled=True, axis_...  4.02 us
    all_to_all x1, waiting for transfers between devices, exchange(): lax.all_to_all(value, 'd', split_axis=0, concat_axis=0, tiled=True, axis_...  3.32 us
    pallas_call x1, Pallas kernels, per_device(): pl.pallas_call(local, in_specs=[smem(), hbm(), hbm(), hbm(), hbm(), hbm()...  2.88 us
  transfers between devices with their start and end apart: 1, of which 1 were waited for; matrix products, arithmetic and copies ran while one was open for 0% of the time, Pallas kernels for 1%

profile of v10, /device:TPU:1, one launch (start us, length us, event | category | flops | bytes accessed | tf_op | source)
XLA Modules:
  0.0 76.2 jit_solution(9558350537718010253)
XLA Ops:
  0.6 2.9 %local.1 = (f32[1,2048,128]{2,1,0:T(8,128)S(1)}, bf16[2048,128]{1,0:T(8,128)(2,1)S(1)}, bf16[2042,128]{1,0:T(8,128)(2,1)S(1)}) custom-call(s32[1]{0:T(128)} %bitcast.args_0_.core_ref, bf16[1,2,512,512]{3,2,1,0:T(8,128)(2,1)} %args_1_.4, bf16[1,2,512,512]{3,2,1,0:T(8,128)(2,1)} %args_2_.4, f32[1,2048,128]{2,1,0:T(8,128)} %args_3_.4, s32[1,2,128]{2,1,0:T(2,128)} %args_4_.4, ...), custom_call_target="tpu_custom_call" | custom-call | tf_op jit(solution)/shard_map/local/pallas_call | solution.py:227
  3.5 9.1 %all-gather.2.both_ref = bf16[2,2042,128]{2,1,0:T(8,128)(2,1)S(1)} all-gather(bf16[1,2042,128]{2,1,0:T(8,128)(2,1)S(1)} %bitcast.6), channel_id=2, replica_groups={{0,1},{2,3},{4,5},{6,7},{8,9},{10,11},{12,13},{14,15},{16,17},{18,19},{..., dimensions={0}, use_global_device_ids=true | all-gather | bytes 1568256 | tf_op jit(solution)/shard_map/all_gather | solution.py:38
  12.6 0.2 pair.1
  12.8 0.0 copy-start
  12.8 0.0 copy-start.1
  12.9 0.0 copy-start.2
  12.9 28.5 %all_to_all.15.arrived_ref = bf16[64,2,16,128]{3,2,1,0:T(8,128)(2,1)S(1)} all-to-all(bf16[64,2,16,128]{3,2,1,0:T(8,128)(2,1)S(1)} %bitcast.4), channel_id=1, replica_groups={{0,2,4,6,8,10,12,14,16,18,20,22,24,26,28,30,32,34,36,38,40,42,44,46,48,..., dimensions={0} | all-to-all | bytes 1048576 | tf_op jit(solution)/shard_map/all_to_all | solution.py:32
  41.3 0.0 copy-done
  41.3 0.0 copy-done.1
  41.3 0.0 copy-done.2
  41.3 0.8 %owner.1 = (bf16[4,2,16,128]{3,2,1,0:T(8,128)(2,1)}, f32[16,128]{1,0:T(8,128)S(1)}, f32[16,128]{1,0:T(8,128)S(1)}) custom-call(bf16[64,2,16,128]{3,2,1,0:T(8,128)(2,1)S(1)} %all_to_all.15.arrived_ref, f32[1,16,128]{2,1,0:T(8,128)S(1)} %copy-done, s32[1,2]{1,0:T(1,128)S(1)} %copy-done.2, s32[1,2,16]{2,1,0:T(2,128)S(1)} %copy-done.1), custom_call_target="tpu_custom_call" | custom-call | tf_op jit(solution)/shard_map/owner/pallas_call | solution.py:266
  42.1 4.0 %all-to-all-start.1 = ((bf16[4,2,16,128]{3,2,1,0:T(8,128)(2,1)}), bf16[4,2,16,128]{3,2,1,0:T(8,128)(2,1)S(1)}, u32[]{:S(2)}, u32[]{:S(2)}) async-start(bf16[4,2,16,128]{3,2,1,0:T(8,128)(2,1)} %get-tuple-element.15), calls=%async_computation.1 | async-start | bytes 65536 | tf_op jit(solution)/shard_map/all_to_all | solution.py:32
  46.1 1.0 %store.1 = f32[1,2048,128]{2,1,0:T(8,128)} custom-call(f32[16,128]{1,0:T(8,128)S(1)} %get-tuple-element.16.after_ref.last_ref, f32[1,2048,128]{2,1,0:T(8,128)S(1)} %get-tuple-element.17.value_ref), custom_call_target="tpu_custom_call" | custom-call | tf_op jit(solution)/shard_map/store/pallas_call | solution.py:275
  47.1 3.3 %all-to-all-done.1.arrived_ref = bf16[4,2,16,128]{3,2,1,0:T(8,128)(2,1)S(1)} async-done(((bf16[4,2,16,128]{3,2,1,0:T(8,128)(2,1)}), bf16[4,2,16,128]{3,2,1,0:T(8,128)(2,1)S(1)}, u32[]{:S(2)}, u32[]{:S(2)}) %all-to-all-start.1) | async-done | bytes 32800 | tf_op jit(solution)/shard_map/all_to_all | solution.py:32
  50.5 19.0 %all_to_all.16 = bf16[64,16,128]{2,1,0:T(8,128)(2,1)S(1)} all-to-all(bf16[64,16,128]{2,1,0:T(8,128)(2,1)S(1)} %update.1), channel_id=1, replica_groups={{0,2,4,6,8,10,12,14,16,18,20,22,24,26,28,30,32,34,36,38,40,42,44,46,48,..., dimensions={0} | all-to-all | bytes 524288 | tf_op jit(solution)/shard_map/all_to_all | solution.py:32
  69.5 5.8 %all-gather.1 = bf16[128,16,128]{2,1,0:T(8,128)(2,1)S(1)} all-gather(bf16[64,16,128]{2,1,0:T(8,128)(2,1)S(1)} %all_to_all.16), channel_id=3, replica_groups={{0,1},{2,3},{4,5},{6,7},{8,9},{10,11},{12,13},{14,15},{16,17},{18,19},{..., dimensions={0}, use_global_device_ids=true | all-gather | bytes 786432 | tf_op jit(solution)/shard_map/all_gather | solution.py:38
  75.3 1.0 %assemble.1 = (bf16[512,512]{1,0:T(8,128)(2,1)}, f32[1,16,128]{2,1,0:T(8,128)}) custom-call(bf16[2,64,16,128]{3,2,1,0:T(8,128)(2,1)S(1)} %bitcast.5, f32[16,128]{1,0:T(8,128)S(1)} %get-tuple-element.16.after_ref.last_ref, f32[16,128]{1,0:T(8,128)S(1)} %get-tuple-element.19.kept_ref), custom_call_target="tpu_custom_call" | custom-call | tf_op jit(solution)/shard_map/assemble/pallas_call | solution.py:294
  (1 shorter events, 0.0 us)
Async XLA Ops:
  12.8 28.5 %copy-start = (f32[1,16,128]{2,1,0:T(8,128)S(1)}, f32[1,16,128]{2,1,0:T(8,128)}, u32[]{:S(2)}) copy-start(f32[1,16,128]{2,1,0:T(8,128)} %oresid_ref.1) | copy-start | bytes 24580
  12.8 28.5 %copy-start.1 = (s32[1,2,16]{2,1,0:T(2,128)S(1)}, s32[1,2,16]{2,1,0:T(2,128)}, u32[]{:S(2)}) copy-start(s32[1,2,16]{2,1,0:T(2,128)} %rank_ref.1) | copy-start | bytes 388
  12.9 28.5 %copy-start.2 = (s32[1,2]{1,0:T(1,128)S(1)}, s32[1,2]{1,0:T(1,128)}, u32[]{:S(2)}) copy-start(s32[1,2]{1,0:T(1,128)} %count_ref.1) | copy-start | bytes 28
  42.1 8.3 %all-to-all-start.1 = ((bf16[4,2,16,128]{3,2,1,0:T(8,128)(2,1)}), bf16[4,2,16,128]{3,2,1,0:T(8,128)(2,1)S(1)}, u32[]{:S(2)}, u32[]{:S(2)}) async-start(bf16[4,2,16,128]{3,2,1,0:T(8,128)(2,1)} %get-tuple-element.15), calls=%async_computation.1 | async-start | bytes 65536 | tf_op jit(solution)/shard_map/all_to_all | solution.py:32

commit v11 on v10

--- a/solution.py
+++ b/solution.py
@@ -28,9 +28,19 @@
     return np.moveaxis(ids, axes, range(4 - len(axes), 4)).reshape(-1, size).tolist()
 
 
-def exchange(value, axes):
+def place_of(core, z, y):
+    return z * NY + y if core == 0 else y * NZ + z
+
+
+def chips_in_place():
+    ids = np.arange(NX * NZ * NY * NC).reshape(NX, NZ, NY, NC)
+    first, second = ids[..., 0], ids[..., 1].swapaxes(1, 2)
+    return first.reshape(NX, -1).tolist() + second.reshape(NX, -1).tolist()
+
+
+def exchange(value, groups):
     return lax.all_to_all(
-        value, "d", split_axis=0, concat_axis=0, tiled=True, axis_index_groups=groups_along(axes)
+        value, "d", split_axis=0, concat_axis=0, tiled=True, axis_index_groups=groups
     )
 
 
@@ -102,7 +112,8 @@
             sent = jnp.where(mask, total, 0.0).astype(BF)
             for i in range(WIDTH // REGION):
                 owner = r * (WIDTH // REGION) + i
-                at = ((owner // NC) * steps + s) * REGION
+                z, y, c = owner // (NY * NC), (owner // NC) % NY, owner % NC
+                at = (place_of(c, z, y) * steps + s) * REGION
                 tile = sent[i * REGION:(i + 1) * REGION, :]
                 if owner % NC == me:
                     keep_ref[at:at + REGION, :] = tile
@@ -260,7 +271,7 @@
         name="pair",
     )(core, keep, of_both_cores(give))
     pair = pair.reshape(CHIPS, steps, REGION, WIDTH)
-    arrived = exchange(pair, (1, 2))
+    arrived = exchange(pair, chips_in_place())
 
     tile = jax.ShapeDtypeStruct((REGION, WIDTH), F32)
     outgoing, last, kept = pl.pallas_call(
@@ -288,9 +299,9 @@
         out_shape=jax.ShapeDtypeStruct((CHIPS, REGION, WIDTH), BF),
         compiler_params=params,
         name="update",
-    )(exchange(outgoing, (0,)))
+    )(exchange(outgoing, groups_along((0,))))
     copies, new_residual = lax.optimization_barrier((copies, new_residual))
-    halves = of_both_cores(exchange(copies, (1, 2)))
+    halves = of_both_cores(exchange(copies, groups_along((1, 2))))
     applied, new_owner = pl.pallas_call(
         assemble_kernel,
         in_specs=[vmem(), vmem(), vmem()],

time: 76.6 us -> 76.5 us (level)
  no operation moved by 1% of the time
where the time goes in v11:
time: 76.5 us; the launch traced here: 76.1 us
  blocking collectives  62.2 us (81%)
  Pallas kernels  5.85 us (8%)
  starting transfers between devices  4.02 us (5%)
  waiting for transfers between devices  3.32 us (4%)
    all_to_all x2, blocking collectives, exchange(): lax.all_to_all(value, 'd', split_axis=0, concat_axis=0, tiled=True, axis_...  47.5 us
    all_gather x2, blocking collectives, of_both_cores(): lax.all_gather(value, 'd', axis=0, axis_index_groups=groups_along((3,)))  14.7 us
    all_to_all x1, starting transfers between devices, exchange(): lax.all_to_all(value, 'd', split_axis=0, concat_axis=0, tiled=True, axis_...  4.02 us
    all_to_all x1, waiting for transfers between devices, exchange(): lax.all_to_all(value, 'd', split_axis=0, concat_axis=0, tiled=True, axis_...  3.32 us
    pallas_call x1, Pallas kernels, per_device(): pl.pallas_call(local, in_specs=[smem(), hbm(), hbm(), hbm(), hbm(), hbm()...  2.89 us
  transfers between devices with their start and end apart: 1, of which 1 were waited for; matrix products, arithmetic and copies ran while one was open for 0% of the time, Pallas kernels for 1%

profile of v11, /device:TPU:1, one launch (start us, length us, event | category | flops | bytes accessed | tf_op | source)
XLA Modules:
  0.0 76.1 jit_solution(16502705875587175543)
XLA Ops:
  0.6 2.9 %local.1 = (f32[1,2048,128]{2,1,0:T(8,128)S(1)}, bf16[2048,128]{1,0:T(8,128)(2,1)S(1)}, bf16[2042,128]{1,0:T(8,128)(2,1)S(1)}) custom-call(s32[1]{0:T(128)} %bitcast.args_0_.core_ref, bf16[1,2,512,512]{3,2,1,0:T(8,128)(2,1)} %args_1_.4, bf16[1,2,512,512]{3,2,1,0:T(8,128)(2,1)} %args_2_.4, f32[1,2048,128]{2,1,0:T(8,128)} %args_3_.4, s32[1,2,128]{2,1,0:T(2,128)} %args_4_.4, ...), custom_call_target="tpu_custom_call" | custom-call | tf_op jit(solution)/shard_map/local/pallas_call | solution.py:238
  3.5 9.1 %all-gather.2.both_ref = bf16[2,2042,128]{2,1,0:T(8,128)(2,1)S(1)} all-gather(bf16[1,2042,128]{2,1,0:T(8,128)(2,1)S(1)} %bitcast.6), channel_id=2, replica_groups={{0,1},{2,3},{4,5},{6,7},{8,9},{10,11},{12,13},{14,15},{16,17},{18,19},{..., dimensions={0}, use_global_device_ids=true | all-gather | bytes 1568256 | tf_op jit(solution)/shard_map/all_gather | solution.py:48
  12.6 0.2 pair.1
  12.8 0.0 copy-start
  12.8 0.0 copy-start.1
  12.9 0.0 copy-start.2
  12.9 27.9 %all_to_all.15.arrived_ref = bf16[64,2,16,128]{3,2,1,0:T(8,128)(2,1)S(1)} all-to-all(bf16[64,2,16,128]{3,2,1,0:T(8,128)(2,1)S(1)} %bitcast.4), channel_id=1, replica_groups={{0,2,4,6,8,10,12,14,16,18,20,22,24,26,28,30,32,34,36,38,40,42,44,46,48,..., dimensions={0} | all-to-all | bytes 1048576 | tf_op jit(solution)/shard_map/all_to_all | solution.py:42
  40.8 0.0 copy-done
  40.8 0.0 copy-done.1
  40.8 0.0 copy-done.2
  40.8 0.8 %owner.1 = (bf16[4,2,16,128]{3,2,1,0:T(8,128)(2,1)}, f32[16,128]{1,0:T(8,128)S(1)}, f32[16,128]{1,0:T(8,128)S(1)}) custom-call(bf16[64,2,16,128]{3,2,1,0:T(8,128)(2,1)S(1)} %all_to_all.15.arrived_ref, f32[1,16,128]{2,1,0:T(8,128)S(1)} %copy-done, s32[1,2]{1,0:T(1,128)S(1)} %copy-done.2, s32[1,2,16]{2,1,0:T(2,128)S(1)} %copy-done.1), custom_call_target="tpu_custom_call" | custom-call | tf_op jit(solution)/shard_map/owner/pallas_call | solution.py:277
  41.6 4.0 %all-to-all-start.1 = ((bf16[4,2,16,128]{3,2,1,0:T(8,128)(2,1)}), bf16[4,2,16,128]{3,2,1,0:T(8,128)(2,1)S(1)}, u32[]{:S(2)}, u32[]{:S(2)}) async-start(bf16[4,2,16,128]{3,2,1,0:T(8,128)(2,1)} %get-tuple-element.15), calls=%async_computation.1 | async-start | bytes 65536 | tf_op jit(solution)/shard_map/all_to_all | solution.py:42
  45.6 1.0 %store.1 = f32[1,2048,128]{2,1,0:T(8,128)} custom-call(f32[16,128]{1,0:T(8,128)S(1)} %get-tuple-element.16.after_ref.last_ref, f32[1,2048,128]{2,1,0:T(8,128)S(1)} %get-tuple-element.17.value_ref), custom_call_target="tpu_custom_call" | custom-call | tf_op jit(solution)/shard_map/store/pallas_call | solution.py:286
  46.6 3.3 %all-to-all-done.1.arrived_ref = bf16[4,2,16,128]{3,2,1,0:T(8,128)(2,1)S(1)} async-done(((bf16[4,2,16,128]{3,2,1,0:T(8,128)(2,1)}), bf16[4,2,16,128]{3,2,1,0:T(8,128)(2,1)S(1)}, u32[]{:S(2)}, u32[]{:S(2)}) %all-to-all-start.1) | async-done | bytes 32800 | tf_op jit(solution)/shard_map/all_to_all | solution.py:42
  49.9 19.6 %all_to_all.16 = bf16[64,16,128]{2,1,0:T(8,128)(2,1)S(1)} all-to-all(bf16[64,16,128]{2,1,0:T(8,128)(2,1)S(1)} %update.1), channel_id=1, replica_groups={{0,2,4,6,8,10,12,14,16,18,20,22,24,26,28,30,32,34,36,38,40,42,44,46,48,..., dimensions={0} | all-to-all | bytes 524288 | tf_op jit(solution)/shard_map/all_to_all | solution.py:42
  69.5 5.6 %all-gather.1 = bf16[128,16,128]{2,1,0:T(8,128)(2,1)S(1)} all-gather(bf16[64,16,128]{2,1,0:T(8,128)(2,1)S(1)} %all_to_all.16), channel_id=3, replica_groups={{0,1},{2,3},{4,5},{6,7},{8,9},{10,11},{12,13},{14,15},{16,17},{18,19},{..., dimensions={0}, use_global_device_ids=true | all-gather | bytes 786432 | tf_op jit(solution)/shard_map/all_gather | solution.py:48
  75.1 1.0 %assemble.1 = (bf16[512,512]{1,0:T(8,128)(2,1)}, f32[1,16,128]{2,1,0:T(8,128)}) custom-call(bf16[2,64,16,128]{3,2,1,0:T(8,128)(2,1)S(1)} %bitcast.5, f32[16,128]{1,0:T(8,128)S(1)} %get-tuple-element.16.after_ref.last_ref, f32[16,128]{1,0:T(8,128)S(1)} %get-tuple-element.19.kept_ref), custom_call_target="tpu_custom_call" | custom-call | tf_op jit(solution)/shard_map/assemble/pallas_call | solution.py:305
  (1 shorter events, 0.0 us)
Async XLA Ops:
  12.8 27.9 %copy-start = (f32[1,16,128]{2,1,0:T(8,128)S(1)}, f32[1,16,128]{2,1,0:T(8,128)}, u32[]{:S(2)}) copy-start(f32[1,16,128]{2,1,0:T(8,128)} %oresid_ref.1) | copy-start | bytes 24580
  12.8 27.9 %copy-start.1 = (s32[1,2,16]{2,1,0:T(2,128)S(1)}, s32[1,2,16]{2,1,0:T(2,128)}, u32[]{:S(2)}) copy-start(s32[1,2,16]{2,1,0:T(2,128)} %rank_ref.1) | copy-start | bytes 388
  12.9 27.9 %copy-start.2 = (s32[1,2]{1,0:T(1,128)S(1)}, s32[1,2]{1,0:T(1,128)}, u32[]{:S(2)}) copy-start(s32[1,2]{1,0:T(1,128)} %count_ref.1) | copy-start | bytes 28
  41.6 8.3 %all-to-all-start.1 = ((bf16[4,2,16,128]{3,2,1,0:T(8,128)(2,1)}), bf16[4,2,16,128]{3,2,1,0:T(8,128)(2,1)S(1)}, u32[]{:S(2)}, u32[]{:S(2)}) async-start(bf16[4,2,16,128]{3,2,1,0:T(8,128)(2,1)} %get-tuple-element.15), calls=%async_computation.1 | async-start | bytes 65536 | tf_op jit(solution)/shard_map/all_to_all | solution.py:42

commit v12 on v10

--- a/solution.py
+++ b/solution.py
@@ -130,13 +130,19 @@
                 select(s, me)
 
 
-def store_kernel(after_ref, value_ref, out_hbm, sem):
-    copy = pltpu.make_async_copy(value_ref, out_hbm, sem)
-    copy.start()
-    copy.wait()
-
-
-def pair_kernel(core_ref, keep_ref, both_ref, out_ref, tile_ref):
+def stored_by(me, core_ref, resid_ref, store_hbm, sem):
+    @pl.when(core_ref[0] == me)
+    def _():
+        copy = pltpu.make_async_copy(resid_ref, store_hbm, sem)
+        copy.start()
+        copy.wait()
+
+
+def late_kernel(core_ref, after_ref, resid_ref, begun_hbm, store_hbm, sem):
+    stored_by(1, core_ref, resid_ref, store_hbm, sem)
+
+
+def pair_kernel(core_ref, keep_ref, both_ref, resid_ref, out_ref, store_hbm, tile_ref, sem):
     core = core_ref[0]
     other = 1 - core
     chunk = 8 * REGION
@@ -153,6 +159,7 @@
     at = pl.multiple_of(WIDTH - NC * REGION + core * REGION, REGION)
     total = keep_ref[WHOLE:WHOLE + REGION, :].astype(F32) + tile_ref[pl.ds(at, REGION), :]
     out_ref[WHOLE:WHOLE + REGION, :] = total.astype(BF)
+    stored_by(0, core_ref, resid_ref, store_hbm, sem)
 
 
 def owner_kernel(arrived_ref, oresid_ref, count_ref, rank_ref, out_ref, last_ref, kept_ref):
@@ -250,15 +257,16 @@
     )(core, *[pltpu.with_memory_space_constraint(v, pltpu.HBM)
             for v in (acts, cotangent, residual, in_count, in_rank)])
 
-    pair = pl.pallas_call(
+    placed = jax.ShapeDtypeStruct(residual.shape, F32)
+    pair, store = pl.pallas_call(
         pair_kernel,
-        in_specs=[smem(), vmem(), vmem()],
-        out_specs=vmem(),
-        out_shape=jax.ShapeDtypeStruct((size, WIDTH), BF),
-        scratch_shapes=[pltpu.VMEM((WIDTH, WIDTH), F32)],
+        in_specs=[smem(), vmem(), vmem(), vmem()],
+        out_specs=[vmem(), hbm()],
+        out_shape=[jax.ShapeDtypeStruct((size, WIDTH), BF), placed],
+        scratch_shapes=[pltpu.VMEM((WIDTH, WIDTH), F32), pltpu.SemaphoreType.DMA],
         compiler_params=params,
         name="pair",
-    )(core, keep, of_both_cores(give))
+    )(core, keep, of_both_cores(give), new_resid)
     pair = pair.reshape(CHIPS, steps, REGION, WIDTH)
     arrived = exchange(pair, (1, 2))
 
@@ -272,15 +280,6 @@
         name="owner",
     )(arrived, owner_residual, out_count, out_rank)
 
-    new_residual = pl.pallas_call(
-        store_kernel,
-        in_specs=[pl.BlockSpec(memory_space=pl.ANY), vmem()],
-        out_specs=hbm(),
-        out_shape=jax.ShapeDtypeStruct(residual.shape, F32),
-        scratch_shapes=[pltpu.SemaphoreType.DMA],
-        compiler_params=params,
-        name="store",
-    )(last, new_resid)
     copies = pl.pallas_call(
         update_kernel,
         in_specs=[vmem()],
@@ -289,8 +288,19 @@
         compiler_params=params,
         name="update",
     )(exchange(outgoing, (0,)))
-    copies, new_residual = lax.optimization_barrier((copies, new_residual))
-    halves = of_both_cores(exchange(copies, (1, 2)))
+    own = exchange(copies, (1, 2))
+    new_residual = pl.pallas_call(
+        late_kernel,
+        in_specs=[smem(), pl.BlockSpec(memory_space=pl.ANY), vmem(), hbm()],
+        out_specs=hbm(),
+        out_shape=placed,
+        scratch_shapes=[pltpu.SemaphoreType.DMA],
+        input_output_aliases={3: 0},
+        compiler_params=params,
+        name="late",
+    )(core, own, new_resid, store)
+    own, new_residual = lax.optimization_barrier((own, new_residual))
+    halves = of_both_cores(own)
     applied, new_owner = pl.pallas_call(
         assemble_kernel,
         in_specs=[vmem(), vmem(), vmem()],

time: 76.6 us -> 75.7 us (0.988)
  blocking collectives: 62.3 us -> 69.4 us
  starting transfers between devices: 4.02 us -> 0 us
  waiting for transfers between devices: 3.32 us -> 0 us
    all_to_all x2 -> x3, blocking collectives: 47.5 us -> 55 us  [exchange(): lax.all_to_all(value, 'd', split_axis=0, concat_axis=0, tiled=True, axis_...]
    all_to_all x1 -> x0, starting transfers between devices: 4.02 us -> none  [exchange(): lax.all_to_all(value, 'd', split_axis=0, concat_axis=0, tiled=True, axis_...]
    all_to_all x1 -> x0, waiting for transfers between devices: 3.32 us -> none  [exchange(): lax.all_to_all(value, 'd', split_axis=0, concat_axis=0, tiled=True, axis_...]
  transfers between devices with their start and end apart: 1 -> 0, of which waited for: 1 -> 0; matrix products, arithmetic and copies ran while one was open for 0% -> 0% of each run, Pallas kernels for 1% -> 0%
where the time goes in v12:
time: 75.7 us; the launch traced here: 75.4 us
  blocking collectives  69.4 us (92%)
  Pallas kernels  5.29 us (7%)
    all_to_all x3, blocking collectives, exchange(): lax.all_to_all(value, 'd', split_axis=0, concat_axis=0, tiled=True, axis_...  55 us
    all_gather x2, blocking collectives, of_both_cores(): lax.all_gather(value, 'd', axis=0, axis_index_groups=groups_along((3,)))  14.4 us
    pallas_call x1, Pallas kernels, per_device(): pl.pallas_call(local, in_specs=[smem(), hbm(), hbm(), hbm(), hbm(), hbm()...  2.92 us

profile of v12, /device:TPU:1, one launch (start us, length us, event | category | flops | bytes accessed | tf_op | source)
XLA Modules:
  0.0 75.4 jit_solution(15578867945393951653)
XLA Ops:
  0.6 2.9 %local.1 = (f32[1,2048,128]{2,1,0:T(8,128)S(1)}, bf16[2048,128]{1,0:T(8,128)(2,1)S(1)}, bf16[2042,128]{1,0:T(8,128)(2,1)S(1)}) custom-call(s32[1]{0:T(128)} %bitcast.args_0_.core_ref, bf16[1,2,512,512]{3,2,1,0:T(8,128)(2,1)} %args_1_.4, bf16[1,2,512,512]{3,2,1,0:T(8,128)(2,1)} %args_2_.4, f32[1,2048,128]{2,1,0:T(8,128)} %args_3_.4, s32[1,2,128]{2,1,0:T(2,128)} %args_4_.4, ...), custom_call_target="tpu_custom_call" | custom-call | tf_op jit(solution)/shard_map/local/pallas_call | solution.py:234
  3.6 9.1 %all-gather.2.both_ref = bf16[2,2042,128]{2,1,0:T(8,128)(2,1)S(1)} all-gather(bf16[1,2042,128]{2,1,0:T(8,128)(2,1)S(1)} %bitcast.5), channel_id=2, replica_groups={{0,1},{2,3},{4,5},{6,7},{8,9},{10,11},{12,13},{14,15},{16,17},{18,19},{..., dimensions={0}, use_global_device_ids=true | all-gather | bytes 1568256 | tf_op jit(solution)/shard_map/all_gather | solution.py:38
  12.6 0.2 pair.1
  12.9 0.0 copy-start
  12.9 0.0 copy-start.1
  12.9 0.0 copy-start.2
  12.9 27.5 %all_to_all.15.arrived_ref = bf16[64,2,16,128]{3,2,1,0:T(8,128)(2,1)S(1)} all-to-all(bf16[64,2,16,128]{3,2,1,0:T(8,128)(2,1)S(1)} %bitcast.6), channel_id=1, replica_groups={{0,2,4,6,8,10,12,14,16,18,20,22,24,26,28,30,32,34,36,38,40,42,44,46,48,..., dimensions={0} | all-to-all | bytes 1048576 | tf_op jit(solution)/shard_map/all_to_all | solution.py:32
  40.4 0.0 copy-done
  40.4 0.0 copy-done.1
  40.4 0.0 copy-done.2
  40.4 0.2 owner.1
  40.6 8.1 %all_to_all.16.arrived_ref = bf16[4,2,16,128]{3,2,1,0:T(8,128)(2,1)S(1)} all-to-all(bf16[4,2,16,128]{3,2,1,0:T(8,128)(2,1)S(1)} %get-tuple-element.19), channel_id=1, replica_groups={{0,128,256,384},{1,129,257,385},{2,130,258,386},{3,131,259,387},{4,132,..., dimensions={0} | all-to-all | bytes 65536 | tf_op jit(solution)/shard_map/all_to_all | solution.py:32
  48.7 19.4 %all_to_all.17.after_ref = bf16[64,16,128]{2,1,0:T(8,128)(2,1)S(1)} all-to-all(bf16[64,16,128]{2,1,0:T(8,128)(2,1)S(1)} %update.1), channel_id=1, replica_groups={{0,2,4,6,8,10,12,14,16,18,20,22,24,26,28,30,32,34,36,38,40,42,44,46,48,..., dimensions={0} | all-to-all | bytes 524288 | tf_op jit(solution)/shard_map/all_to_all | solution.py:32
  68.1 1.0 %late.1 = f32[1,2048,128]{2,1,0:T(8,128)} custom-call(s32[1]{0:T(128)} %bitcast.args_0_.core_ref, bf16[64,16,128]{2,1,0:T(8,128)(2,1)S(1)} %all_to_all.17.after_ref, f32[1,2048,128]{2,1,0:T(8,128)S(1)} %get-tuple-element.17.resid_ref, f32[1,2048,128]{2,1,0:T(8,128)} %get-tuple-element.20.begun_hbm), custom_call_target="tpu_custom_call", output_to_operand_aliasing={{}: (3, {})} | custom-call | tf_op jit(solution)/shard_map/late/pallas_call | solution.py:292
  69.1 5.3 %all-gather.1 = bf16[128,16,128]{2,1,0:T(8,128)(2,1)S(1)} all-gather(bf16[64,16,128]{2,1,0:T(8,128)(2,1)S(1)} %all_to_all.17.after_ref), channel_id=3, replica_groups={{0,1},{2,3},{4,5},{6,7},{8,9},{10,11},{12,13},{14,15},{16,17},{18,19},{..., dimensions={0}, use_global_device_ids=true | all-gather | bytes 786432 | tf_op jit(solution)/shard_map/all_gather | solution.py:38
  74.4 1.0 %assemble.1 = (bf16[512,512]{1,0:T(8,128)(2,1)}, f32[1,16,128]{2,1,0:T(8,128)}) custom-call(bf16[2,64,16,128]{3,2,1,0:T(8,128)(2,1)S(1)} %bitcast.4, f32[16,128]{1,0:T(8,128)S(1)} %get-tuple-element.22.last_ref, f32[16,128]{1,0:T(8,128)S(1)} %get-tuple-element.23.kept_ref), custom_call_target="tpu_custom_call" | custom-call | tf_op jit(solution)/shard_map/assemble/pallas_call | solution.py:304
  (1 shorter events, 0.0 us)
Async XLA Ops:
  12.9 27.5 %copy-start = (f32[1,16,128]{2,1,0:T(8,128)S(1)}, f32[1,16,128]{2,1,0:T(8,128)}, u32[]{:S(2)}) copy-start(f32[1,16,128]{2,1,0:T(8,128)} %oresid_ref.1) | copy-start | bytes 24580
  12.9 27.5 %copy-start.1 = (s32[1,2,16]{2,1,0:T(2,128)S(1)}, s32[1,2,16]{2,1,0:T(2,128)}, u32[]{:S(2)}) copy-start(s32[1,2,16]{2,1,0:T(2,128)} %rank_ref.1) | copy-start | bytes 388
  12.9 27.5 %copy-start.2 = (s32[1,2]{1,0:T(1,128)S(1)}, s32[1,2]{1,0:T(1,128)}, u32[]{:S(2)}) copy-start(s32[1,2]{1,0:T(1,128)} %count_ref.1) | copy-start | bytes 28

commit v13 on v12

--- a/solution.py
+++ b/solution.py
@@ -94,7 +94,7 @@
 
     def select(s, me):
         columns = chosen_ref[s]
-        for r in range(groups):
+        for r in reversed(range(groups)):
             span = slice(r * WIDTH, (r + 1) * WIDTH)
             total = resid_ref[0, span, :] + acc_ref[s, span, :]
             mask = jnp.broadcast_to(columns[:, r:r + 1], (WIDTH, WIDTH)) > 0.5
@@ -145,11 +145,6 @@
 def pair_kernel(core_ref, keep_ref, both_ref, resid_ref, out_ref, store_hbm, tile_ref, sem):
     core = core_ref[0]
     other = 1 - core
-    chunk = 8 * REGION
-    for at in range(0, WHOLE, chunk):
-        span = slice(at, min(at + chunk, WHOLE))
-        total = keep_ref[span, :].astype(F32) + both_ref[other, span, :].astype(F32)
-        out_ref[span, :] = total.astype(BF)
     packed = both_ref[other, WHOLE:WHOLE + CAP, :].astype(F32)
     packed = jnp.concatenate([packed, jnp.zeros_like(packed)], axis=0).astype(BF)
     slots = both_ref[other, WHOLE + CAP:WHOLE + CAP + 2, :].astype(F32)[0:1, :]
@@ -159,6 +154,11 @@
     at = pl.multiple_of(WIDTH - NC * REGION + core * REGION, REGION)
     total = keep_ref[WHOLE:WHOLE + REGION, :].astype(F32) + tile_ref[pl.ds(at, REGION), :]
     out_ref[WHOLE:WHOLE + REGION, :] = total.astype(BF)
+    chunk = 8 * REGION
+    for at in range(0, WHOLE, chunk):
+        span = slice(at, min(at + chunk, WHOLE))
+        total = keep_ref[span, :].astype(F32) + both_ref[other, span, :].astype(F32)
+        out_ref[span, :] = total.astype(BF)
     stored_by(0, core_ref, resid_ref, store_hbm, sem)
 
 

time: 75.7 us -> 75.7 us (level)
  no operation moved by 1% of the time
where the time goes in v13:
time: 75.7 us; the launch traced here: 75.4 us
  blocking collectives  69.4 us (92%)
  Pallas kernels  5.31 us (7%)
    all_to_all x3, blocking collectives, exchange(): lax.all_to_all(value, 'd', split_axis=0, concat_axis=0, tiled=True, axis_...  55 us
    all_gather x2, blocking collectives, of_both_cores(): lax.all_gather(value, 'd', axis=0, axis_index_groups=groups_along((3,)))  14.4 us
    pallas_call x1, Pallas kernels, per_device(): pl.pallas_call(local, in_specs=[smem(), hbm(), hbm(), hbm(), hbm(), hbm()...  2.95 us

profile of v13, /device:TPU:1, one launch (start us, length us, event | category | flops | bytes accessed | tf_op | source)
XLA Modules:
  0.0 75.4 jit_solution(4215999775666625357)
XLA Ops:
  0.6 2.9 %local.1 = (f32[1,2048,128]{2,1,0:T(8,128)S(1)}, bf16[2048,128]{1,0:T(8,128)(2,1)S(1)}, bf16[2042,128]{1,0:T(8,128)(2,1)S(1)}) custom-call(s32[1]{0:T(128)} %bitcast.args_0_.core_ref, bf16[1,2,512,512]{3,2,1,0:T(8,128)(2,1)} %args_1_.4, bf16[1,2,512,512]{3,2,1,0:T(8,128)(2,1)} %args_2_.4, f32[1,2048,128]{2,1,0:T(8,128)} %args_3_.4, s32[1,2,128]{2,1,0:T(2,128)} %args_4_.4, ...), custom_call_target="tpu_custom_call" | custom-call | tf_op jit(solution)/shard_map/local/pallas_call | solution.py:234
  3.6 9.1 %all-gather.2.both_ref = bf16[2,2042,128]{2,1,0:T(8,128)(2,1)S(1)} all-gather(bf16[1,2042,128]{2,1,0:T(8,128)(2,1)S(1)} %bitcast.5), channel_id=2, replica_groups={{0,1},{2,3},{4,5},{6,7},{8,9},{10,11},{12,13},{14,15},{16,17},{18,19},{..., dimensions={0}, use_global_device_ids=true | all-gather | bytes 1568256 | tf_op jit(solution)/shard_map/all_gather | solution.py:38
  12.7 0.2 pair.1
  12.9 0.0 copy-start
  12.9 0.0 copy-start.1
  12.9 0.0 copy-start.2
  13.0 27.5 %all_to_all.15.arrived_ref = bf16[64,2,16,128]{3,2,1,0:T(8,128)(2,1)S(1)} all-to-all(bf16[64,2,16,128]{3,2,1,0:T(8,128)(2,1)S(1)} %bitcast.6), channel_id=1, replica_groups={{0,2,4,6,8,10,12,14,16,18,20,22,24,26,28,30,32,34,36,38,40,42,44,46,48,..., dimensions={0} | all-to-all | bytes 1048576 | tf_op jit(solution)/shard_map/all_to_all | solution.py:32
  40.4 0.0 copy-done
  40.4 0.0 copy-done.1
  40.4 0.0 copy-done.2
  40.5 0.2 owner.1
  40.6 8.1 %all_to_all.16.arrived_ref = bf16[4,2,16,128]{3,2,1,0:T(8,128)(2,1)S(1)} all-to-all(bf16[4,2,16,128]{3,2,1,0:T(8,128)(2,1)S(1)} %get-tuple-element.19), channel_id=1, replica_groups={{0,128,256,384},{1,129,257,385},{2,130,258,386},{3,131,259,387},{4,132,..., dimensions={0} | all-to-all | bytes 65536 | tf_op jit(solution)/shard_map/all_to_all | solution.py:32
  48.7 19.4 %all_to_all.17.after_ref = bf16[64,16,128]{2,1,0:T(8,128)(2,1)S(1)} all-to-all(bf16[64,16,128]{2,1,0:T(8,128)(2,1)S(1)} %update.1), channel_id=1, replica_groups={{0,2,4,6,8,10,12,14,16,18,20,22,24,26,28,30,32,34,36,38,40,42,44,46,48,..., dimensions={0} | all-to-all | bytes 524288 | tf_op jit(solution)/shard_map/all_to_all | solution.py:32
  68.2 1.0 %late.1 = f32[1,2048,128]{2,1,0:T(8,128)} custom-call(s32[1]{0:T(128)} %bitcast.args_0_.core_ref, bf16[64,16,128]{2,1,0:T(8,128)(2,1)S(1)} %all_to_all.17.after_ref, f32[1,2048,128]{2,1,0:T(8,128)S(1)} %get-tuple-element.17.resid_ref, f32[1,2048,128]{2,1,0:T(8,128)} %get-tuple-element.20.begun_hbm), custom_call_target="tpu_custom_call", output_to_operand_aliasing={{}: (3, {})} | custom-call | tf_op jit(solution)/shard_map/late/pallas_call | solution.py:292
  69.2 5.3 %all-gather.1 = bf16[128,16,128]{2,1,0:T(8,128)(2,1)S(1)} all-gather(bf16[64,16,128]{2,1,0:T(8,128)(2,1)S(1)} %all_to_all.17.after_ref), channel_id=3, replica_groups={{0,1},{2,3},{4,5},{6,7},{8,9},{10,11},{12,13},{14,15},{16,17},{18,19},{..., dimensions={0}, use_global_device_ids=true | all-gather | bytes 786432 | tf_op jit(solution)/shard_map/all_gather | solution.py:38
  74.5 1.0 %assemble.1 = (bf16[512,512]{1,0:T(8,128)(2,1)}, f32[1,16,128]{2,1,0:T(8,128)}) custom-call(bf16[2,64,16,128]{3,2,1,0:T(8,128)(2,1)S(1)} %bitcast.4, f32[16,128]{1,0:T(8,128)S(1)} %get-tuple-element.22.last_ref, f32[16,128]{1,0:T(8,128)S(1)} %get-tuple-element.23.kept_ref), custom_call_target="tpu_custom_call" | custom-call | tf_op jit(solution)/shard_map/assemble/pallas_call | solution.py:304
  (1 shorter events, 0.0 us)
Async XLA Ops:
  12.9 27.5 %copy-start = (f32[1,16,128]{2,1,0:T(8,128)S(1)}, f32[1,16,128]{2,1,0:T(8,128)}, u32[]{:S(2)}) copy-start(f32[1,16,128]{2,1,0:T(8,128)} %oresid_ref.1) | copy-start | bytes 24580
  12.9 27.5 %copy-start.1 = (s32[1,2,16]{2,1,0:T(2,128)S(1)}, s32[1,2,16]{2,1,0:T(2,128)}, u32[]{:S(2)}) copy-start(s32[1,2,16]{2,1,0:T(2,128)} %rank_ref.1) | copy-start | bytes 388
  12.9 27.5 %copy-start.2 = (s32[1,2]{1,0:T(1,128)S(1)}, s32[1,2]{1,0:T(1,128)}, u32[]{:S(2)}) copy-start(s32[1,2]{1,0:T(1,128)} %count_ref.1) | copy-start | bytes 28

commit v14 on v13

--- a/solution.py
+++ b/solution.py
@@ -157,8 +157,7 @@
     chunk = 8 * REGION
     for at in range(0, WHOLE, chunk):
         span = slice(at, min(at + chunk, WHOLE))
-        total = keep_ref[span, :].astype(F32) + both_ref[other, span, :].astype(F32)
-        out_ref[span, :] = total.astype(BF)
+        out_ref[span, :] = keep_ref[span, :] + both_ref[other, span, :]
     stored_by(0, core_ref, resid_ref, store_hbm, sem)
 
 

time: 75.7 us -> 75.7 us (level)
  no operation moved by 1% of the time
where the time goes in v14:
time: 75.7 us; the launch traced here: 75.4 us
  blocking collectives  69.4 us (92%)
  Pallas kernels  5.29 us (7%)
    all_to_all x3, blocking collectives, exchange(): lax.all_to_all(value, 'd', split_axis=0, concat_axis=0, tiled=True, axis_...  55.1 us
    all_gather x2, blocking collectives, of_both_cores(): lax.all_gather(value, 'd', axis=0, axis_index_groups=groups_along((3,)))  14.3 us
    pallas_call x1, Pallas kernels, per_device(): pl.pallas_call(local, in_specs=[smem(), hbm(), hbm(), hbm(), hbm(), hbm()...  2.95 us

profile of v14, /device:TPU:1, one launch (start us, length us, event | category | flops | bytes accessed | tf_op | source)
XLA Modules:
  0.0 75.4 jit_solution(8339547703466699610)
XLA Ops:
  0.6 2.9 %local.1 = (f32[1,2048,128]{2,1,0:T(8,128)S(1)}, bf16[2048,128]{1,0:T(8,128)(2,1)S(1)}, bf16[2042,128]{1,0:T(8,128)(2,1)S(1)}) custom-call(s32[1]{0:T(128)} %bitcast.args_0_.core_ref, bf16[1,2,512,512]{3,2,1,0:T(8,128)(2,1)} %args_1_.4, bf16[1,2,512,512]{3,2,1,0:T(8,128)(2,1)} %args_2_.4, f32[1,2048,128]{2,1,0:T(8,128)} %args_3_.4, s32[1,2,128]{2,1,0:T(2,128)} %args_4_.4, ...), custom_call_target="tpu_custom_call" | custom-call | tf_op jit(solution)/shard_map/local/pallas_call | solution.py:233
  3.6 9.1 %all-gather.2.both_ref = bf16[2,2042,128]{2,1,0:T(8,128)(2,1)S(1)} all-gather(bf16[1,2042,128]{2,1,0:T(8,128)(2,1)S(1)} %bitcast.5), channel_id=2, replica_groups={{0,1},{2,3},{4,5},{6,7},{8,9},{10,11},{12,13},{14,15},{16,17},{18,19},{..., dimensions={0}, use_global_device_ids=true | all-gather | bytes 1568256 | tf_op jit(solution)/shard_map/all_gather | solution.py:38
  12.7 0.2 pair.1
  12.9 0.0 copy-start
  12.9 0.0 copy-start.1
  12.9 0.0 copy-start.2
  12.9 27.5 %all_to_all.15.arrived_ref = bf16[64,2,16,128]{3,2,1,0:T(8,128)(2,1)S(1)} all-to-all(bf16[64,2,16,128]{3,2,1,0:T(8,128)(2,1)S(1)} %bitcast.6), channel_id=1, replica_groups={{0,2,4,6,8,10,12,14,16,18,20,22,24,26,28,30,32,34,36,38,40,42,44,46,48,..., dimensions={0} | all-to-all | bytes 1048576 | tf_op jit(solution)/shard_map/all_to_all | solution.py:32
  40.4 0.0 copy-done
  40.4 0.0 copy-done.1
  40.4 0.0 copy-done.2
  40.4 0.2 owner.1
  40.6 8.1 %all_to_all.16.arrived_ref = bf16[4,2,16,128]{3,2,1,0:T(8,128)(2,1)S(1)} all-to-all(bf16[4,2,16,128]{3,2,1,0:T(8,128)(2,1)S(1)} %get-tuple-element.19), channel_id=1, replica_groups={{0,128,256,384},{1,129,257,385},{2,130,258,386},{3,131,259,387},{4,132,..., dimensions={0} | all-to-all | bytes 65536 | tf_op jit(solution)/shard_map/all_to_all | solution.py:32
  48.7 19.5 %all_to_all.17.after_ref = bf16[64,16,128]{2,1,0:T(8,128)(2,1)S(1)} all-to-all(bf16[64,16,128]{2,1,0:T(8,128)(2,1)S(1)} %update.1), channel_id=1, replica_groups={{0,2,4,6,8,10,12,14,16,18,20,22,24,26,28,30,32,34,36,38,40,42,44,46,48,..., dimensions={0} | all-to-all | bytes 524288 | tf_op jit(solution)/shard_map/all_to_all | solution.py:32
  68.2 1.0 %late.1 = f32[1,2048,128]{2,1,0:T(8,128)} custom-call(s32[1]{0:T(128)} %bitcast.args_0_.core_ref, bf16[64,16,128]{2,1,0:T(8,128)(2,1)S(1)} %all_to_all.17.after_ref, f32[1,2048,128]{2,1,0:T(8,128)S(1)} %get-tuple-element.17.resid_ref, f32[1,2048,128]{2,1,0:T(8,128)} %get-tuple-element.20.begun_hbm), custom_call_target="tpu_custom_call", output_to_operand_aliasing={{}: (3, {})} | custom-call | tf_op jit(solution)/shard_map/late/pallas_call | solution.py:291
  69.2 5.3 %all-gather.1 = bf16[128,16,128]{2,1,0:T(8,128)(2,1)S(1)} all-gather(bf16[64,16,128]{2,1,0:T(8,128)(2,1)S(1)} %all_to_all.17.after_ref), channel_id=3, replica_groups={{0,1},{2,3},{4,5},{6,7},{8,9},{10,11},{12,13},{14,15},{16,17},{18,19},{..., dimensions={0}, use_global_device_ids=true | all-gather | bytes 786432 | tf_op jit(solution)/shard_map/all_gather | solution.py:38
  74.5 1.0 %assemble.1 = (bf16[512,512]{1,0:T(8,128)(2,1)}, f32[1,16,128]{2,1,0:T(8,128)}) custom-call(bf16[2,64,16,128]{3,2,1,0:T(8,128)(2,1)S(1)} %bitcast.4, f32[16,128]{1,0:T(8,128)S(1)} %get-tuple-element.22.last_ref, f32[16,128]{1,0:T(8,128)S(1)} %get-tuple-element.23.kept_ref), custom_call_target="tpu_custom_call" | custom-call | tf_op jit(solution)/shard_map/assemble/pallas_call | solution.py:303
  (1 shorter events, 0.0 us)
Async XLA Ops:
  12.9 27.5 %copy-start = (f32[1,16,128]{2,1,0:T(8,128)S(1)}, f32[1,16,128]{2,1,0:T(8,128)}, u32[]{:S(2)}) copy-start(f32[1,16,128]{2,1,0:T(8,128)} %oresid_ref.1) | copy-start | bytes 24580
  12.9 27.5 %copy-start.1 = (s32[1,2,16]{2,1,0:T(2,128)S(1)}, s32[1,2,16]{2,1,0:T(2,128)}, u32[]{:S(2)}) copy-start(s32[1,2,16]{2,1,0:T(2,128)} %rank_ref.1) | copy-start | bytes 388
  12.9 27.5 %copy-start.2 = (s32[1,2]{1,0:T(1,128)S(1)}, s32[1,2]{1,0:T(1,128)}, u32[]{:S(2)}) copy-start(s32[1,2]{1,0:T(1,128)} %count_ref.1) | copy-start | bytes 28
